TPU v7x, 128 devices: a whole 4x4x4 slice. The times are simulated.
128 devices in a mesh: rep: 2 (over x_hi), fsdp: 16 (over y, x_lo, core), tp: 4 (over z).
Axes of the slice: x: 4 (x_hi: 2, x_lo: 2; x = x_hi * 2 + x_lo), y: 4, z: 4, core: 2. Of those that a mesh axis runs over, the one named last changes fastest.
Arguments:
- gate_up_master: float32 [2, 4096, 14336], P(None, 'fsdp', ('rep', 'tp')), may hold values from -0.09375 to 0.09375
- gate_up_moment: float32 [2, 4096, 14336], P(None, 'fsdp', ('rep', 'tp')), may hold values from -0.00018310547 to 0.00018310547
- gate_up_second: float32 [2, 4096, 14336], P(None, 'fsdp', ('rep', 'tp')), may hold values from 8.5149493e-10 to 8.51495e-09
- gate_up_grad: bfloat16 [2, 4096, 14336], P(None, 'fsdp', ('rep', 'tp')), may hold values from -8 to 8
- down_master: float32 [4096, 14336], P('fsdp', ('rep', 'tp')), may hold values from -0.046875 to 0.046875
- down_moment: float32 [4096, 14336], P('fsdp', ('rep', 'tp')), may hold values from -0.00018310547 to 0.00018310547
- down_second: float32 [4096, 14336], P('fsdp', ('rep', 'tp')), may hold values from 8.5149493e-10 to 8.51495e-09
- down_grad: bfloat16 [4096, 14336], P('fsdp', ('rep', 'tp')), may hold values from -8 to 8
- norm_gain: float32 [4096], replicated, may hold values from 0.1 to 1.9
- start_rows: bfloat16 [1024, 4096], P(('rep', 'fsdp', 'tp')), may hold values from -6 to 6
- queries: bfloat16 [2, 1024, 4096], P(None, ('rep', 'fsdp', 'tp')), may hold values from -6 to 6
- new_kv: bfloat16 [2, 1024, 2, 1024], P(None, ('rep', 'fsdp', 'tp')), may hold values from -6 to 6
- kv_pool: bfloat16 [8192, 16, 2, 1024], P(('rep', 'fsdp', 'tp')), may hold values from -6 to 6
- page_table: int32 [1024, 8], P(('rep', 'fsdp', 'tp')), may hold values from 0 to 63, as said below
- cache_len: int32 [1024], P(('rep', 'fsdp', 'tp')), may hold values from 1 to 128, as said below
Outputs:
- final_rows: bfloat16 [1024, 4096], P(('rep', 'fsdp', 'tp'))
Inputs may be any that keep to these rules, and one draw needn't show every extreme that they name: `page_table`: within each aligned block of 8 rows, the entries name each of the 64 pages of that block exactly once. `cache_len`: some row has exactly 128 cached positions.
All inputs are finite; a program needn't handle non-finite values.
Results may differ from a plain program's by a relative error of at most 0.019.
Values may be sent and summed in bfloat16 or wider, within the bound.
No kernel may reach another device: no remote copies, remote signals or barrier semaphores. Data moves between devices by JAX's collectives and lax.ppermute only.
A program may use at most 128 MiB of HBM per device.

v0:
```python
import jax
import jax.numpy as jnp
from jax import lax
from jax.sharding import PartitionSpec as P

D = 4096
HD = 128


beta_one = 0.9
beta_two = 0.95
adam_eps = 1e-08
adam_time = 100.0
norm_eps = 1e-05


def adam_new(master, moment, second, grad, clip):
    learn_rate = 2.0 / D**0.5
    g = grad.astype(jnp.float32) * clip
    m = beta_one * moment + (1.0 - beta_one) * g
    v = beta_two * second + (1.0 - beta_two) * g * g
    first_fix = 1.0 - beta_one**adam_time
    second_fix = 1.0 - beta_two**adam_time
    return (master - learn_rate * (m / first_fix) / (jnp.sqrt(v / second_fix) + adam_eps)).astype(
        jnp.bfloat16
    )


def attend(query, keys, values, valid, fresh_k, fresh_v, step):
    scale = query.shape[-1] ** (-0.5)
    old = jnp.einsum("rjgh,rcjh->rjgc", query, keys, preferred_element_type=jnp.float32) * scale
    old = jnp.where(valid[:, None, None, :], old, -1e30)
    new = jnp.einsum("rjgh,srjh->rjgs", query, fresh_k, preferred_element_type=jnp.float32) * scale
    allowed = jnp.arange(fresh_k.shape[0]) <= step
    new = jnp.where(allowed[None, None, None, :], new, -1e30)
    top = jnp.maximum(jnp.max(old, axis=-1, keepdims=True), jnp.max(new, axis=-1, keepdims=True))
    exp_old = jnp.exp(old - top)
    exp_new = jnp.exp(new - top)
    total = jnp.sum(exp_old, axis=-1, keepdims=True) + jnp.sum(exp_new, axis=-1, keepdims=True)
    prob_old = (exp_old / total).astype(jnp.bfloat16)
    prob_new = (exp_new / total).astype(jnp.bfloat16)
    out = jnp.einsum("rjgc,rcjh->rjgh", prob_old, values, preferred_element_type=jnp.float32)
    out = out + jnp.einsum("rjgs,srjh->rjgh", prob_new, fresh_v, preferred_element_type=jnp.float32)
    return out.reshape(out.shape[0], -1)


def shards(
    gate_up_master,
    gate_up_moment,
    gate_up_second,
    gate_up_grad,
    down_master,
    down_moment,
    down_second,
    down_grad,
    norm_gain,
    start_rows,
    queries,
    new_kv,
    kv_pool,
    page_table,
    cache_len,
):
    local_squares = jnp.sum(jnp.square(gate_up_grad.astype(jnp.float32))) + jnp.sum(
        jnp.square(down_grad.astype(jnp.float32))
    )
    total = lax.psum(local_squares, ("rep", "fsdp", "tp"))
    clip = jnp.minimum(1.0, 1.0 / jnp.sqrt(total))
    gate_up = adam_new(gate_up_master, gate_up_moment, gate_up_second, gate_up_grad, clip)
    down_t = adam_new(down_master, down_moment, down_second, down_grad, clip)[None]
    n_fsdp = lax.axis_size("fsdp")
    n_rep = lax.axis_size("rep")
    cols = gate_up.shape[2]
    copied = (
        lax.all_gather(gate_up, "rep", axis=2, tiled=True),
        lax.all_gather(down_t, "rep", axis=2, tiled=True),
    )
    shaped = tuple(
        (a.reshape(a.shape[0], a.shape[1], n_rep, n_fsdp, cols // n_fsdp) for a in copied)
    )
    moved = (
        lax.all_to_all(shaped[0], "fsdp", split_axis=3, concat_axis=1, tiled=True),
        lax.all_to_all(shaped[1], "fsdp", split_axis=3, concat_axis=1, tiled=True),
    )
    weights = tuple((a.reshape(a.shape[0], a.shape[1], -1) for a in moved))
    roll_gate_up = weights[0]
    roll_down = weights[1][0]
    local_rows = start_rows.shape[0]
    kv_width = new_kv.shape[-1]
    head_dim = HD
    key_heads = kv_width // head_dim
    cache = kv_pool[page_table].reshape(local_rows, -1, 2, key_heads, head_dim)
    keys = cache[:, :, 0]
    values = cache[:, :, 1]
    valid = jnp.arange(keys.shape[1], dtype=jnp.int32)[None, :] < cache_len[:, None]
    fresh = new_kv.reshape(new_kv.shape[0], local_rows, 2, key_heads, head_dim)
    fresh_k = fresh[:, :, 0]
    fresh_v = fresh[:, :, 1]
    rows = start_rows
    for step in range(queries.shape[0]):
        query = queries[step].reshape(local_rows, key_heads, -1, head_dim)
        attended = attend(query, keys, values, valid, fresh_k, fresh_v, step)
        mixed = (rows.astype(jnp.float32) + attended).astype(jnp.bfloat16)
        mixed_f = mixed.astype(jnp.float32)
        normed = (
            mixed_f
            * lax.rsqrt(jnp.mean(mixed_f * mixed_f, axis=-1, keepdims=True) + norm_eps)
            * norm_gain
        ).astype(jnp.bfloat16)
        whole = lax.all_gather(normed, ("fsdp", "tp"), axis=0, tiled=True)
        gate = jnp.dot(whole, roll_gate_up[0], preferred_element_type=jnp.float32)
        upper = jnp.dot(whole, roll_gate_up[1], preferred_element_type=jnp.float32)
        hidden = (jax.nn.silu(gate) * upper).astype(jnp.bfloat16)
        summed = lax.psum_scatter(
            lax.dot_general(
                hidden, roll_down, (((1,), (1,)), ((), ())), preferred_element_type=jnp.float32
            ),
            ("fsdp", "tp"),
            scatter_dimension=0,
            tiled=True,
        )
        rows = (mixed_f + summed).astype(jnp.bfloat16)
    return rows


def solution(mesh):
    in_specs = (
        P(None, "fsdp", ("rep", "tp")),
        P(None, "fsdp", ("rep", "tp")),
        P(None, "fsdp", ("rep", "tp")),
        P(None, "fsdp", ("rep", "tp")),
        P("fsdp", ("rep", "tp")),
        P("fsdp", ("rep", "tp")),
        P("fsdp", ("rep", "tp")),
        P("fsdp", ("rep", "tp")),
        P(),
        P(("rep", "fsdp", "tp"), None),
        P(None, ("rep", "fsdp", "tp"), None),
        P(None, ("rep", "fsdp", "tp"), None, None),
        P(("rep", "fsdp", "tp"), None, None, None),
        P(("rep", "fsdp", "tp"), None),
        P(("rep", "fsdp", "tp")),
    )
    out_specs = P(("rep", "fsdp", "tp"), None)
    return jax.shard_map(shards, mesh=mesh, in_specs=in_specs, out_specs=out_specs, check_vma=False)
```

profile of v0, /device:TPU:0, one launch (start us, length us, event | category | flops | bytes accessed | tf_op | source)
XLA Modules:
  0.0 1184.5 jit_solution(11952147557319080114)
XLA Ops:
  6.5 1.5 copy.41
  8.0 1.2 fusion.20
  9.1 2.8 copy.40
  12.0 1.5 fusion.5
  14.8 68.2 %psum.7 = f32[]{:T(128)} all-reduce(f32[]{:T(128)S(6)} %add.102), channel_id=1, replica_groups=mesh['rep'=2,'fsdp'=16,'tp'=4] {'rep','fsdp','tp'}, use_global_device_ids=true, to_apply=%region_7.8 | all-reduce | flops 1 | bytes 8 | tf_op jit(solution)/shard_map/psum | solution.py:67
  83.7 2.8 copy.49
  86.5 2.8 copy.47
  89.2 2.7 copy.48
  91.9 5.0 fusion.25
  97.0 5.1 copy.43
  102.2 5.3 copy.39
  107.5 5.1 copy.42
  112.6 6.7 fusion.10
  119.8 12.9 %gather_fusion = bf16[64,16,2,1024]{3,2,1,0:T(2,128)(2,1)} fusion(bf16[64,16,2,1024]{3,2,1,0:T(2,128)(2,1)} %param.27, s32[1024]{0:T(1024)S(1)} %pad_clamp_fusion), kind=kCustom, calls=%fused_computation | custom fusion | bytes 8388864 | tf_op jit(solution)/shard_map/gather | solution.py:92
  132.7 7.8 reshape.110
  140.9 2.9 fusion.72
  143.9 1.3 fusion.78
  145.6 0.3 fusion.68
  145.9 0.7 fusion.30
  146.9 0.7 fusion.54
  147.6 2.9 copy.50
  150.6 3.7 all-to-all-start.1
  154.3 48.9 %all-gather.8.cloned.1.call-done = bf16[2,256,3584]{1,2,0:T(8,128)(2,1)} async-done(((bf16[2,256,1792]{1,2,0:T(8,128)(2,1)}), bf16[2,256,3584]{1,2,0:T(8,128)(2,1)}) %all-gather.8.cloned.1.call-update) | async-done | bytes 3670032 | tf_op jit(solution)/shard_map/all_gather | solution.py:75
  203.1 4.4 copy.44
  207.5 4.5 all-to-all-start
  212.3 1.0 copy.51
  213.4 0.8 copy.64
  214.2 45.9 %all-to-all-done = bf16[2,256,2,16,112]{1,4,2,0,3:T(8,128)(2,1)} async-done(((bf16[2,256,2,16,112]{1,4,2,0,3:T(8,128)(2,1)}), bf16[2,256,2,16,112]{1,4,2,0,3:T(8,128)(2,1)}, u32[]{:S(2)}, u32[]{:S(2)}) %all-to-all-start) | async-done | bytes 3670048 | tf_op jit(solution)/shard_map/all_to_all | solution.py:82
  260.1 2.3 fusion.73
  262.3 1.0 copy.45
  263.4 2.1 copy.62
  265.5 1.0 copy.46
  266.5 2.1 copy.63
  268.6 124.0 %all-gather.6.cloned.1.call-done = bf16[512,4096]{1,0:T(8,128)(2,1)} async-done(((bf16[8,4096]{1,0:T(8,128)(2,1)}), bf16[512,4096]{1,0:T(8,128)(2,1)}) %all-gather.6.cloned.1.call-update) | async-done | bytes 4194320 | tf_op jit(solution)/shard_map/all_gather | solution.py:110
  392.6 4.2 fusion.80
  396.9 8.7 fusion.27
  405.9 3.0 fusion.76
  409.3 0.3 fusion.69
  409.6 0.7 fusion.31
  410.4 294.7 %reduce-scatter.3.cloned.1.call-done = f32[8,4096]{1,0:T(8,128)} async-done(((f32[512,4096]{1,0:T(8,128)}), f32[8,4096]{1,0:T(8,128)}) %reduce-scatter.3.cloned.1.call-update) | async-done | bytes 131088 | tf_op jit(solution)/shard_map/reduce_scatter | solution.py:114
  705.2 1.1 fusion.56
  706.2 0.7 fusion.58
  707.0 0.3 reduce-scatter.5.cloned.1.call-start
  707.3 156.1 %all-gather.10.cloned.1.call-done = bf16[512,4096]{1,0:T(8,128)(2,1)} async-done(((bf16[8,4096]{1,0:T(8,128)(2,1)}), bf16[512,4096]{1,0:T(8,128)(2,1)}) %all-gather.10.cloned.1.call-update) | async-done | bytes 4194320 | tf_op jit(solution)/shard_map/all_gather | solution.py:110
  863.4 4.2 fusion.81
  867.6 8.8 fusion.29
  876.5 299.7 %reduce-scatter.5.cloned.1.call-done = f32[8,4096]{1,0:T(8,128)} async-done(((f32[512,4096]{1,0:T(8,128)}), f32[8,4096]{1,0:T(8,128)}) %reduce-scatter.5.cloned.1.call-update) | async-done | bytes 131088 | tf_op jit(solution)/shard_map/reduce_scatter | solution.py:114
  1176.1 1.5 fusion.59
  (57 shorter events, 2.7 us)
Async XLA Ops:
  6.5 141.1 %all-gather.12.cloned.1.call-start = ((), (), s32[]{:S(2)}) async-start(), calls=%async_computation.9 | async-start | bytes 2752512 | tf_op jit(solution)/shard_map/all_gather | solution.py:76
  97.0 106.2 %all-gather.8.cloned.1.call-start = ((), (), s32[]{:S(2)}) async-start(), calls=%async_computation.5 | async-start | bytes 5505024 | tf_op jit(solution)/shard_map/all_gather | solution.py:75
  112.6 7.0 copy-start.7
  112.6 7.1 copy-start.5
  112.6 7.1 copy-start.3
  119.3 273.3 %all-gather.6.cloned.1.call-start = ((), (), s32[]{:S(2)}) async-start(), calls=%async_computation.4 | async-start | bytes 4259840 | tf_op jit(solution)/shard_map/all_gather | solution.py:110
  132.7 7.8 copy-start.8
  143.9 2.0 copy-start.2
  143.9 2.0 copy-start
  145.9 0.8 copy-start.6
  145.9 1.0 copy-start.4
  150.6 56.9 %all-to-all-start.1 = ((bf16[1,256,2,16,112]{1,4,2,0,3:T(8,128)(2,1)}), bf16[1,256,2,16,112]{1,4,2,0,3:T(8,128)(2,1)S(1)}, u32[]{:S(2)}, u32[]{:S(2)}) async-start(bf16[1,256,2,16,112]{1,4,2,0,3:T(8,128)(2,1)} %copy.50), calls=%async_computation.1 | async-start | bytes 3670016 | tf_op jit(solution)/shard_map/all_to_all | solution.py:83
  207.5 52.5 %all-to-all-start = ((bf16[2,256,2,16,112]{1,4,2,0,3:T(8,128)(2,1)}), bf16[2,256,2,16,112]{1,4,2,0,3:T(8,128)(2,1)}, u32[]{:S(2)}, u32[]{:S(2)}) async-start(bf16[2,256,2,16,112]{1,4,2,0,3:T(8,128)(2,1)} %copy.44), calls=%async_computation | async-start | bytes 7340032 | tf_op jit(solution)/shard_map/all_to_all | solution.py:82
  212.1 493.1 %reduce-scatter.3.cloned.1.call-start = ((), (), s32[]{:S(2)}) async-start(), calls=%async_computation.6 | async-start | bytes 8519680 | tf_op jit(solution)/shard_map/reduce_scatter | solution.py:114
  405.5 457.9 %all-gather.10.cloned.1.call-start = ((), (), s32[]{:S(2)}) async-start(), calls=%async_computation.7 | async-start | bytes 4259840 | tf_op jit(solution)/shard_map/all_gather | solution.py:110
  405.9 3.7 copy-start.1
  707.0 469.2 %reduce-scatter.5.cloned.1.call-start = ((), (), s32[]{:S(2)}) async-start(), calls=%async_computation.8 | async-start | bytes 8519680 | tf_op jit(solution)/shard_map/reduce_scatter | solution.py:114
Sparse Core Ops, SparseCore 0:
  97.1 30.3 all-gather.11
  129.1 73.9 all-gather.7
  204.8 187.7 all-gather.5
  405.7 299.4 reduce-scatter.2
  707.1 156.2 all-gather.9
  876.6 299.5 reduce-scatter.4
where the time goes:
time: 1190 us; the launch traced here: 1180 us
  waiting for transfers between devices  969 us (81%)
  local copies, waits for them, and re-layouts  69.8 us (6%)
  blocking collectives  68.2 us (6%)
  matrix products  32.6 us (3%)
  other arithmetic  19.5 us (2%)
  between operations  15.8 us (1%)
    reduce_scatter x2, waiting for transfers between devices, shards(): lax.psum_scatter(lax.dot_general(hidden, roll_down, (((1,), (1,)), ((), (...  594 us
    all_gather x2, waiting for transfers between devices, shards(): whole = lax.all_gather(normed, ('fsdp', 'tp'), axis=0, tiled=True)  280 us
    psum x1, blocking collectives, shards(): total = lax.psum(local_squares, ('rep', 'fsdp', 'tp'))  68.2 us
    all_gather x1, waiting for transfers between devices, shards(): lax.all_gather(gate_up, 'rep', axis=2, tiled=True)  48.9 us
    all_to_all x1, waiting for transfers between devices, shards(): lax.all_to_all(shaped[0], 'fsdp', split_axis=3, concat_axis=1, tiled=True)  45.9 us
    unnamed x29, local copies, waits for them, and re-layouts  33.1 us
  transfers between devices with their start and end apart: 8, of which 6 were waited for; matrix products, arithmetic and copies ran while one was open for 6% of the time, Pallas kernels for 0%

commit v1 on v0

v1 whole, which is shorter than its diff:
```python
import jax
import jax.numpy as jnp
from jax import lax
from jax.experimental import pallas as pl
from jax.experimental.pallas import tpu as pltpu
from jax.sharding import Mesh, PartitionSpec as P

D = 4096
HD = 128
BLK = 256

beta_one = 0.9
beta_two = 0.95
adam_eps = 1e-08
adam_time = 100.0
norm_eps = 1e-05

ALL = ("xh", "y", "xl", "c", "z")
GROUP = ("xh", "y", "xl", "z")
F32 = jnp.float32
BF16 = jnp.bfloat16


def adam_new(master, moment, second, grad, clip):
    learn_rate = 2.0 / D**0.5
    g = grad.astype(F32) * clip
    m = beta_one * moment + (1.0 - beta_one) * g
    v = beta_two * second + (1.0 - beta_two) * g * g
    first_fix = 1.0 - beta_one**adam_time
    second_fix = 1.0 - beta_two**adam_time
    return master - learn_rate * (m / first_fix) / (jnp.sqrt(v / second_fix) + adam_eps)


def gate_up_body(y_ref, clip_ref, master, moment, second, grad, *outs):
    clip = clip_ref[0]
    y = y_ref[0]
    wide = master.shape[2] // 4
    new = [
        adam_new(master[s], moment[s], second[s], grad[s], clip).astype(BF16) for s in range(2)
    ]
    for me in range(4):

        @pl.when(y == me)
        def _():
            for k, out in enumerate(outs):
                lo = (me ^ k) * wide
                out[:, :wide] = new[0][:, lo : lo + wide]
                out[:, wide:] = new[1][:, lo : lo + wide]


def down_body(y_ref, clip_ref, master, moment, second, grad, *outs):
    clip = clip_ref[0]
    y = y_ref[0]
    wide = master.shape[1] // 4
    new = adam_new(master[...], moment[...], second[...], grad[...], clip).astype(BF16)
    for me in range(4):

        @pl.when(y == me)
        def _():
            for k, out in enumerate(outs):
                lo = (me ^ k) * wide
                out[:, :wide] = new[:, lo : lo + wide]
                out[:, wide:] = jnp.zeros((out.shape[0], out.shape[1] - wide), BF16)


def updated(body, y, clip, arrays, width, tile):
    stack = arrays[0].shape[:-2]
    rows, cols = arrays[0].shape[-2:]
    zeros = (0,) * len(stack)
    spec = pl.BlockSpec(stack + (tile, cols), lambda i: zeros + (i, 0))
    smem = pl.BlockSpec(memory_space=pltpu.SMEM)
    return pl.pallas_call(
        body,
        grid=(rows // tile,),
        in_specs=[smem, smem] + [spec] * 4,
        out_specs=[pl.BlockSpec((tile, width), lambda i: (i, 0))] * 4,
        out_shape=[jax.ShapeDtypeStruct((rows, width), BF16)] * 4,
        compiler_params=pltpu.CompilerParams(vmem_limit_bytes=48 << 20),
    )(y, clip, *arrays)


def first_body(xl_ref, x, *refs):
    blocks, (send, keep) = refs[:-2], refs[-2:]
    half = x.shape[0] // 2
    xl = xl_ref[0]
    for out, part in ((send, 1 - xl), (keep, xl)):
        acc = None
        for b, w in enumerate(blocks):
            lhs = x[pl.ds(pl.multiple_of(part * half, half), half), b * BLK : (b + 1) * BLK]
            dot = jnp.dot(lhs, w[...], preferred_element_type=F32)
            acc = dot if acc is None else acc + dot
        out[...] = acc.astype(out.dtype)


def first_products(xl, x, blocks):
    half, width = x.shape[0] // 2, blocks[0].shape[1]
    vmem = pl.BlockSpec(memory_space=pltpu.VMEM)
    return pl.pallas_call(
        first_body,
        in_specs=[pl.BlockSpec(memory_space=pltpu.SMEM)] + [vmem] * (1 + len(blocks)),
        out_specs=[vmem, vmem],
        out_shape=[
            jax.ShapeDtypeStruct((half, width), BF16),
            jax.ShapeDtypeStruct((half, width), F32),
        ],
        compiler_params=pltpu.CompilerParams(vmem_limit_bytes=48 << 20),
    )(xl, x, *blocks)


def hidden_body(keep, other, out):
    both = keep[...] + other[...].astype(F32)
    wide = both.shape[1] // 2
    gate, upper = both[:, :wide], both[:, wide:]
    out[:, :wide] = (gate * jax.nn.sigmoid(gate) * upper).astype(BF16)
    out[:, wide:] = jnp.zeros((out.shape[0], out.shape[1] - wide), BF16)


def second_body(xl_ref, own, other, *refs):
    blocks, out = refs[:-1], refs[-1]
    half = own.shape[0]
    xl = xl_ref[0]
    for h, part in ((own, xl), (other, 1 - xl)):
        for b, w in enumerate(blocks):
            dot = lax.dot_general(
                h[...], w[...], (((1,), (1,)), ((), ())), preferred_element_type=F32
            )
            out[pl.ds(pl.multiple_of(part * half, half), half), b * BLK : (b + 1) * BLK] = (
                dot.astype(BF16)
            )


def second_products(xl, own, other, blocks):
    vmem = pl.BlockSpec(memory_space=pltpu.VMEM)
    return pl.pallas_call(
        second_body,
        in_specs=[pl.BlockSpec(memory_space=pltpu.SMEM)] + [vmem] * (2 + len(blocks)),
        out_specs=vmem,
        out_shape=jax.ShapeDtypeStruct((2 * own.shape[0], BLK * len(blocks)), BF16),
        compiler_params=pltpu.CompilerParams(vmem_limit_bytes=48 << 20),
    )(xl, own, other, *blocks)


def attend(query, keys, values, valid, fresh_k, fresh_v, step):
    scale = query.shape[-1] ** (-0.5)
    old = jnp.einsum("rjgh,rcjh->rjgc", query, keys, preferred_element_type=F32) * scale
    old = jnp.where(valid[:, None, None, :], old, -1e30)
    new = jnp.einsum("rjgh,srjh->rjgs", query, fresh_k, preferred_element_type=F32) * scale
    allowed = jnp.arange(fresh_k.shape[0]) <= step
    new = jnp.where(allowed[None, None, None, :], new, -1e30)
    top = jnp.maximum(jnp.max(old, axis=-1, keepdims=True), jnp.max(new, axis=-1, keepdims=True))
    exp_old = jnp.exp(old - top)
    exp_new = jnp.exp(new - top)
    total = jnp.sum(exp_old, axis=-1, keepdims=True) + jnp.sum(exp_new, axis=-1, keepdims=True)
    prob_old = (exp_old / total).astype(BF16)
    prob_new = (exp_new / total).astype(BF16)
    out = jnp.einsum("rjgc,rcjh->rjgh", prob_old, values, preferred_element_type=F32)
    out = out + jnp.einsum("rjgs,srjh->rjgh", prob_new, fresh_v, preferred_element_type=F32)
    return out.reshape(out.shape[0], -1)


def pairs(axis, k):
    return [(i, i ^ k) for i in range(lax.axis_size(axis))]


def hand_out(normed, c):
    r = normed.shape[0]
    n = normed.reshape(r, 4, 2, 2, BLK)
    n = jnp.where(c == 0, n, n[:, :, :, ::-1])
    n = n.transpose(1, 2, 0, 3, 4)
    to = jnp.stack([jnp.stack([n[y ^ k] for k in range(4)], axis=2) for y in range(4)])
    to = to.reshape(1, 4, 2, 1, r, D // 2)
    to = jnp.broadcast_to(to, (2, 4, 2, 4, r, D // 2)).reshape(64, r, D // 2)
    return lax.all_to_all(to, GROUP, 0, 0).reshape(64 * r, D // 2)


def hand_back(partial, c):
    r = partial.shape[0] // 64
    got = lax.all_to_all(partial.reshape(64, r, D // 2), GROUP, 0, 0)
    got = got.reshape(2, 4, 2, 4, r, 4, 2, BLK).astype(F32)
    got = got.sum(axis=(0, 3))
    out = jnp.stack([sum(got[s, :, :, y ^ s] for s in range(4)) for y in range(4)])
    out = out.transpose(2, 0, 1, 3, 4)
    out = jnp.where(c == 0, out, out[:, :, :, ::-1])
    return out.reshape(r, D)


def shards(
    gate_up_master,
    gate_up_moment,
    gate_up_second,
    gate_up_grad,
    down_master,
    down_moment,
    down_second,
    down_grad,
    norm_gain,
    start_rows,
    queries,
    new_kv,
    kv_pool,
    page_table,
    cache_len,
):
    y, xl, c = (lax.axis_index(a) for a in ("y", "xl", "c"))
    y1, xl1 = y.astype(jnp.int32)[None], xl.astype(jnp.int32)[None]
    local_squares = jnp.sum(jnp.square(gate_up_grad.astype(F32))) + jnp.sum(
        jnp.square(down_grad.astype(F32))
    )
    squares = lax.all_to_all(jnp.broadcast_to(local_squares, (128, 128)), ALL, 0, 0)
    total = jnp.sum(squares[:, 0])
    clip = jnp.minimum(1.0, 1.0 / jnp.sqrt(total))[None]
    wide = gate_up_master.shape[2] // 4
    pad = -(-wide // 128) * 128
    gate_up = updated(
        gate_up_body,
        y1,
        clip,
        (gate_up_master, gate_up_moment, gate_up_second, gate_up_grad),
        2 * wide,
        32,
    )
    down_t = updated(
        down_body, y1, clip, (down_master, down_moment, down_second, down_grad), pad, 64
    )

    def collect(pieces):
        blocks = []
        for k, piece in enumerate(pieces):
            mine = piece if k == 0 else lax.ppermute(piece, "y", pairs("y", k))
            blocks += [mine, lax.ppermute(mine, "c", pairs("c", 1))]
        return blocks

    gate_up = collect(gate_up)
    down_t = collect(down_t)

    local_rows = start_rows.shape[0]
    key_heads = new_kv.shape[-1] // HD
    cache = kv_pool[page_table].reshape(local_rows, -1, 2, key_heads, HD)
    keys = cache[:, :, 0]
    values = cache[:, :, 1]
    valid = jnp.arange(keys.shape[1], dtype=jnp.int32)[None, :] < cache_len[:, None]
    fresh = new_kv.reshape(new_kv.shape[0], local_rows, 2, key_heads, HD)
    rows = start_rows
    attended = [
        attend(
            queries[step].reshape(local_rows, key_heads, -1, HD),
            keys,
            values,
            valid,
            fresh[:, :, 0],
            fresh[:, :, 1],
            step,
        )
        for step in range(queries.shape[0])
    ]
    for step in range(queries.shape[0]):
        mixed = (rows.astype(F32) + attended[step]).astype(BF16)
        mixed_f = mixed.astype(F32)
        normed = (
            mixed_f
            * lax.rsqrt(jnp.mean(mixed_f * mixed_f, axis=-1, keepdims=True) + norm_eps)
            * norm_gain
        ).astype(BF16)
        whole = hand_out(normed, c)
        send, keep = first_products(xl1, whole, gate_up)
        other = lax.ppermute(send, "xl", pairs("xl", 1))
        hidden = pl.pallas_call(
            hidden_body, out_shape=jax.ShapeDtypeStruct((keep.shape[0], pad), BF16)
        )(keep, other)
        hidden_other = lax.ppermute(hidden, "xl", pairs("xl", 1))
        partial = second_products(xl1, hidden, hidden_other, down_t)
        rows = (mixed_f + hand_back(partial, c)).astype(BF16)
    return rows


def solution(mesh):
    fine = Mesh(mesh.devices.reshape(2, 4, 2, 2, 4), ALL)
    fsdp, cols, rows = ("y", "xl", "c"), ("xh", "z"), ALL
    in_specs = (
        *[P(None, fsdp, cols)] * 4,
        *[P(fsdp, cols)] * 4,
        P(),
        P(rows, None),
        P(None, rows, None),
        P(None, rows, None, None),
        P(rows, None, None, None),
        P(rows, None),
        P(rows),
    )
    return jax.shard_map(
        shards, mesh=fine, in_specs=in_specs, out_specs=P(rows, None), check_vma=False
    )
```

time: 1190 us -> 310 us (0.26)
  waiting for transfers between devices: 969 us -> 89.9 us
  starting transfers between devices: 9.11 us -> 44.6 us
  Pallas kernels: 0 us -> 32.8 us
  local copies, waits for them, and re-layouts: 69.8 us -> 45.1 us
  matrix products: 32.6 us -> 10.1 us
  between operations: 15.8 us -> 2.55 us
    reduce_scatter x2 -> x0, waiting for transfers between devices: 594 us -> none  [shards(): lax.psum_scatter(lax.dot_general(hidden, roll_down, (((1,), (1,)), ((), (...]
    all_gather x4 -> x0, waiting for transfers between devices: 329 us -> none  [the longest x2 280 us: shards(): whole = lax.all_gather(normed, ('fsdp', 'tp'), axis=0, tiled=True)]
    all_to_all x0 -> x2, blocking collectives: none -> 71.6 us  [the longest x1 36.4 us: hand_back(): got = lax.all_to_all(partial.reshape(64, r, D // 2), GROUP, 0, 0)]
    psum x1 -> x0, blocking collectives: 68.2 us -> none  [shards(): total = lax.psum(local_squares, ('rep', 'fsdp', 'tp'))]
    ppermute x0 -> x18, waiting for transfers between devices: none -> 68.1 us  [the longest x6 43.5 us: collect(): mine = piece if k == 0 else lax.ppermute(piece, 'y', pairs('y', k))]
    pallas_call x0 -> x8, Pallas kernels: none -> 32.8 us  [the longest x2 13.3 us: updated(): pl.pallas_call(body, grid=(rows // tile,), in_specs=[smem, smem] + [spec]...]
    unnamed x29 -> x48, local copies, waits for them, and re-layouts: 33.1 us -> 5.45 us
    all_to_all x2 -> x3, waiting for transfers between devices: 45.9 us -> 21.8 us  [the longest x1 21.8 us: hand_back(): got = lax.all_to_all(partial.reshape(64, r, D // 2), GROUP, 0, 0)]
  transfers between devices with their start and end apart: 8 -> 21, of which waited for: 6 -> 11; matrix products, arithmetic and copies ran while one was open for 6% -> 13% of each run, Pallas kernels for 0% -> 5%
where the time goes in v1:
time: 310 us; the launch traced here: 308 us
  waiting for transfers between devices  89.9 us (29%)
  blocking collectives  71.6 us (23%)
  local copies, waits for them, and re-layouts  45.1 us (15%)
  starting transfers between devices  44.6 us (14%)
  Pallas kernels  32.8 us (11%)
  other arithmetic  11.2 us (4%)
  matrix products  10.1 us (3%)
    ppermute x6, waiting for transfers between devices, collect(): mine = piece if k == 0 else lax.ppermute(piece, 'y', pairs('y', k))  43.5 us
    all_to_all x1, blocking collectives, hand_back(): got = lax.all_to_all(partial.reshape(64, r, D // 2), GROUP, 0, 0)  36.4 us
    all_to_all x1, blocking collectives, hand_out(): return lax.all_to_all(to, GROUP, 0, 0).reshape(64 * r, D // 2)  35.2 us
    all_to_all x1, waiting for transfers between devices, hand_back(): got = lax.all_to_all(partial.reshape(64, r, D // 2), GROUP, 0, 0)  21.8 us
    ppermute x2, waiting for transfers between devices, shards(): hidden_other = lax.ppermute(hidden, 'xl', pairs('xl', 1))  13.8 us
    pallas_call x2, Pallas kernels, updated(): pl.pallas_call(body, grid=(rows // tile,), in_specs=[smem, smem] + [spec]...  13.3 us
    gather x1, local copies, waits for them, and re-layouts, shards(): cache = kv_pool[page_table].reshape(local_rows, -1, 2, key_heads, HD)  13 us
    all_to_all x1, starting transfers between devices, shards(): lax.all_to_all(jnp.broadcast_to(local_squares, (128, 128)), ALL, 0, 0)  11.2 us
  transfers between devices with their start and end apart: 21, of which 11 were waited for; matrix products, arithmetic and copies ran while one was open for 13% of the time, Pallas kernels for 5%

profile of v1, /device:TPU:0, one launch (start us, length us, event | category | flops | bytes accessed | tf_op | source)
XLA Modules:
  0.0 307.9 jit_solution(17643680844352511588)
XLA Ops:
  0.0 3.1 %multiply_reduce_fusion = f32[]{:T(128)} fusion(bf16[2,256,1792]{2,1,0:T(8,128)(2,1)} %grad.2), kind=kLoop, calls=%fused_computation.3 | loop fusion | flops 2752511 | bytes 1835012 | tf_op jit(solution)/shard_map/reduce_sum | solution.py:206
  3.2 1.1 multiply_reduce_fusion.1
  6.2 11.2 %all-to-all-start.1 = ((f32[128,1,128]{2,1,0:T(1,128)}), f32[128,1,128]{2,1,0:T(1,128)S(1)}, u32[]{:S(2)}, u32[]{:S(2)}) async-start(f32[128,1,128]{2,1,0:T(1,128)} %broadcast_in_dim.90), calls=%async_computation.1 | async-start | bytes 131072 | tf_op jit(solution)/shard_map/all_to_all | solution.py:209
  18.2 13.0 %gather_fusion = bf16[64,16,2,1024]{3,2,1,0:T(2,128)(2,1)} fusion(bf16[64,16,2,1024]{3,2,1,0:T(2,128)(2,1)} %param.27, s32[1024]{0:T(1024)S(1)} %pad_clamp_fusion), kind=kCustom, calls=%fused_computation | custom fusion | bytes 8388864 | tf_op jit(solution)/shard_map/gather | solution.py:238
  31.2 7.6 %reshape.481 = bf16[8,128,2,8,128]{4,3,2,1,0:T(8,128)(2,1)} reshape(bf16[64,16,2,1024]{3,2,1,0:T(2,128)(2,1)} %gather_fusion) | data formatting | bytes 8388608 | tf_op jit(solution)/shard_map/reshape | solution.py:238
  38.8 3.9 %fusion.63 = (bf16[8,128,1,8,128]{4,3,2,1,0:T(8,128)(2,1)S(1)}, bf16[8,128,1,8,128]{4,3,2,1,0:T(8,128)(2,1)}) fusion(bf16[8,128,2,8,128]{4,3,2,1,0:T(8,128)(2,1)} %reshape.481), kind=kLoop, calls=%fused_computation.153 | loop fusion | bytes 8388608 | tf_op jit(solution)/shard_map/slice | solution.py:240
  43.1 3.2 %fusion.68 = (f32[8,8,4]{2,1,0:T(8,128)S(1)}, f32[8,8,4,128]{3,2,1,0:T(4,128)S(1)}) fusion(bf16[8,8,4,128]{3,2,1,0:T(4,128)(2,1)S(1)} %reshape_squeeze.6, bf16[8,128,1,8,128]{4,3,2,1,0:T(8,128)(2,1)} %get-tuple-element.34, pred[8,128]{1,0:T(8,128)(4,1)S(1)} %iota_compare_fusion), kind=kOutput, calls=%fused_computation.158 | convolution fusion | flops 8486656 | bytes 2295808 | tf_op jit(solution)/shard_map/rjgh,rcjh->rjgc/dot_general | solution.py:145
  48.7 1.6 broadcast_in_dim.88
  50.3 10.5 %all-to-all-start = ((bf16[64,8,2048]{2,1,0:T(8,128)(2,1)}), bf16[64,8,2048]{2,1,0:T(8,128)(2,1)}, u32[]{:S(2)}, u32[]{:S(2)}) async-start(bf16[64,8,2048]{2,1,0:T(8,128)(2,1)} %bitcast.267), calls=%async_computation | async-start | bytes 4194304 | tf_op jit(solution)/shard_map/all_to_all | solution.py:173
  62.2 9.0 %shard_map.145 = (bf16[256,896]{1,0:T(8,128)(2,1)S(1)}, bf16[256,896]{1,0:T(8,128)(2,1)S(1)}, bf16[256,896]{1,0:T(8,128)(2,1)S(1)}, bf16[256,896]{1,0:T(8,128)(2,1)S(1)}) custom-call(s32[1]{0:T(128)} %bitcast.15.y_ref, f32[1]{0:T(128)} %bitcast.17.clip_ref, f32[2,256,1792]{2,1,0:T(8,128)} %master.2, f32[2,256,1792]{2,1,0:T(8,128)} %moment.2, ...), custom_call_target="tpu_custom_call" | custom-call | tf_op jit(solution)/shard_map/pallas_call | solution.py:72
  71.2 1.6 collective-permute-start.1
  72.8 2.7 collective-permute-start.3
  76.0 20.8 %collective-permute-done.1.refs_2_ = bf16[256,896]{1,0:T(8,128)(2,1)S(1)} collective-permute-done((bf16[256,896]{1,0:T(8,128)(2,1)S(1)}, bf16[256,896]{1,0:T(8,128)(2,1)S(1)}, u32[]{:S(2)}, u32[]{:S(2)}) %collective-permute-start.1) | collective-permute-done | bytes 458784 | tf_op jit(solution)/shard_map/ppermute | solution.py:229
  96.8 9.9 %collective-permute-done.3.refs_4_ = bf16[256,896]{1,0:T(8,128)(2,1)S(1)} collective-permute-done((bf16[256,896]{1,0:T(8,128)(2,1)S(1)}, bf16[256,896]{1,0:T(8,128)(2,1)S(1)}, u32[]{:S(2)}, u32[]{:S(2)}) %collective-permute-start.3) | collective-permute-done | bytes 458784 | tf_op jit(solution)/shard_map/ppermute | solution.py:229
  107.2 1.4 collective-permute-done.4.refs_5_
  109.3 4.4 %shard_map.146 = (bf16[256,896]{1,0:T(8,128)(2,1)S(1)}, f32[256,896]{1,0:T(8,128)S(1)}) custom-call(s32[1]{0:T(128)} %bitcast.5.xl_ref, bf16[512,2048]{1,0:T(8,128)(2,1)} %bitcast.14.x, bf16[256,896]{1,0:T(8,128)(2,1)S(1)} %get-tuple-element.17.refs_0_, bf16[256,896]{1,0:T(8,128)(2,1)S(1)} %collective-permute-done.refs_1_, ...), custom_call_target="tpu_custom_call" | custom-call | tf_op jit(solution)/shard_map/pallas_call | solution.py:98
  115.6 4.3 %shard_map.148 = (bf16[256,512]{1,0:T(8,128)(2,1)S(1)}, bf16[256,512]{1,0:T(8,128)(2,1)S(1)}, bf16[256,512]{1,0:T(8,128)(2,1)S(1)}, bf16[256,512]{1,0:T(8,128)(2,1)S(1)}) custom-call(s32[1]{0:T(128)} %bitcast.15.y_ref, f32[1]{0:T(128)} %bitcast.17.clip_ref, f32[256,1792]{1,0:T(8,128)S(1)} %copy-done.2, f32[256,1792]{1,0:T(8,128)S(1)} %copy-done.3, ...), custom_call_target="tpu_custom_call" | custom-call | tf_op jit(solution)/shard_map/pallas_call | solution.py:72
  119.9 1.0 collective-permute-start.10
  120.9 2.3 collective-permute-start.12
  123.2 1.5 collective-permute-start.14
  124.7 4.5 %collective-permute-done.10.refs_2_ = bf16[256,512]{1,0:T(8,128)(2,1)S(1)} collective-permute-done((bf16[256,512]{1,0:T(8,128)(2,1)S(1)}, bf16[256,512]{1,0:T(8,128)(2,1)S(1)}, u32[]{:S(2)}, u32[]{:S(2)}) %collective-permute-start.10) | collective-permute-done | bytes 262176 | tf_op jit(solution)/shard_map/ppermute | solution.py:229
  129.1 5.8 %collective-permute-done.12.refs_4_ = bf16[256,512]{1,0:T(8,128)(2,1)S(1)} collective-permute-done((bf16[256,512]{1,0:T(8,128)(2,1)S(1)}, bf16[256,512]{1,0:T(8,128)(2,1)S(1)}, u32[]{:S(2)}, u32[]{:S(2)}) %collective-permute-start.12) | collective-permute-done | bytes 262176 | tf_op jit(solution)/shard_map/ppermute | solution.py:229
  134.9 2.6 collective-permute-done.14.refs_6_
  138.3 2.2 shard_map.147.own
  141.4 8.1 %collective-permute-done.8.other = bf16[256,512]{1,0:T(8,128)(2,1)S(1)} collective-permute-done((bf16[256,512]{1,0:T(8,128)(2,1)}, bf16[256,512]{1,0:T(8,128)(2,1)S(1)}, u32[]{:S(2)}, u32[]{:S(2)}) %collective-permute-start.8) | collective-permute-done | bytes 262176 | tf_op jit(solution)/shard_map/ppermute | solution.py:270
  149.5 0.9 copy-done.4
  150.4 3.8 %shard_map.149 = bf16[512,2048]{1,0:T(8,128)(2,1)} custom-call(s32[1]{0:T(128)} %bitcast.5.xl_ref, bf16[256,512]{1,0:T(8,128)(2,1)S(1)} %copy-done.4, bf16[256,512]{1,0:T(8,128)(2,1)S(1)} %collective-permute-done.8.other, bf16[256,512]{1,0:T(8,128)(2,1)S(1)} %get-tuple-element.23.refs_0_, bf16[256,512]{1,0:T(8,128)(2,1)} %collective-permute-done.9.refs_1_, ...), custom_call_target="tpu_custom_call" | custom-call | tf_op jit(solution)/shard_map/pallas_call | solution.py:134
  154.2 9.4 %all-to-all-start.2 = ((bf16[64,8,2048]{2,1,0:T(8,128)(2,1)}), bf16[64,8,2048]{2,1,0:T(8,128)(2,1)}, u32[]{:S(2)}, u32[]{:S(2)}) async-start(bf16[64,8,2048]{2,1,0:T(8,128)(2,1)} %bitcast.18), calls=%async_computation.2 | async-start | bytes 4194304 | tf_op jit(solution)/shard_map/all_to_all | solution.py:178
  163.7 1.0 fusion.67
  164.7 3.0 fusion.66
  168.5 1.4 fusion.5
  169.8 1.6 reshape.462
  171.4 21.8 %all-to-all-done.2 = bf16[64,8,2048]{2,1,0:T(8,128)(2,1)} async-done(((bf16[64,8,2048]{2,1,0:T(8,128)(2,1)}), bf16[64,8,2048]{2,1,0:T(8,128)(2,1)}, u32[]{:S(2)}, u32[]{:S(2)}) %all-to-all-start.2) | async-done | bytes 2097184 | tf_op jit(solution)/shard_map/all_to_all | solution.py:178
  193.2 2.0 convert_reduce_fusion.1
  197.0 1.5 stack.85
  198.5 1.5 copy.141
  200.0 1.5 stack.83
  201.5 1.5 copy.140
  203.1 1.5 stack.81
  206.1 0.9 maximum_bitcast_fusion.1
  207.3 35.2 %all_to_all.29 = bf16[64,8,2048]{2,1,0:T(8,128)(2,1)} all-to-all(bf16[64,8,2048]{2,1,0:T(8,128)(2,1)S(1)} %bitcast.268), channel_id=1, replica_groups=mesh['xh'=2,'y'=4,'xl'=2,'c'=2,'z'=4] {'xh','y','xl','z'}, dimensions={0} | all-to-all | bytes 4194304 | tf_op jit(solution)/shard_map/all_to_all | solution.py:173
  242.5 4.3 %shard_map.150 = (bf16[256,896]{1,0:T(8,128)(2,1)S(1)}, f32[256,896]{1,0:T(8,128)S(1)}) custom-call(s32[1]{0:T(128)} %bitcast.5.xl_ref, bf16[512,2048]{1,0:T(8,128)(2,1)} %bitcast.265, bf16[256,896]{1,0:T(8,128)(2,1)S(1)} %get-tuple-element.17.refs_0_, bf16[256,896]{1,0:T(8,128)(2,1)S(1)} %collective-permute-done.refs_1_, ...), custom_call_target="tpu_custom_call" | custom-call | tf_op jit(solution)/shard_map/pallas_call | solution.py:98
  248.6 8.7 %collective-permute-done.16.other = bf16[256,896]{1,0:T(8,128)(2,1)S(1)} collective-permute-done((bf16[256,896]{1,0:T(8,128)(2,1)S(1)}, bf16[256,896]{1,0:T(8,128)(2,1)S(1)}, u32[]{:S(2)}, u32[]{:S(2)}) %collective-permute-start.16) | collective-permute-done | bytes 458784 | tf_op jit(solution)/shard_map/ppermute | solution.py:266
  258.2 2.2 shard_map.151.own
  261.3 5.7 %collective-permute-done.17.other = bf16[256,512]{1,0:T(8,128)(2,1)S(1)} collective-permute-done((bf16[256,512]{1,0:T(8,128)(2,1)}, bf16[256,512]{1,0:T(8,128)(2,1)S(1)}, u32[]{:S(2)}, u32[]{:S(2)}) %collective-permute-start.17) | collective-permute-done | bytes 262176 | tf_op jit(solution)/shard_map/ppermute | solution.py:270
  267.0 0.9 copy-done.5
  267.9 2.5 shard_map.152
  270.4 36.4 %all_to_all.30 = bf16[64,8,2048]{2,1,0:T(8,128)(2,1)S(1)} all-to-all(bf16[64,8,2048]{2,1,0:T(8,128)(2,1)S(1)} %bitcast.264), channel_id=1, replica_groups=mesh['xh'=2,'y'=4,'xl'=2,'c'=2,'z'=4] {'xh','y','xl','z'}, dimensions={0} | all-to-all | bytes 4194304 | tf_op jit(solution)/shard_map/all_to_all | solution.py:178
  (130 shorter events, 18.6 us)
Async XLA Ops:
  0.0 3.1 %copy-start.1 = (bf16[256,1792]{1,0:T(8,128)(2,1)S(1)}, bf16[256,1792]{1,0:T(8,128)(2,1)}, u32[]{:S(2)}) copy-start(bf16[256,1792]{1,0:T(8,128)(2,1)} %grad.3) | copy-start | bytes 2752516
  0.0 17.4 %copy-start.14 = (bf16[2,8,4096]{2,1,0:T(8,128)(2,1)S(1)}, bf16[2,8,4096]{2,1,0:T(8,128)(2,1)}, u32[]{:S(2)}) copy-start(bf16[2,8,4096]{2,1,0:T(8,128)(2,1)} %param.25) | copy-start | bytes 393220
  0.0 18.0 %copy-start.16 = (bf16[2,8,2,1024]{3,2,1,0:T(2,128)(2,1)S(1)}, bf16[2,8,2,1024]{3,2,1,0:T(2,128)(2,1)}, u32[]{:S(2)}) copy-start(bf16[2,8,2,1024]{3,2,1,0:T(2,128)(2,1)} %param.26) | copy-start | bytes 196612
  0.0 18.1 %copy-start.21 = (s32[8,8]{1,0:T(8,128)S(1)}, s32[8,8]{1,0:T(8,128)}, u32[]{:S(2)}) copy-start(s32[8,8]{1,0:T(8,128)} %param.28) | copy-start | bytes 772
  6.2 42.5 %all-to-all-start.1 = ((f32[128,1,128]{2,1,0:T(1,128)}), f32[128,1,128]{2,1,0:T(1,128)S(1)}, u32[]{:S(2)}, u32[]{:S(2)}) async-start(f32[128,1,128]{2,1,0:T(1,128)} %broadcast_in_dim.90), calls=%async_computation.1 | async-start | bytes 131072 | tf_op jit(solution)/shard_map/all_to_all | solution.py:209
  18.1 24.7 %copy-start.20 = (bf16[2,8,1,8,128]{4,3,2,1,0:T(8,128)(2,1)}, bf16[2,8,1,8,128]{4,3,2,1,0:T(8,128)(2,1)S(1)}, u32[]{:S(2)}) copy-start(bf16[2,8,1,8,128]{4,3,2,1,0:T(8,128)(2,1)S(1)} %get-tuple-element.61) | copy-start | bytes 98308
  18.1 28.7 %copy-start.18 = (bf16[2,8,1,8,128]{4,3,2,1,0:T(8,128)(2,1)}, bf16[2,8,1,8,128]{4,3,2,1,0:T(8,128)(2,1)S(1)}, u32[]{:S(2)}) copy-start(bf16[2,8,1,8,128]{4,3,2,1,0:T(8,128)(2,1)S(1)} %get-tuple-element.60) | copy-start | bytes 98308
  38.8 3.9 %copy-start.22 = (s32[8]{0:T(128)S(1)}, s32[8]{0:T(128)}, u32[]{:S(2)}) copy-start(s32[8]{0:T(128)} %param.29) | copy-start | bytes 100
  42.7 4.4 %copy-start.8 = (bf16[8,128,1,8,128]{4,3,2,1,0:T(8,128)(2,1)}, bf16[8,128,1,8,128]{4,3,2,1,0:T(8,128)(2,1)S(1)}, u32[]{:S(2)}) copy-start(bf16[8,128,1,8,128]{4,3,2,1,0:T(8,128)(2,1)S(1)} %get-tuple-element.33) | copy-start | bytes 6291460
  42.8 3.8 %copy-start.23 = (pred[8,128]{1,0:T(8,128)(4,1)}, pred[8,128]{1,0:T(8,128)(4,1)S(1)}, u32[]{:S(2)}) copy-start(pred[8,128]{1,0:T(8,128)(4,1)S(1)} %iota_compare_fusion) | copy-start | bytes 3076
  47.1 0.9 copy-start.17
  47.1 1.0 copy-start.15
  50.3 11.8 %copy-start = (bf16[2,256,1792]{2,1,0:T(8,128)(2,1)S(1)}, bf16[2,256,1792]{2,1,0:T(8,128)(2,1)}, u32[]{:S(2)}) copy-start(bf16[2,256,1792]{2,1,0:T(8,128)(2,1)} %grad.2) | copy-start | bytes 5505028
  50.3 58.9 %all-to-all-start = ((bf16[64,8,2048]{2,1,0:T(8,128)(2,1)}), bf16[64,8,2048]{2,1,0:T(8,128)(2,1)}, u32[]{:S(2)}, u32[]{:S(2)}) async-start(bf16[64,8,2048]{2,1,0:T(8,128)(2,1)} %bitcast.267), calls=%async_computation | async-start | bytes 4194304 | tf_op jit(solution)/shard_map/all_to_all | solution.py:173
  71.2 25.5 %collective-permute-start.1 = (bf16[256,896]{1,0:T(8,128)(2,1)S(1)}, bf16[256,896]{1,0:T(8,128)(2,1)S(1)}, u32[]{:S(2)}, u32[]{:S(2)}) collective-permute-start(bf16[256,896]{1,0:T(8,128)(2,1)S(1)} %get-tuple-element.18), channel_id=1, source_target_pairs={{0,16},{16,0},{32,48},{48,32},{1,17},{17,1},{33,49},{49,33},{2,18}... | collective-permute-start | bytes 1376264 | tf_op jit(solution)/shard_map/ppermute | solution.py:229
  72.8 33.9 %collective-permute-start.3 = (bf16[256,896]{1,0:T(8,128)(2,1)S(1)}, bf16[256,896]{1,0:T(8,128)(2,1)S(1)}, u32[]{:S(2)}, u32[]{:S(2)}) collective-permute-start(bf16[256,896]{1,0:T(8,128)(2,1)S(1)} %get-tuple-element.19), channel_id=1, source_target_pairs={{0,32},{16,48},{32,0},{48,16},{1,33},{17,49},{33,1},{49,17},{2,34}... | collective-permute-start | bytes 1376264 | tf_op jit(solution)/shard_map/ppermute | solution.py:229
  75.5 31.2 %collective-permute-start.5 = (bf16[256,896]{1,0:T(8,128)(2,1)S(1)}, bf16[256,896]{1,0:T(8,128)(2,1)S(1)}, u32[]{:S(2)}, u32[]{:S(2)}) collective-permute-start(bf16[256,896]{1,0:T(8,128)(2,1)S(1)} %get-tuple-element.20), channel_id=1, source_target_pairs={{0,48},{16,32},{32,16},{48,0},{1,49},{17,33},{33,17},{49,1},{2,50}... | collective-permute-start | bytes 1376264 | tf_op jit(solution)/shard_map/ppermute | solution.py:229
  76.0 31.2 %collective-permute-start = (bf16[256,896]{1,0:T(8,128)(2,1)S(1)}, bf16[256,896]{1,0:T(8,128)(2,1)S(1)}, u32[]{:S(2)}, u32[]{:S(2)}) collective-permute-start(bf16[256,896]{1,0:T(8,128)(2,1)S(1)} %get-tuple-element.17.refs_0_), channel_id=1, source_target_pairs={{0,4},{4,0},{1,5},{5,1},{2,6},{6,2},{3,7},{7,3},{8,12},{12,8},{9,1... | collective-permute-start | bytes 1376264 | tf_op jit(solution)/shard_map/ppermute | solution.py:230
  96.8 10.4 %collective-permute-start.2 = (bf16[256,896]{1,0:T(8,128)(2,1)S(1)}, bf16[256,896]{1,0:T(8,128)(2,1)}, u32[]{:S(2)}, u32[]{:S(2)}) collective-permute-start(bf16[256,896]{1,0:T(8,128)(2,1)S(1)} %collective-permute-done.1.refs_2_), channel_id=1, source_target_pairs={{0,4},{4,0},{1,5},{5,1},{2,6},{6,2},{3,7},{7,3},{8,12},{12,8},{9,1... | collective-permute-start | bytes 1376264 | tf_op jit(solution)/shard_map/ppermute | solution.py:230
  106.7 1.9 collective-permute-start.4
  106.7 2.6 collective-permute-start.6
  109.3 6.3 %copy-start.2 = (f32[256,1792]{1,0:T(8,128)S(1)}, f32[256,1792]{1,0:T(8,128)}, u32[]{:S(2)}) copy-start(f32[256,1792]{1,0:T(8,128)} %master.3) | copy-start | bytes 5505028
  109.3 6.3 %copy-start.3 = (f32[256,1792]{1,0:T(8,128)S(1)}, f32[256,1792]{1,0:T(8,128)}, u32[]{:S(2)}) copy-start(f32[256,1792]{1,0:T(8,128)} %moment.3) | copy-start | bytes 5505028
  113.7 0.9 copy-start.6
  114.6 22.9 %collective-permute-start.7 = (bf16[256,896]{1,0:T(8,128)(2,1)S(1)}, bf16[256,896]{1,0:T(8,128)(2,1)S(1)}, u32[]{:S(2)}, u32[]{:S(2)}) collective-permute-start(bf16[256,896]{1,0:T(8,128)(2,1)S(1)} %get-tuple-element.22), channel_id=1, source_target_pairs={{0,8},{8,0},{1,9},{9,1},{2,10},{10,2},{3,11},{11,3},{4,12},{12,4},... | collective-permute-start | bytes 1376264 | tf_op jit(solution)/shard_map/ppermute | solution.py:266
  119.9 9.3 %collective-permute-start.10 = (bf16[256,512]{1,0:T(8,128)(2,1)S(1)}, bf16[256,512]{1,0:T(8,128)(2,1)S(1)}, u32[]{:S(2)}, u32[]{:S(2)}) collective-permute-start(bf16[256,512]{1,0:T(8,128)(2,1)S(1)} %get-tuple-element.24), channel_id=1, source_target_pairs={{0,16},{16,0},{32,48},{48,32},{1,17},{17,1},{33,49},{49,33},{2,18}... | collective-permute-start | bytes 786440 | tf_op jit(solution)/shard_map/ppermute | solution.py:229
  120.9 14.1 %collective-permute-start.12 = (bf16[256,512]{1,0:T(8,128)(2,1)S(1)}, bf16[256,512]{1,0:T(8,128)(2,1)S(1)}, u32[]{:S(2)}, u32[]{:S(2)}) collective-permute-start(bf16[256,512]{1,0:T(8,128)(2,1)S(1)} %get-tuple-element.25), channel_id=1, source_target_pairs={{0,32},{16,48},{32,0},{48,16},{1,33},{17,49},{33,1},{49,17},{2,34}... | collective-permute-start | bytes 786440 | tf_op jit(solution)/shard_map/ppermute | solution.py:229
  123.2 14.3 %collective-permute-start.14 = (bf16[256,512]{1,0:T(8,128)(2,1)S(1)}, bf16[256,512]{1,0:T(8,128)(2,1)S(1)}, u32[]{:S(2)}, u32[]{:S(2)}) collective-permute-start(bf16[256,512]{1,0:T(8,128)(2,1)S(1)} %get-tuple-element.26), channel_id=1, source_target_pairs={{0,48},{16,32},{32,16},{48,0},{1,49},{17,33},{33,17},{49,1},{2,50}... | collective-permute-start | bytes 786440 | tf_op jit(solution)/shard_map/ppermute | solution.py:229
  124.7 16.7 %collective-permute-start.9 = (bf16[256,512]{1,0:T(8,128)(2,1)S(1)}, bf16[256,512]{1,0:T(8,128)(2,1)}, u32[]{:S(2)}, u32[]{:S(2)}) collective-permute-start(bf16[256,512]{1,0:T(8,128)(2,1)S(1)} %get-tuple-element.23.refs_0_), channel_id=1, source_target_pairs={{0,4},{4,0},{1,5},{5,1},{2,6},{6,2},{3,7},{7,3},{8,12},{12,8},{9,1... | collective-permute-start | bytes 786440 | tf_op jit(solution)/shard_map/ppermute | solution.py:230
  129.1 12.2 %collective-permute-start.11 = (bf16[256,512]{1,0:T(8,128)(2,1)S(1)}, bf16[256,512]{1,0:T(8,128)(2,1)}, u32[]{:S(2)}, u32[]{:S(2)}) collective-permute-start(bf16[256,512]{1,0:T(8,128)(2,1)S(1)} %collective-permute-done.10.refs_2_), channel_id=1, source_target_pairs={{0,4},{4,0},{1,5},{5,1},{2,6},{6,2},{3,7},{7,3},{8,12},{12,8},{9,1... | collective-permute-start | bytes 786440 | tf_op jit(solution)/shard_map/ppermute | solution.py:230
  134.9 6.4 %collective-permute-start.13 = (bf16[256,512]{1,0:T(8,128)(2,1)S(1)}, bf16[256,512]{1,0:T(8,128)(2,1)}, u32[]{:S(2)}, u32[]{:S(2)}) collective-permute-start(bf16[256,512]{1,0:T(8,128)(2,1)S(1)} %collective-permute-done.12.refs_4_), channel_id=1, source_target_pairs={{0,4},{4,0},{1,5},{5,1},{2,6},{6,2},{3,7},{7,3},{8,12},{12,8},{9,1... | collective-permute-start | bytes 786440 | tf_op jit(solution)/shard_map/ppermute | solution.py:230
  137.5 3.8 %collective-permute-start.15 = (bf16[256,512]{1,0:T(8,128)(2,1)S(1)}, bf16[256,512]{1,0:T(8,128)(2,1)}, u32[]{:S(2)}, u32[]{:S(2)}) collective-permute-start(bf16[256,512]{1,0:T(8,128)(2,1)S(1)} %collective-permute-done.14.refs_6_), channel_id=1, source_target_pairs={{0,4},{4,0},{1,5},{5,1},{2,6},{6,2},{3,7},{7,3},{8,12},{12,8},{9,1... | collective-permute-start | bytes 786440 | tf_op jit(solution)/shard_map/ppermute | solution.py:230
  137.5 0.8 copy-start.11
  140.5 8.9 %collective-permute-start.8 = (bf16[256,512]{1,0:T(8,128)(2,1)}, bf16[256,512]{1,0:T(8,128)(2,1)S(1)}, u32[]{:S(2)}, u32[]{:S(2)}) collective-permute-start(bf16[256,512]{1,0:T(8,128)(2,1)} %shard_map.147.own), channel_id=1, source_target_pairs={{0,8},{8,0},{1,9},{9,1},{2,10},{10,2},{3,11},{11,3},{4,12},{12,4},... | collective-permute-start | bytes 786440 | tf_op jit(solution)/shard_map/ppermute | solution.py:270
  149.5 1.0 copy-start.4
  154.2 9.4 %copy-start.13 = (bf16[1,8,4096]{2,1,0:T(8,128)(2,1)S(1)}, bf16[1,8,4096]{2,1,0:T(8,128)(2,1)}, u32[]{:S(2)}) copy-start(bf16[1,8,4096]{2,1,0:T(8,128)(2,1)} %get-tuple-element.43) | copy-start | bytes 196612
  154.2 39.0 %all-to-all-start.2 = ((bf16[64,8,2048]{2,1,0:T(8,128)(2,1)}), bf16[64,8,2048]{2,1,0:T(8,128)(2,1)}, u32[]{:S(2)}, u32[]{:S(2)}) async-start(bf16[64,8,2048]{2,1,0:T(8,128)(2,1)} %bitcast.18), calls=%async_computation.2 | async-start | bytes 4194304 | tf_op jit(solution)/shard_map/all_to_all | solution.py:178
  163.7 4.5 %copy-start.19 = (bf16[2,8,1,8,128]{4,3,2,1,0:T(8,128)(2,1)S(1)}, bf16[2,8,1,8,128]{4,3,2,1,0:T(8,128)(2,1)}, u32[]{:S(2)}) copy-start(bf16[2,8,1,8,128]{4,3,2,1,0:T(8,128)(2,1)} %copy-done.18) | copy-start | bytes 98308
  164.7 3.7 %copy-start.9 = (bf16[8,128,1,8,128]{4,3,2,1,0:T(8,128)(2,1)S(1)}, bf16[8,128,1,8,128]{4,3,2,1,0:T(8,128)(2,1)}, u32[]{:S(2)}) copy-start(bf16[8,128,1,8,128]{4,3,2,1,0:T(8,128)(2,1)} %copy-done.8) | copy-start | bytes 6291460
  193.2 2.1 copy-start.10
  246.8 0.9 copy-start.7
  247.8 9.6 %collective-permute-start.16 = (bf16[256,896]{1,0:T(8,128)(2,1)S(1)}, bf16[256,896]{1,0:T(8,128)(2,1)S(1)}, u32[]{:S(2)}, u32[]{:S(2)}) collective-permute-start(bf16[256,896]{1,0:T(8,128)(2,1)S(1)} %get-tuple-element.28), channel_id=1, source_target_pairs={{0,8},{8,0},{1,9},{9,1},{2,10},{10,2},{3,11},{11,3},{4,12},{12,4},... | collective-permute-start | bytes 1376264 | tf_op jit(solution)/shard_map/ppermute | solution.py:266
  257.4 0.8 copy-start.12
  260.4 6.6 %collective-permute-start.17 = (bf16[256,512]{1,0:T(8,128)(2,1)}, bf16[256,512]{1,0:T(8,128)(2,1)S(1)}, u32[]{:S(2)}, u32[]{:S(2)}) collective-permute-start(bf16[256,512]{1,0:T(8,128)(2,1)} %shard_map.151.own), channel_id=1, source_target_pairs={{0,8},{8,0},{1,9},{9,1},{2,10},{10,2},{3,11},{11,3},{4,12},{12,4},... | collective-permute-start | bytes 786440 | tf_op jit(solution)/shard_map/ppermute | solution.py:270
  267.0 1.0 copy-start.5

commit v2 on v1

v2 whole, which is shorter than its diff:
```python
import jax
import jax.numpy as jnp
from jax import lax
from jax.experimental import pallas as pl
from jax.experimental.pallas import tpu as pltpu
from jax.sharding import Mesh, PartitionSpec as P

D = 4096
HD = 128
BLK = 256

beta_one = 0.9
beta_two = 0.95
adam_eps = 1e-08
adam_time = 100.0
norm_eps = 1e-05

ALL = ("xh", "y", "xl", "c", "z")
GROUP = ("xh", "y", "xl", "z")
F32 = jnp.float32
BF16 = jnp.bfloat16


def adam_new(master, moment, second, grad, clip):
    first_fix = 1.0 - beta_one**adam_time
    second_fix = 1.0 - beta_two**adam_time
    rate = 2.0 / D**0.5 / first_fix
    g = grad.astype(F32)
    m = (rate * beta_one) * moment + (rate * (1.0 - beta_one) * clip) * g
    v = (beta_two / second_fix) * second + ((1.0 - beta_two) / second_fix * (clip * clip)) * (g * g)
    return master - m / (v * lax.rsqrt(v) + adam_eps)


def squares_body(first, second, out, acc):
    step = pl.program_id(0)

    @pl.when(step == 0)
    def _():
        acc[...] = jnp.zeros(acc.shape, F32)

    total = acc[...]
    for block in (first[0], first[1], second[...]):
        for lo in range(0, block.shape[0], 8):
            x = block[lo : lo + 8].astype(F32)
            total = total + x * x
    acc[...] = total

    @pl.when(step == pl.num_programs(0) - 1)
    def _():
        out[...] = jnp.full(out.shape, jnp.sum(acc[...]), F32)


def sum_of_squares(first, second, tile):
    rows, cols = second.shape
    return pl.pallas_call(
        squares_body,
        grid=(rows // tile,),
        in_specs=[
            pl.BlockSpec((2, tile, cols), lambda i: (0, i, 0)),
            pl.BlockSpec((tile, cols), lambda i: (i, 0)),
        ],
        out_specs=pl.BlockSpec((128, 128), lambda i: (0, 0)),
        out_shape=jax.ShapeDtypeStruct((128, 128), F32),
        scratch_shapes=[pltpu.VMEM((8, cols), F32)],
        compiler_params=pltpu.CompilerParams(vmem_limit_bytes=48 << 20),
    )(first, second)


def gate_up_body(y_ref, clip_ref, master, moment, second, grad, *outs):
    clip = clip_ref[0]
    y = y_ref[0]
    wide = master.shape[2] // 4
    new = [
        adam_new(master[s], moment[s], second[s], grad[s], clip).astype(BF16) for s in range(2)
    ]
    for me in range(4):

        @pl.when(y == me)
        def _():
            for k, out in enumerate(outs):
                lo = (me ^ k) * wide
                out[:, :wide] = new[0][:, lo : lo + wide]
                out[:, wide:] = new[1][:, lo : lo + wide]


def down_body(y_ref, clip_ref, master, moment, second, grad, *outs):
    clip = clip_ref[0]
    y = y_ref[0]
    wide = master.shape[1] // 4
    new = adam_new(master[...], moment[...], second[...], grad[...], clip).astype(BF16)
    for me in range(4):

        @pl.when(y == me)
        def _():
            for k, out in enumerate(outs):
                lo = (me ^ k) * wide
                out[:, :wide] = new[:, lo : lo + wide]
                out[:, wide:] = jnp.zeros((out.shape[0], out.shape[1] - wide), BF16)


def updated(body, y, clip, arrays, width, tile):
    stack = arrays[0].shape[:-2]
    rows, cols = arrays[0].shape[-2:]
    zeros = (0,) * len(stack)
    spec = pl.BlockSpec(stack + (tile, cols), lambda i: zeros + (i, 0))
    smem = pl.BlockSpec(memory_space=pltpu.SMEM)
    return pl.pallas_call(
        body,
        grid=(rows // tile,),
        in_specs=[smem, smem] + [spec] * 4,
        out_specs=[pl.BlockSpec((tile, width), lambda i: (i, 0))] * 4,
        out_shape=[jax.ShapeDtypeStruct((rows, width), BF16)] * 4,
        compiler_params=pltpu.CompilerParams(vmem_limit_bytes=48 << 20),
    )(y, clip, *arrays)


def first_body(xl_ref, x, *refs):
    blocks, (send, keep) = refs[:-2], refs[-2:]
    half = x.shape[0] // 2
    xl = xl_ref[0]
    for out, part in ((send, 1 - xl), (keep, xl)):
        acc = None
        for b, w in enumerate(blocks):
            lhs = x[pl.ds(pl.multiple_of(part * half, half), half), b * BLK : (b + 1) * BLK]
            dot = jnp.dot(lhs, w[...], preferred_element_type=F32)
            acc = dot if acc is None else acc + dot
        out[...] = acc.astype(out.dtype)


def first_products(xl, x, blocks):
    half, width = x.shape[0] // 2, blocks[0].shape[1]
    vmem = pl.BlockSpec(memory_space=pltpu.VMEM)
    return pl.pallas_call(
        first_body,
        in_specs=[pl.BlockSpec(memory_space=pltpu.SMEM)] + [vmem] * (1 + len(blocks)),
        out_specs=[vmem, vmem],
        out_shape=[
            jax.ShapeDtypeStruct((half, width), BF16),
            jax.ShapeDtypeStruct((half, width), F32),
        ],
        compiler_params=pltpu.CompilerParams(vmem_limit_bytes=48 << 20),
    )(xl, x, *blocks)


def hidden_body(keep, other, out):
    both = keep[...] + other[...].astype(F32)
    wide = both.shape[1] // 2
    gate, upper = both[:, :wide], both[:, wide:]
    out[:, :wide] = (gate * jax.nn.sigmoid(gate) * upper).astype(BF16)
    out[:, wide:] = jnp.zeros((out.shape[0], out.shape[1] - wide), BF16)


def hidden_units(keep, other, width):
    vmem = pl.BlockSpec(memory_space=pltpu.VMEM)
    return pl.pallas_call(
        hidden_body,
        in_specs=[vmem, vmem],
        out_specs=vmem,
        out_shape=jax.ShapeDtypeStruct((keep.shape[0], width), BF16),
    )(keep, other)


def second_body(xl_ref, own, other, *refs):
    blocks, out = refs[:-1], refs[-1]
    half = own.shape[0]
    xl = xl_ref[0]
    for h, part in ((own, xl), (other, 1 - xl)):
        for b, w in enumerate(blocks):
            dot = lax.dot_general(
                h[...], w[...], (((1,), (1,)), ((), ())), preferred_element_type=F32
            )
            out[pl.ds(pl.multiple_of(part * half, half), half), b * BLK : (b + 1) * BLK] = (
                dot.astype(BF16)
            )


def second_products(xl, own, other, blocks):
    vmem = pl.BlockSpec(memory_space=pltpu.VMEM)
    return pl.pallas_call(
        second_body,
        in_specs=[pl.BlockSpec(memory_space=pltpu.SMEM)] + [vmem] * (2 + len(blocks)),
        out_specs=vmem,
        out_shape=jax.ShapeDtypeStruct((2 * own.shape[0], BLK * len(blocks)), BF16),
        compiler_params=pltpu.CompilerParams(vmem_limit_bytes=48 << 20),
    )(xl, own, other, *blocks)


def attention_body(pages, lens, q_ref, fresh_ref, kv_ref, out_ref, q32, fresh32, q_rows):
    steps, rows, _ = q_ref.shape
    heads = kv_ref.shape[2] // HD
    group = q_ref.shape[2] // HD // heads
    n_pages = kv_ref.shape[0] // rows
    per_head = steps * group
    count = heads * per_head
    scale = HD**-0.5
    q32[...] = q_ref[...].astype(F32)
    fresh32[...] = fresh_ref[...].astype(F32)
    ctx = n_pages * kv_ref.shape[1]
    lane = lax.broadcasted_iota(jnp.int32, (count, ctx), 1)
    step_of = lax.broadcasted_iota(jnp.int32, (count, 1), 0) % per_head // group
    for r in range(rows):
        for j in range(heads):
            for s in range(steps):
                for g in range(group):
                    at = r * count + j * per_head + s * group + g
                    lo = (j * group + g) * HD
                    q_rows[at : at + 1, :] = q32[s, r : r + 1, lo : lo + HD]

    def spread(t, r, first):
        parts = []
        for j in range(heads):
            lo = (first + j) * HD
            row = fresh32[t, r : r + 1, lo : lo + HD]
            parts.append(jnp.broadcast_to(row, (per_head, HD)))
        return jnp.concatenate(parts, axis=0)

    for r in range(rows):
        kv = [kv_ref[pages[r * n_pages + p]] for p in range(n_pages)]
        head_kv = [
            jnp.concatenate([page[:, j * HD : (j + 1) * HD] for page in kv], axis=0)
            for j in range(heads)
        ]
        q = q_rows[r * count : (r + 1) * count, :]
        q_low = q.astype(BF16)
        old = jnp.concatenate(
            [
                lax.dot_general(
                    q_low[j * per_head : (j + 1) * per_head],
                    head_kv[j],
                    (((1,), (1,)), ((), ())),
                    preferred_element_type=F32,
                )
                for j in range(heads)
            ],
            axis=0,
        )
        usable = (lane % 2 == 0) & (lane // 2 < lens[r])
        old = jnp.where(usable, old * scale, -1e30)
        top = jnp.max(old, axis=-1, keepdims=True)
        new = []
        for t in range(steps):
            score = jnp.sum(q * spread(t, r, 0), axis=-1, keepdims=True) * scale
            score = jnp.where(step_of >= t, score, -1e30)
            top = jnp.maximum(top, score)
            new.append(score)
        old = jnp.exp(old - top)
        new = [jnp.exp(n - top) for n in new]
        total = jnp.sum(old, axis=-1, keepdims=True) + sum(new)
        weights = pltpu.roll(old / total, 1, axis=1).astype(BF16)
        out = jnp.concatenate(
            [
                jnp.dot(
                    weights[j * per_head : (j + 1) * per_head],
                    head_kv[j],
                    preferred_element_type=F32,
                )
                for j in range(heads)
            ],
            axis=0,
        )
        for t in range(steps):
            out = out + (new[t] / total).astype(BF16).astype(F32) * spread(t, r, heads)
        for j in range(heads):
            for s in range(steps):
                for g in range(group):
                    lo = (j * group + g) * HD
                    at = j * per_head + s * group + g
                    out_ref[s, r : r + 1, lo : lo + HD] = out[at : at + 1, :]


def attention(page_table, cache_len, queries, new_kv, kv_pool):
    steps, rows, width = queries.shape
    kv_width = new_kv.shape[-1]
    fresh = new_kv.reshape(steps, rows, 2 * kv_width)
    pool = kv_pool.reshape(kv_pool.shape[0], -1, kv_width)
    smem, vmem = (pl.BlockSpec(memory_space=m) for m in (pltpu.SMEM, pltpu.VMEM))
    return pl.pallas_call(
        attention_body,
        in_specs=[smem, smem, vmem, vmem, vmem],
        out_specs=vmem,
        out_shape=jax.ShapeDtypeStruct((steps, rows, width), F32),
        scratch_shapes=[
            pltpu.VMEM((steps, rows, width), F32),
            pltpu.VMEM((steps, rows, 2 * kv_width), F32),
            pltpu.VMEM((steps * rows * width // HD, HD), F32),
        ],
        cost_estimate=pl.CostEstimate(
            flops=16 * steps * width * pool.shape[0] * pool.shape[1],
            transcendentals=steps * width // HD * pool.shape[0] * pool.shape[1],
            bytes_accessed=16 * pool.size,
        ),
        compiler_params=pltpu.CompilerParams(vmem_limit_bytes=48 << 20),
    )(page_table.reshape(-1), cache_len, queries, fresh, pool)


def pairs(axis, k):
    return [(i, i ^ k) for i in range(lax.axis_size(axis))]


def add_partials(c, got, total):
    for b in range(16):
        y, xl, cc = b // 4, b // 2 % 2, b % 2
        sums = []
        for j in range(2):
            acc = None
            for xh in range(2):
                for ys in range(4):
                    for z in range(4):
                        lo = ((y ^ ys) * 2 + j) * BLK
                        piece = got[xh * 32 + ys * 8 + xl * 4 + z, :, lo : lo + BLK].astype(F32)
                        acc = piece if acc is None else acc + piece
            sums.append(acc)
        total[:, b * BLK : (b + 1) * BLK] = jnp.where(c == 0, sums[cc], sums[1 - cc])


def normed_out(c, mixed, gain, normed, payload):
    mixed_f = mixed.astype(F32)
    normed[...] = (
        mixed_f * lax.rsqrt(jnp.mean(mixed_f * mixed_f, axis=-1, keepdims=True) + norm_eps) * gain
    )
    for y in range(4):
        for xl in range(2):
            for k in range(4):
                lo = ((y ^ k) * 4 + xl * 2) * BLK
                pair = normed[:, lo : lo + BLK], normed[:, lo + BLK : lo + 2 * BLK]
                for j in range(2):
                    piece = jnp.where(c == 0, pair[j], pair[1 - j]).astype(BF16)
                    at = (k * 2 + j) * BLK
                    for xh in range(2):
                        for z in range(4):
                            payload[xh * 32 + y * 8 + xl * 4 + z, :, at : at + BLK] = piece


def open_body(c_ref, rows, attended, gain, mixed, payload, normed):
    new = (rows[...].astype(F32) + attended[0]).astype(BF16)
    mixed[...] = new
    normed_out(c_ref[0], new, gain[...], normed, payload)


def next_body(c_ref, rows, got, attended, gain, mixed, payload, total, normed):
    add_partials(c_ref[0], got, total)
    done = (rows[...].astype(F32) + total[...]).astype(BF16)
    new = (done.astype(F32) + attended[1]).astype(BF16)
    mixed[...] = new
    normed_out(c_ref[0], new, gain[...], normed, payload)


def last_body(c_ref, rows, got, out, total):
    add_partials(c_ref[0], got, total)
    out[...] = (rows[...].astype(F32) + total[...]).astype(BF16)


def row_call(body, rows, scratch, payload, c, *arrays):
    shape = jax.ShapeDtypeStruct(rows.shape, BF16)
    if payload:
        shape = [shape, jax.ShapeDtypeStruct((64, rows.shape[0], D // 2), BF16)]
    vmem = pl.BlockSpec(memory_space=pltpu.VMEM)
    return pl.pallas_call(
        body,
        in_specs=[pl.BlockSpec(memory_space=pltpu.SMEM)] + [vmem] * (1 + len(arrays)),
        out_specs=[vmem, vmem] if payload else vmem,
        out_shape=shape,
        scratch_shapes=[pltpu.VMEM(rows.shape, F32)] * scratch,
        compiler_params=pltpu.CompilerParams(vmem_limit_bytes=48 << 20),
    )(c, rows, *arrays)


def shards(
    gate_up_master,
    gate_up_moment,
    gate_up_second,
    gate_up_grad,
    down_master,
    down_moment,
    down_second,
    down_grad,
    norm_gain,
    start_rows,
    queries,
    new_kv,
    kv_pool,
    page_table,
    cache_len,
):
    y, xl, c = (lax.axis_index(a).astype(jnp.int32)[None] for a in ("y", "xl", "c"))
    squares = sum_of_squares(gate_up_grad, down_grad, 64)
    squares = lax.all_to_all(squares, ALL, 0, 0)
    clip = jnp.minimum(1.0, 1.0 / jnp.sqrt(jnp.sum(squares[:, 0])))[None]
    wide = gate_up_master.shape[2] // 4
    pad = -(-wide // 128) * 128
    gate_up = updated(
        gate_up_body,
        y,
        clip,
        (gate_up_master, gate_up_moment, gate_up_second, gate_up_grad),
        2 * wide,
        32,
    )
    page_table, *gate_up = lax.optimization_barrier((page_table, *gate_up))
    attended = attention(page_table, cache_len, queries, new_kv, kv_pool)
    mixed, payload = row_call(open_body, start_rows, 1, True, c, attended, norm_gain[None])
    handed = lax.all_to_all(payload, GROUP, 0, 0)
    clip, payload = lax.optimization_barrier((clip, payload))
    down_t = updated(
        down_body, y, clip, (down_master, down_moment, down_second, down_grad), pad, 64
    )

    def over_y(pieces):
        return [p if k == 0 else lax.ppermute(p, "y", pairs("y", k)) for k, p in enumerate(pieces)]

    def over_c(pieces):
        return [q for p in pieces for q in (p, lax.ppermute(p, "c", pairs("c", 1)))]

    gate_up = over_c(over_y(gate_up))
    gate_up, down_t = lax.optimization_barrier((gate_up, down_t))
    down_t = over_y(down_t)

    for step in range(queries.shape[0]):
        whole = handed.reshape(-1, D // 2)
        send, keep = first_products(xl, whole, gate_up)
        other = lax.ppermute(send, "xl", pairs("xl", 1))
        hidden = hidden_units(keep, other, pad)
        if step == 0:
            down_t = over_c(lax.optimization_barrier((down_t, hidden))[0])
        hidden_other = lax.ppermute(hidden, "xl", pairs("xl", 1))
        partial = second_products(xl, hidden, hidden_other, down_t)
        got = lax.all_to_all(partial.reshape(64, -1, D // 2), GROUP, 0, 0)
        if step == 0:
            mixed, payload = row_call(next_body, mixed, 2, True, c, got, attended, norm_gain[None])
            handed = lax.all_to_all(payload, GROUP, 0, 0)
    return row_call(last_body, mixed, 1, False, c, got)


def solution(mesh):
    fine = Mesh(mesh.devices.reshape(2, 4, 2, 2, 4), ALL)
    fsdp, cols, rows = ("y", "xl", "c"), ("xh", "z"), ALL
    in_specs = (
        *[P(None, fsdp, cols)] * 4,
        *[P(fsdp, cols)] * 4,
        P(),
        P(rows, None),
        P(None, rows, None),
        P(None, rows, None, None),
        P(rows, None, None, None),
        P(rows, None),
        P(rows),
    )
    return jax.shard_map(
        shards, mesh=fine, in_specs=in_specs, out_specs=P(rows, None), check_vma=False
    )
```

time: 310 us -> 284 us (0.916)
  blocking collectives: 71.6 us -> 110 us
  local copies, waits for them, and re-layouts: 45.1 us -> 25.1 us
  waiting for transfers between devices: 89.9 us -> 72.9 us
  other arithmetic: 11.2 us -> 0.62 us
  matrix products: 10.1 us -> 0 us
  starting transfers between devices: 44.6 us -> 35.5 us
  Pallas kernels: 32.8 us -> 38 us
    all_to_all x2 -> x3, blocking collectives: 71.6 us -> 110 us  [the longest x2 74.8 us: shards(): got = lax.all_to_all(partial.reshape(64, -1, D // 2), GROUP, 0, 0)]
    all_to_all x3 -> x2, waiting for transfers between devices: 21.8 us -> 2 us  [the longest x1 2 us: shards(): squares = lax.all_to_all(squares, ALL, 0, 0)]
    gather x1 -> x0, local copies, waits for them, and re-layouts: 13 us -> none  [shards(): cache = kv_pool[page_table].reshape(local_rows, -1, 2, key_heads, HD)]
    unnamed x48 -> x60, local copies, waits for them, and re-layouts: 5.45 us -> 17.6 us
    all_to_all x3 -> x2, starting transfers between devices: 31 us -> 19.6 us  [the longest x1 11.1 us: shards(): squares = lax.all_to_all(squares, ALL, 0, 0)]
    another operation x20 -> x0, local copies, waits for them, and re-layouts: 10.2 us -> none  [the longest x8 5.5 us: hand_out(): jnp.stack([jnp.stack([n[y ^ k] for k in range(4)], axis=2) for y in range...]
    dot_general x8 -> x0, matrix products: 10.1 us -> none  [the longest x2 6.22 us: attend(): jnp.einsum('rjgh,rcjh->rjgc', query, keys, preferred_element_type=F32)]
    pallas_call x2 -> x7, Pallas kernels: 4.42 us -> 13.8 us  [the longest x1 4.65 us: attention(): pl.pallas_call(attention_body, in_specs=[smem, smem, vmem, vmem, vmem], o...]
  transfers between devices with their start and end apart: 21 -> 20, of which waited for: 11 -> 12; matrix products, arithmetic and copies ran while one was open for 13% -> 3% of each run, Pallas kernels for 5% -> 2%
where the time goes in v2:
time: 284 us; the launch traced here: 283 us
  blocking collectives  110 us (39%)
  waiting for transfers between devices  72.9 us (26%)
  Pallas kernels  38 us (13%)
  starting transfers between devices  35.5 us (12%)
  local copies, waits for them, and re-layouts  25.1 us (9%)
    all_to_all x2, blocking collectives, shards(): got = lax.all_to_all(partial.reshape(64, -1, D // 2), GROUP, 0, 0)  74.8 us
    ppermute x6, waiting for transfers between devices, over_y(): lax.ppermute(p, 'y', pairs('y', k))  44 us
    all_to_all x1, blocking collectives, shards(): handed = lax.all_to_all(payload, GROUP, 0, 0)  35 us
    unnamed x60, local copies, waits for them, and re-layouts  17.6 us
    ppermute x2, waiting for transfers between devices, shards(): other = lax.ppermute(send, 'xl', pairs('xl', 1))  14.3 us
    pallas_call x2, Pallas kernels, updated(): pl.pallas_call(body, grid=(rows // tile,), in_specs=[smem, smem] + [spec]...  12.8 us
    ppermute x2, waiting for transfers between devices, shards(): hidden_other = lax.ppermute(hidden, 'xl', pairs('xl', 1))  11.8 us
    all_to_all x1, starting transfers between devices, shards(): squares = lax.all_to_all(squares, ALL, 0, 0)  11.1 us
  transfers between devices with their start and end apart: 20, of which 12 were waited for; matrix products, arithmetic and copies ran while one was open for 3% of the time, Pallas kernels for 2%

profile of v2, /device:TPU:0, one launch (start us, length us, event | category | flops | bytes accessed | tf_op | source)
XLA Modules:
  0.0 282.9 jit_solution(17278687785908403206)
XLA Ops:
  0.0 1.5 copy-done.1
  1.5 1.2 copy-done.3
  2.7 1.5 shard_map.145
  4.2 11.1 %all-to-all-start = ((f32[128,1,128]{2,1,0:T(1,128)}), f32[128,1,128]{2,1,0:T(1,128)S(1)}, u32[]{:S(2)}, u32[]{:S(2)}) async-start(f32[128,1,128]{2,1,0:T(1,128)} %bitcast.3), calls=%async_computation | async-start | bytes 131072 | tf_op jit(solution)/shard_map/all_to_all | solution.py:387
  15.4 7.3 %reshape.25.kv_ref = bf16[64,32,1024]{2,1,0:T(8,128)(2,1)} reshape(bf16[64,16,2,1024]{3,2,1,0:T(2,128)(2,1)} %param.27) | data formatting | bytes 8388608 | tf_op jit(solution)/shard_map/reshape | solution.py:275
  22.8 2.0 all-to-all-done
  26.1 8.6 %shard_map.146 = (bf16[256,896]{1,0:T(8,128)(2,1)S(1)}, bf16[256,896]{1,0:T(8,128)(2,1)}, bf16[256,896]{1,0:T(8,128)(2,1)}, bf16[256,896]{1,0:T(8,128)(2,1)S(1)}) custom-call(s32[1]{0:T(128)} %bitcast.1.y_ref, f32[1]{0:T(128)} %bitcast.5.clip_ref, f32[2,256,1792]{2,1,0:T(8,128)} %master.2, f32[2,256,1792]{2,1,0:T(8,128)} %moment.2, f32[2,256,1792]{2,1,0:T(8,128)} %second.4, ...), custom_call_target="tpu_custom_call" | custom-call | tf_op jit(solution)/shard_map/pallas_call | solution.py:107
  35.6 2.2 copy-done
  37.8 4.6 %shard_map.147.attended = f32[2,8,4096]{2,1,0:T(8,128)S(1)} custom-call(s32[64]{0:T(128)S(1)} %reshape.23.pages, s32[8]{0:T(128)S(1)} %copy-done.22, bf16[2,8,4096]{2,1,0:T(8,128)(2,1)S(1)} %copy-done.19, bf16[2,8,2048]{2,1,0:T(8,128)(2,1)S(1)} %reshape.24.fresh_ref, bf16[64,32,1024]{2,1,0:T(8,128)(2,1)S(1)} %copy-done), custom_call_target="tpu_custom_call" | custom-call | flops 268435456 | bytes 33554432 | tf_op jit(solution)/shard_map/pallas_call | solution.py:277
  42.5 1.7 shard_map.148
  44.1 8.5 %all-to-all-start.1 = ((bf16[64,8,2048]{2,1,0:T(8,128)(2,1)}), bf16[64,8,2048]{2,1,0:T(8,128)(2,1)}, u32[]{:S(2)}, u32[]{:S(2)}) async-start(bf16[64,8,2048]{2,1,0:T(8,128)(2,1)} %get-tuple-element.49), calls=%async_computation.1 | async-start | bytes 4194304 | tf_op jit(solution)/shard_map/all_to_all | solution.py:402
  52.6 1.6 collective-permute-start.1
  54.2 2.7 collective-permute-start.3
  57.4 31.1 %collective-permute-done.1.refs_2_ = bf16[256,896]{1,0:T(8,128)(2,1)S(1)} collective-permute-done((bf16[256,896]{1,0:T(8,128)(2,1)}, bf16[256,896]{1,0:T(8,128)(2,1)S(1)}, u32[]{:S(2)}, u32[]{:S(2)}) %collective-permute-start.1) | collective-permute-done | bytes 458784 | tf_op jit(solution)/shard_map/ppermute | solution.py:409
  88.6 9.3 %collective-permute-done.3.refs_4_ = bf16[256,896]{1,0:T(8,128)(2,1)S(1)} collective-permute-done((bf16[256,896]{1,0:T(8,128)(2,1)}, bf16[256,896]{1,0:T(8,128)(2,1)S(1)}, u32[]{:S(2)}, u32[]{:S(2)}) %collective-permute-start.3) | collective-permute-done | bytes 458784 | tf_op jit(solution)/shard_map/ppermute | solution.py:409
  98.4 1.5 copy-done.5
  99.9 1.5 copy-done.6
  101.4 4.2 %shard_map.149 = (bf16[256,512]{1,0:T(8,128)(2,1)S(1)}, bf16[256,512]{1,0:T(8,128)(2,1)}, bf16[256,512]{1,0:T(8,128)(2,1)}, bf16[256,512]{1,0:T(8,128)(2,1)S(1)}) custom-call(s32[1]{0:T(128)} %bitcast.1.y_ref, f32[1]{0:T(128)} %bitcast.5.clip_ref, f32[256,1792]{1,0:T(8,128)S(1)} %copy-done.5, f32[256,1792]{1,0:T(8,128)S(1)} %copy-done.6, ...), custom_call_target="tpu_custom_call" | custom-call | tf_op jit(solution)/shard_map/pallas_call | solution.py:107
  106.4 4.5 %shard_map.150 = (bf16[256,896]{1,0:T(8,128)(2,1)S(1)}, f32[256,896]{1,0:T(8,128)S(1)}) custom-call(s32[1]{0:T(128)} %bitcast.7.xl_ref, bf16[512,2048]{1,0:T(8,128)(2,1)} %bitcast.8.x, bf16[256,896]{1,0:T(8,128)(2,1)S(1)} %get-tuple-element.59.refs_0_, bf16[256,896]{1,0:T(8,128)(2,1)} %collective-permute-done.refs_1_, ...), custom_call_target="tpu_custom_call" | custom-call | tf_op jit(solution)/shard_map/pallas_call | solution.py:133
  110.8 1.0 copy-done.17
  111.8 1.5 collective-permute-start.7
  113.3 0.9 collective-permute-start.9
  114.2 2.3 collective-permute-start.10
  116.5 1.5 collective-permute-start.11
  118.0 6.2 %collective-permute-done.7.other = bf16[256,896]{1,0:T(8,128)(2,1)S(1)} collective-permute-done((bf16[256,896]{1,0:T(8,128)(2,1)S(1)}, bf16[256,896]{1,0:T(8,128)(2,1)S(1)}, u32[]{:S(2)}, u32[]{:S(2)}) %collective-permute-start.7) | collective-permute-done | bytes 458784 | tf_op jit(solution)/shard_map/ppermute | solution.py:421
  125.0 2.2 shard_map.151.own
  127.2 1.2 collective-permute-done.10.refs_4_
  128.4 2.4 collective-permute-done.11.refs_6_
  131.8 0.8 collective-permute-start.8
  133.4 6.8 %collective-permute-done.8.other = bf16[256,512]{1,0:T(8,128)(2,1)S(1)} collective-permute-done((bf16[256,512]{1,0:T(8,128)(2,1)}, bf16[256,512]{1,0:T(8,128)(2,1)S(1)}, u32[]{:S(2)}, u32[]{:S(2)}) %collective-permute-start.8) | collective-permute-done | bytes 262176 | tf_op jit(solution)/shard_map/ppermute | solution.py:425
  140.2 0.9 copy-done.15
  141.1 1.3 shard_map.152
  142.5 37.7 %all_to_all.32.got = bf16[64,8,2048]{2,1,0:T(8,128)(2,1)S(1)} all-to-all(bf16[64,8,2048]{2,1,0:T(8,128)(2,1)S(1)} %bitcast.14), channel_id=1, replica_groups=mesh['xh'=2,'y'=4,'xl'=2,'c'=2,'z'=4] {'xh','y','xl','z'}, dimensions={0} | all-to-all | bytes 4194304 | tf_op jit(solution)/shard_map/all_to_all | solution.py:427
  180.8 35.0 %all_to_all.33 = bf16[64,8,2048]{2,1,0:T(8,128)(2,1)} all-to-all(bf16[64,8,2048]{2,1,0:T(8,128)(2,1)S(1)} %get-tuple-element.78), channel_id=1, replica_groups=mesh['xh'=2,'y'=4,'xl'=2,'c'=2,'z'=4] {'xh','y','xl','z'}, dimensions={0} | all-to-all | bytes 4194304 | tf_op jit(solution)/shard_map/all_to_all | solution.py:430
  215.8 4.5 %shard_map.154 = (bf16[256,896]{1,0:T(8,128)(2,1)S(1)}, f32[256,896]{1,0:T(8,128)S(1)}) custom-call(s32[1]{0:T(128)} %bitcast.7.xl_ref, bf16[512,2048]{1,0:T(8,128)(2,1)} %bitcast.17, bf16[256,896]{1,0:T(8,128)(2,1)S(1)} %get-tuple-element.59.refs_0_, bf16[256,896]{1,0:T(8,128)(2,1)} %collective-permute-done.refs_1_, ...), custom_call_target="tpu_custom_call" | custom-call | tf_op jit(solution)/shard_map/pallas_call | solution.py:133
  220.3 1.0 copy-done.18
  221.3 1.0 collective-permute-start.16
  222.2 8.0 %collective-permute-done.16.other = bf16[256,896]{1,0:T(8,128)(2,1)S(1)} collective-permute-done((bf16[256,896]{1,0:T(8,128)(2,1)S(1)}, bf16[256,896]{1,0:T(8,128)(2,1)S(1)}, u32[]{:S(2)}, u32[]{:S(2)}) %collective-permute-start.16) | collective-permute-done | bytes 458784 | tf_op jit(solution)/shard_map/ppermute | solution.py:421
  231.0 2.2 shard_map.155.own
  233.2 1.6 collective-permute-start.17
  234.8 5.0 %collective-permute-done.17.other = bf16[256,512]{1,0:T(8,128)(2,1)S(1)} collective-permute-done((bf16[256,512]{1,0:T(8,128)(2,1)}, bf16[256,512]{1,0:T(8,128)(2,1)S(1)}, u32[]{:S(2)}, u32[]{:S(2)}) %collective-permute-start.17) | collective-permute-done | bytes 262176 | tf_op jit(solution)/shard_map/ppermute | solution.py:425
  239.8 0.9 copy-done.10
  240.8 0.9 copy-done.12
  241.7 0.9 copy-done.14
  242.7 0.9 copy-done.16
  243.6 1.3 shard_map.156
  244.9 37.0 %all_to_all.34.got = bf16[64,8,2048]{2,1,0:T(8,128)(2,1)S(1)} all-to-all(bf16[64,8,2048]{2,1,0:T(8,128)(2,1)S(1)} %bitcast.13), channel_id=1, replica_groups=mesh['xh'=2,'y'=4,'xl'=2,'c'=2,'z'=4] {'xh','y','xl','z'}, dimensions={0} | all-to-all | bytes 4194304 | tf_op jit(solution)/shard_map/all_to_all | solution.py:427
  282.0 0.9 shard_map.157
  (72 shorter events, 7.3 us)
Async XLA Ops:
  0.0 1.5 copy-start.1
  1.5 1.2 copy-start.3
  2.7 12.7 %copy-start.28 = (bf16[2,8,2,1024]{3,2,1,0:T(2,128)(2,1)S(1)}, bf16[2,8,2,1024]{3,2,1,0:T(2,128)(2,1)}, u32[]{:S(2)}) copy-start(bf16[2,8,2,1024]{3,2,1,0:T(2,128)(2,1)} %param.26) | copy-start | bytes 196612
  4.2 20.6 %all-to-all-start = ((f32[128,1,128]{2,1,0:T(1,128)}), f32[128,1,128]{2,1,0:T(1,128)S(1)}, u32[]{:S(2)}, u32[]{:S(2)}) async-start(f32[128,1,128]{2,1,0:T(1,128)} %bitcast.3), calls=%async_computation | async-start | bytes 131072 | tf_op jit(solution)/shard_map/all_to_all | solution.py:387
  15.4 10.7 %copy-start.2 = (bf16[2,256,1792]{2,1,0:T(8,128)(2,1)S(1)}, bf16[2,256,1792]{2,1,0:T(8,128)(2,1)}, u32[]{:S(2)}) copy-start(bf16[2,256,1792]{2,1,0:T(8,128)(2,1)} %grad.2) | copy-start | bytes 5505028
  26.1 9.4 %copy-start.29 = (s32[8,8]{1,0:T(8,128)S(1)}, s32[8,8]{1,0:T(8,128)}, u32[]{:S(2)}) copy-start(s32[8,8]{1,0:T(8,128)} %param.28) | copy-start | bytes 772
  26.1 9.5 %copy-start.19 = (bf16[2,8,4096]{2,1,0:T(8,128)(2,1)S(1)}, bf16[2,8,4096]{2,1,0:T(8,128)(2,1)}, u32[]{:S(2)}) copy-start(bf16[2,8,4096]{2,1,0:T(8,128)(2,1)} %q_ref.1) | copy-start | bytes 393220
  26.1 9.5 %copy-start.22 = (s32[8]{0:T(128)S(1)}, s32[8]{0:T(128)}, u32[]{:S(2)}) copy-start(s32[8]{0:T(128)} %lens.1) | copy-start | bytes 100
  34.7 0.8 copy-start.23
  35.6 2.2 copy-start
  37.8 4.7 %copy-start.20 = (f32[4096]{0:T(1024)S(1)}, f32[4096]{0:T(1024)}, u32[]{:S(2)}) copy-start(f32[4096]{0:T(1024)} %param.23) | copy-start | bytes 49156
  37.8 4.7 %copy-start.21 = (bf16[8,4096]{1,0:T(8,128)(2,1)S(1)}, bf16[8,4096]{1,0:T(8,128)(2,1)}, u32[]{:S(2)}) copy-start(bf16[8,4096]{1,0:T(8,128)(2,1)} %rows.1) | copy-start | bytes 196612
  44.1 54.3 %copy-start.4 = (bf16[256,1792]{1,0:T(8,128)(2,1)S(1)}, bf16[256,1792]{1,0:T(8,128)(2,1)}, u32[]{:S(2)}) copy-start(bf16[256,1792]{1,0:T(8,128)(2,1)} %grad.3) | copy-start | bytes 2752516
  44.1 62.2 %all-to-all-start.1 = ((bf16[64,8,2048]{2,1,0:T(8,128)(2,1)}), bf16[64,8,2048]{2,1,0:T(8,128)(2,1)}, u32[]{:S(2)}, u32[]{:S(2)}) async-start(bf16[64,8,2048]{2,1,0:T(8,128)(2,1)} %get-tuple-element.49), calls=%async_computation.1 | async-start | bytes 4194304 | tf_op jit(solution)/shard_map/all_to_all | solution.py:402
  52.6 35.9 %collective-permute-start.1 = (bf16[256,896]{1,0:T(8,128)(2,1)}, bf16[256,896]{1,0:T(8,128)(2,1)S(1)}, u32[]{:S(2)}, u32[]{:S(2)}) collective-permute-start(bf16[256,896]{1,0:T(8,128)(2,1)} %get-tuple-element.51), channel_id=1, source_target_pairs={{0,16},{16,0},{32,48},{48,32},{1,17},{17,1},{33,49},{49,33},{2,18}... | collective-permute-start | bytes 1376264 | tf_op jit(solution)/shard_map/ppermute | solution.py:409
  54.2 43.7 %collective-permute-start.3 = (bf16[256,896]{1,0:T(8,128)(2,1)}, bf16[256,896]{1,0:T(8,128)(2,1)S(1)}, u32[]{:S(2)}, u32[]{:S(2)}) collective-permute-start(bf16[256,896]{1,0:T(8,128)(2,1)} %get-tuple-element.52), channel_id=1, source_target_pairs={{0,32},{16,48},{32,0},{48,16},{1,33},{17,49},{33,1},{49,17},{2,34}... | collective-permute-start | bytes 1376264 | tf_op jit(solution)/shard_map/ppermute | solution.py:409
  56.9 41.0 %collective-permute-start.5 = (bf16[256,896]{1,0:T(8,128)(2,1)}, bf16[256,896]{1,0:T(8,128)(2,1)S(1)}, u32[]{:S(2)}, u32[]{:S(2)}) collective-permute-start(bf16[256,896]{1,0:T(8,128)(2,1)} %copy-done.23), channel_id=1, source_target_pairs={{0,48},{16,32},{32,16},{48,0},{1,49},{17,33},{33,17},{49,1},{2,50}... | collective-permute-start | bytes 1376264 | tf_op jit(solution)/shard_map/ppermute | solution.py:409
  57.4 48.9 %collective-permute-start = (bf16[256,896]{1,0:T(8,128)(2,1)S(1)}, bf16[256,896]{1,0:T(8,128)(2,1)}, u32[]{:S(2)}, u32[]{:S(2)}) collective-permute-start(bf16[256,896]{1,0:T(8,128)(2,1)S(1)} %get-tuple-element.59.refs_0_), channel_id=1, source_target_pairs={{0,4},{4,0},{1,5},{5,1},{2,6},{6,2},{3,7},{7,3},{8,12},{12,8},{9,1... | collective-permute-start | bytes 1376264 | tf_op jit(solution)/shard_map/ppermute | solution.py:412
  88.5 17.8 %collective-permute-start.2 = (bf16[256,896]{1,0:T(8,128)(2,1)S(1)}, bf16[256,896]{1,0:T(8,128)(2,1)}, u32[]{:S(2)}, u32[]{:S(2)}) collective-permute-start(bf16[256,896]{1,0:T(8,128)(2,1)S(1)} %collective-permute-done.1.refs_2_), channel_id=1, source_target_pairs={{0,4},{4,0},{1,5},{5,1},{2,6},{6,2},{3,7},{7,3},{8,12},{12,8},{9,1... | collective-permute-start | bytes 1376264 | tf_op jit(solution)/shard_map/ppermute | solution.py:412
  97.9 8.5 %collective-permute-start.4 = (bf16[256,896]{1,0:T(8,128)(2,1)S(1)}, bf16[256,896]{1,0:T(8,128)(2,1)}, u32[]{:S(2)}, u32[]{:S(2)}) collective-permute-start(bf16[256,896]{1,0:T(8,128)(2,1)S(1)} %collective-permute-done.3.refs_4_), channel_id=1, source_target_pairs={{0,4},{4,0},{1,5},{5,1},{2,6},{6,2},{3,7},{7,3},{8,12},{12,8},{9,1... | collective-permute-start | bytes 1376264 | tf_op jit(solution)/shard_map/ppermute | solution.py:412
  97.9 8.5 %collective-permute-start.6 = (bf16[256,896]{1,0:T(8,128)(2,1)S(1)}, bf16[256,896]{1,0:T(8,128)(2,1)}, u32[]{:S(2)}, u32[]{:S(2)}) collective-permute-start(bf16[256,896]{1,0:T(8,128)(2,1)S(1)} %collective-permute-done.5.refs_6_), channel_id=1, source_target_pairs={{0,4},{4,0},{1,5},{5,1},{2,6},{6,2},{3,7},{7,3},{8,12},{12,8},{9,1... | collective-permute-start | bytes 1376264 | tf_op jit(solution)/shard_map/ppermute | solution.py:412
  98.4 1.5 copy-start.5
  99.9 1.5 copy-start.6
  106.4 10.2 %copy-start.25 = (bf16[256,512]{1,0:T(8,128)(2,1)S(1)}, bf16[256,512]{1,0:T(8,128)(2,1)}, u32[]{:S(2)}) copy-start(bf16[256,512]{1,0:T(8,128)(2,1)} %copy-done.24) | copy-start | bytes 786436
  110.8 1.0 copy-start.17
  111.8 12.4 %collective-permute-start.7 = (bf16[256,896]{1,0:T(8,128)(2,1)S(1)}, bf16[256,896]{1,0:T(8,128)(2,1)S(1)}, u32[]{:S(2)}, u32[]{:S(2)}) collective-permute-start(bf16[256,896]{1,0:T(8,128)(2,1)S(1)} %get-tuple-element.68), channel_id=1, source_target_pairs={{0,8},{8,0},{1,9},{9,1},{2,10},{10,2},{3,11},{11,3},{4,12},{12,4},... | collective-permute-start | bytes 1376264 | tf_op jit(solution)/shard_map/ppermute | solution.py:421
  113.3 13.9 %collective-permute-start.9 = (bf16[256,512]{1,0:T(8,128)(2,1)}, bf16[256,512]{1,0:T(8,128)(2,1)S(1)}, u32[]{:S(2)}, u32[]{:S(2)}) collective-permute-start(bf16[256,512]{1,0:T(8,128)(2,1)} %get-tuple-element.70), channel_id=1, source_target_pairs={{0,16},{16,0},{32,48},{48,32},{1,17},{17,1},{33,49},{49,33},{2,18}... | collective-permute-start | bytes 786440 | tf_op jit(solution)/shard_map/ppermute | solution.py:409
  114.2 14.2 %collective-permute-start.10 = (bf16[256,512]{1,0:T(8,128)(2,1)}, bf16[256,512]{1,0:T(8,128)(2,1)S(1)}, u32[]{:S(2)}, u32[]{:S(2)}) collective-permute-start(bf16[256,512]{1,0:T(8,128)(2,1)} %get-tuple-element.71), channel_id=1, source_target_pairs={{0,32},{16,48},{32,0},{48,16},{1,33},{17,49},{33,1},{49,17},{2,34}... | collective-permute-start | bytes 786440 | tf_op jit(solution)/shard_map/ppermute | solution.py:409
  116.5 14.2 %collective-permute-start.11 = (bf16[256,512]{1,0:T(8,128)(2,1)S(1)}, bf16[256,512]{1,0:T(8,128)(2,1)S(1)}, u32[]{:S(2)}, u32[]{:S(2)}) collective-permute-start(bf16[256,512]{1,0:T(8,128)(2,1)S(1)} %copy-done.25), channel_id=1, source_target_pairs={{0,48},{16,32},{32,16},{48,0},{1,49},{17,33},{33,17},{49,1},{2,50}... | collective-permute-start | bytes 786440 | tf_op jit(solution)/shard_map/ppermute | solution.py:409
  124.2 0.8 copy-start.26
  130.8 1.8 collective-permute-start.12
  130.8 1.9 collective-permute-start.13
  131.3 1.8 collective-permute-start.14
  131.3 2.1 collective-permute-start.15
  131.8 8.4 %collective-permute-start.8 = (bf16[256,512]{1,0:T(8,128)(2,1)}, bf16[256,512]{1,0:T(8,128)(2,1)S(1)}, u32[]{:S(2)}, u32[]{:S(2)}) collective-permute-start(bf16[256,512]{1,0:T(8,128)(2,1)} %shard_map.151.own), channel_id=1, source_target_pairs={{0,8},{8,0},{1,9},{9,1},{2,10},{10,2},{3,11},{11,3},{4,12},{12,4},... | collective-permute-start | bytes 786440 | tf_op jit(solution)/shard_map/ppermute | solution.py:425
  132.6 9.8 %copy-start.7 = (bf16[256,512]{1,0:T(8,128)(2,1)}, bf16[256,512]{1,0:T(8,128)(2,1)S(1)}, u32[]{:S(2)}) copy-start(bf16[256,512]{1,0:T(8,128)(2,1)S(1)} %collective-permute-done.12.refs_1_) | copy-start | bytes 786436
  132.7 9.8 %copy-start.9 = (bf16[256,512]{1,0:T(8,128)(2,1)}, bf16[256,512]{1,0:T(8,128)(2,1)S(1)}, u32[]{:S(2)}) copy-start(bf16[256,512]{1,0:T(8,128)(2,1)S(1)} %collective-permute-done.13.refs_3_) | copy-start | bytes 786436
  133.0 9.4 %copy-start.11 = (bf16[256,512]{1,0:T(8,128)(2,1)}, bf16[256,512]{1,0:T(8,128)(2,1)S(1)}, u32[]{:S(2)}) copy-start(bf16[256,512]{1,0:T(8,128)(2,1)S(1)} %collective-permute-done.14.refs_5_) | copy-start | bytes 786436
  133.4 9.1 %copy-start.13 = (bf16[256,512]{1,0:T(8,128)(2,1)}, bf16[256,512]{1,0:T(8,128)(2,1)S(1)}, u32[]{:S(2)}) copy-start(bf16[256,512]{1,0:T(8,128)(2,1)S(1)} %collective-permute-done.15.refs_7_) | copy-start | bytes 786436
  140.2 1.0 copy-start.15
  215.8 24.0 %copy-start.8 = (bf16[256,512]{1,0:T(8,128)(2,1)S(1)}, bf16[256,512]{1,0:T(8,128)(2,1)}, u32[]{:S(2)}) copy-start(bf16[256,512]{1,0:T(8,128)(2,1)} %copy-done.7) | copy-start | bytes 786436
  220.3 1.0 copy-start.18
  221.3 9.0 %collective-permute-start.16 = (bf16[256,896]{1,0:T(8,128)(2,1)S(1)}, bf16[256,896]{1,0:T(8,128)(2,1)S(1)}, u32[]{:S(2)}, u32[]{:S(2)}) collective-permute-start(bf16[256,896]{1,0:T(8,128)(2,1)S(1)} %get-tuple-element.80), channel_id=1, source_target_pairs={{0,8},{8,0},{1,9},{9,1},{2,10},{10,2},{3,11},{11,3},{4,12},{12,4},... | collective-permute-start | bytes 1376264 | tf_op jit(solution)/shard_map/ppermute | solution.py:421
  233.2 6.6 %collective-permute-start.17 = (bf16[256,512]{1,0:T(8,128)(2,1)}, bf16[256,512]{1,0:T(8,128)(2,1)S(1)}, u32[]{:S(2)}, u32[]{:S(2)}) collective-permute-start(bf16[256,512]{1,0:T(8,128)(2,1)} %shard_map.155.own), channel_id=1, source_target_pairs={{0,8},{8,0},{1,9},{9,1},{2,10},{10,2},{3,11},{11,3},{4,12},{12,4},... | collective-permute-start | bytes 786440 | tf_op jit(solution)/shard_map/ppermute | solution.py:425
  239.8 1.0 copy-start.10
  240.8 0.9 copy-start.12
  241.7 0.9 copy-start.14
  242.7 0.9 copy-start.16
  (2 other events, 1.5 us)

commit v3 on v2

--- a/solution.py
+++ b/solution.py
@@ -16,7 +16,8 @@
 norm_eps = 1e-05
 
 ALL = ("xh", "y", "xl", "c", "z")
-GROUP = ("xh", "y", "xl", "z")
+PLANE = ("xh", "xl", "z")
+GROUP = PLANE + ("y",)
 F32 = jnp.float32
 BF16 = jnp.bfloat16
 
@@ -31,56 +32,87 @@
     return master - m / (v * lax.rsqrt(v) + adam_eps)
 
 
-def squares_body(first, second, out, acc):
-    step = pl.program_id(0)
-
-    @pl.when(step == 0)
-    def _():
-        acc[...] = jnp.zeros(acc.shape, F32)
-
-    total = acc[...]
-    for block in (first[0], first[1], second[...]):
-        for lo in range(0, block.shape[0], 8):
-            x = block[lo : lo + 8].astype(F32)
-            total = total + x * x
-    acc[...] = total
-
-    @pl.when(step == pl.num_programs(0) - 1)
-    def _():
-        out[...] = jnp.full(out.shape, jnp.sum(acc[...]), F32)
+def fetch_all(pairs_of, sems, tile):
+    rows = pairs_of[0][0].shape[-2]
+
+    def copy(i, t):
+        far, near = pairs_of[i]
+        lead = (slice(None),) * (len(far.shape) - 2)
+        at = lead + (pl.ds(pl.multiple_of(t * tile, tile), tile),)
+        return pltpu.make_async_copy(far.at[at], near.at[at], sems.at[i, t])
+
+    for t in range(rows // tile):
+        for i in range(len(pairs_of)):
+            copy(i, t).start()
+    return copy
+
+
+def squares_body(first, second, out, near, near_second, sems):
+    tile = second.shape[0] // sems.shape[1]
+    copy = fetch_all([(first, near), (second, near_second)], sems, tile)
+    total = jnp.zeros((8, second.shape[1]), F32)
+    for t in range(sems.shape[1]):
+        copy(0, t).wait()
+        copy(1, t).wait()
+        for lo in range(t * tile, (t + 1) * tile, 8):
+            for x in (near[0, lo : lo + 8], near[1, lo : lo + 8], near_second[lo : lo + 8]):
+                x = x.astype(F32)
+                total = total + x * x
+    out[...] = jnp.full(out.shape, jnp.sum(total), F32)
 
 
 def sum_of_squares(first, second, tile):
-    rows, cols = second.shape
+    hbm, vmem = (pl.BlockSpec(memory_space=m) for m in (pltpu.HBM, pltpu.VMEM))
     return pl.pallas_call(
         squares_body,
-        grid=(rows // tile,),
-        in_specs=[
-            pl.BlockSpec((2, tile, cols), lambda i: (0, i, 0)),
-            pl.BlockSpec((tile, cols), lambda i: (i, 0)),
+        in_specs=[hbm, hbm],
+        out_specs=vmem,
+        out_shape=jax.ShapeDtypeStruct((128, 128), F32),
+        scratch_shapes=[
+            pltpu.VMEM(first.shape, first.dtype),
+            pltpu.VMEM(second.shape, second.dtype),
+            pltpu.SemaphoreType.DMA((2, second.shape[0] // tile)),
         ],
-        out_specs=pl.BlockSpec((128, 128), lambda i: (0, 0)),
-        out_shape=jax.ShapeDtypeStruct((128, 128), F32),
-        scratch_shapes=[pltpu.VMEM((8, cols), F32)],
-        compiler_params=pltpu.CompilerParams(vmem_limit_bytes=48 << 20),
+        compiler_params=pltpu.CompilerParams(vmem_limit_bytes=60 << 20),
     )(first, second)
 
 
-def gate_up_body(y_ref, clip_ref, master, moment, second, grad, *outs):
+def gate_up_body(y_ref, clip_ref, *refs):
+    far, outs, near, sems = refs[:4], refs[4:8], refs[8:12], refs[12]
     clip = clip_ref[0]
     y = y_ref[0]
-    wide = master.shape[2] // 4
-    new = [
-        adam_new(master[s], moment[s], second[s], grad[s], clip).astype(BF16) for s in range(2)
-    ]
-    for me in range(4):
-
-        @pl.when(y == me)
-        def _():
-            for k, out in enumerate(outs):
-                lo = (me ^ k) * wide
-                out[:, :wide] = new[0][:, lo : lo + wide]
-                out[:, wide:] = new[1][:, lo : lo + wide]
+    wide = far[0].shape[2] // 4
+    tile = far[0].shape[1] // sems.shape[1]
+    copy = fetch_all(list(zip(far, near)), sems, tile)
+
+    @pl.loop(0, sems.shape[1])
+    def _(t):
+        at = pl.ds(pl.multiple_of(t * tile, tile), tile)
+        for i in range(4):
+            copy(i, t).wait()
+        new = [adam_new(*(a[s, at, :] for a in near), clip).astype(BF16) for s in range(2)]
+        for me in range(4):
+
+            @pl.when(y == me)
+            def _():
+                for k, out in enumerate(outs):
+                    lo = (me ^ k) * wide
+                    out[at, :wide] = new[0][:, lo : lo + wide]
+                    out[at, wide:] = new[1][:, lo : lo + wide]
+
+
+def updated_gate_up(y, clip, arrays, tile):
+    _, rows, cols = arrays[0].shape
+    smem, vmem = (pl.BlockSpec(memory_space=m) for m in (pltpu.SMEM, pltpu.VMEM))
+    return pl.pallas_call(
+        gate_up_body,
+        in_specs=[smem, smem] + [pl.BlockSpec(memory_space=pltpu.HBM)] * 4,
+        out_specs=[vmem] * 4,
+        out_shape=[jax.ShapeDtypeStruct((rows, cols // 2), BF16)] * 4,
+        scratch_shapes=[pltpu.VMEM(a.shape, a.dtype) for a in arrays]
+        + [pltpu.SemaphoreType.DMA((4, rows // tile))],
+        compiler_params=pltpu.CompilerParams(vmem_limit_bytes=54 << 20),
+    )(y, clip, *arrays)
 
 
 def down_body(y_ref, clip_ref, master, moment, second, grad, *outs):
@@ -98,48 +130,41 @@
                 out[:, wide:] = jnp.zeros((out.shape[0], out.shape[1] - wide), BF16)
 
 
-def updated(body, y, clip, arrays, width, tile):
-    stack = arrays[0].shape[:-2]
-    rows, cols = arrays[0].shape[-2:]
-    zeros = (0,) * len(stack)
-    spec = pl.BlockSpec(stack + (tile, cols), lambda i: zeros + (i, 0))
+def updated_down(y, clip, arrays, width, tile):
+    rows, cols = arrays[0].shape
+    spec = pl.BlockSpec((tile, cols), lambda i: (i, 0))
     smem = pl.BlockSpec(memory_space=pltpu.SMEM)
     return pl.pallas_call(
-        body,
+        down_body,
         grid=(rows // tile,),
         in_specs=[smem, smem] + [spec] * 4,
         out_specs=[pl.BlockSpec((tile, width), lambda i: (i, 0))] * 4,
         out_shape=[jax.ShapeDtypeStruct((rows, width), BF16)] * 4,
-        compiler_params=pltpu.CompilerParams(vmem_limit_bytes=48 << 20),
+        compiler_params=pltpu.CompilerParams(vmem_limit_bytes=14 << 20),
     )(y, clip, *arrays)
 
 
-def first_body(xl_ref, x, *refs):
-    blocks, (send, keep) = refs[:-2], refs[-2:]
-    half = x.shape[0] // 2
-    xl = xl_ref[0]
-    for out, part in ((send, 1 - xl), (keep, xl)):
-        acc = None
-        for b, w in enumerate(blocks):
-            lhs = x[pl.ds(pl.multiple_of(part * half, half), half), b * BLK : (b + 1) * BLK]
-            dot = jnp.dot(lhs, w[...], preferred_element_type=F32)
-            acc = dot if acc is None else acc + dot
-        out[...] = acc.astype(out.dtype)
-
-
-def first_products(xl, x, blocks):
-    half, width = x.shape[0] // 2, blocks[0].shape[1]
+def first_body(part_ref, x, *refs):
+    blocks, out = refs[:-1], refs[-1]
+    half = out.shape[0]
+    start = pl.multiple_of(part_ref[0] * half, half)
+    acc = None
+    for b, w in enumerate(blocks):
+        lhs = x[pl.ds(start, half), b * BLK : (b + 1) * BLK]
+        dot = jnp.dot(lhs, w[...], preferred_element_type=F32)
+        acc = dot if acc is None else acc + dot
+    out[...] = acc.astype(out.dtype)
+
+
+def first_products(part, x, blocks, dtype):
     vmem = pl.BlockSpec(memory_space=pltpu.VMEM)
     return pl.pallas_call(
         first_body,
         in_specs=[pl.BlockSpec(memory_space=pltpu.SMEM)] + [vmem] * (1 + len(blocks)),
-        out_specs=[vmem, vmem],
-        out_shape=[
-            jax.ShapeDtypeStruct((half, width), BF16),
-            jax.ShapeDtypeStruct((half, width), F32),
-        ],
-        compiler_params=pltpu.CompilerParams(vmem_limit_bytes=48 << 20),
-    )(xl, x, *blocks)
+        out_specs=vmem,
+        out_shape=jax.ShapeDtypeStruct((x.shape[0] // 2, blocks[0].shape[1]), dtype),
+        compiler_params=pltpu.CompilerParams(vmem_limit_bytes=12 << 20),
+    )(part, x, *blocks)
 
 
 def hidden_body(keep, other, out):
@@ -157,6 +182,7 @@
         in_specs=[vmem, vmem],
         out_specs=vmem,
         out_shape=jax.ShapeDtypeStruct((keep.shape[0], width), BF16),
+        compiler_params=pltpu.CompilerParams(vmem_limit_bytes=4 << 20),
     )(keep, other)
 
 
@@ -181,11 +207,22 @@
         in_specs=[pl.BlockSpec(memory_space=pltpu.SMEM)] + [vmem] * (2 + len(blocks)),
         out_specs=vmem,
         out_shape=jax.ShapeDtypeStruct((2 * own.shape[0], BLK * len(blocks)), BF16),
-        compiler_params=pltpu.CompilerParams(vmem_limit_bytes=48 << 20),
+        compiler_params=pltpu.CompilerParams(vmem_limit_bytes=8 << 20),
     )(xl, own, other, *blocks)
 
 
-def attention_body(pages, lens, q_ref, fresh_ref, kv_ref, out_ref, q32, fresh32, q_rows):
+def attention_body(
+    pages, lens, q_ref, fresh_ref, kv_far, out_ref, kv_ref, q32, fresh32, q_rows, sems
+):
+    chunk = kv_far.shape[0] // sems.shape[0]
+    fetches = [
+        pltpu.make_async_copy(
+            kv_far.at[pl.ds(i * chunk, chunk)], kv_ref.at[pl.ds(i * chunk, chunk)], sems.at[i]
+        )
+        for i in range(sems.shape[0])
+    ]
+    for fetch in fetches:
+        fetch.start()
     steps, rows, _ = q_ref.shape
     heads = kv_ref.shape[2] // HD
     group = q_ref.shape[2] // HD // heads
@@ -214,6 +251,8 @@
             parts.append(jnp.broadcast_to(row, (per_head, HD)))
         return jnp.concatenate(parts, axis=0)
 
+    for fetch in fetches:
+        fetch.wait()
     for r in range(rows):
         kv = [kv_ref[pages[r * n_pages + p]] for p in range(n_pages)]
         head_kv = [
@@ -276,20 +315,22 @@
     smem, vmem = (pl.BlockSpec(memory_space=m) for m in (pltpu.SMEM, pltpu.VMEM))
     return pl.pallas_call(
         attention_body,
-        in_specs=[smem, smem, vmem, vmem, vmem],
+        in_specs=[smem, smem, vmem, vmem, pl.BlockSpec(memory_space=pltpu.HBM)],
         out_specs=vmem,
         out_shape=jax.ShapeDtypeStruct((steps, rows, width), F32),
         scratch_shapes=[
+            pltpu.VMEM(pool.shape, pool.dtype),
             pltpu.VMEM((steps, rows, width), F32),
             pltpu.VMEM((steps, rows, 2 * kv_width), F32),
             pltpu.VMEM((steps * rows * width // HD, HD), F32),
+            pltpu.SemaphoreType.DMA((8,)),
         ],
         cost_estimate=pl.CostEstimate(
             flops=16 * steps * width * pool.shape[0] * pool.shape[1],
             transcendentals=steps * width // HD * pool.shape[0] * pool.shape[1],
             bytes_accessed=16 * pool.size,
         ),
-        compiler_params=pltpu.CompilerParams(vmem_limit_bytes=48 << 20),
+        compiler_params=pltpu.CompilerParams(vmem_limit_bytes=60 << 20),
     )(page_table.reshape(-1), cache_len, queries, fresh, pool)
 
 
@@ -307,17 +348,19 @@
                 for ys in range(4):
                     for z in range(4):
                         lo = ((y ^ ys) * 2 + j) * BLK
-                        piece = got[xh * 32 + ys * 8 + xl * 4 + z, :, lo : lo + BLK].astype(F32)
+                        piece = got[xh * 32 + xl * 16 + z * 4 + ys, :, lo : lo + BLK].astype(F32)
                         acc = piece if acc is None else acc + piece
             sums.append(acc)
         total[:, b * BLK : (b + 1) * BLK] = jnp.where(c == 0, sums[cc], sums[1 - cc])
 
 
+def norm(mixed, gain):
+    mixed = mixed.astype(F32)
+    return mixed * lax.rsqrt(jnp.mean(mixed * mixed, axis=-1, keepdims=True) + norm_eps) * gain
+
+
 def normed_out(c, mixed, gain, normed, payload):
-    mixed_f = mixed.astype(F32)
-    normed[...] = (
-        mixed_f * lax.rsqrt(jnp.mean(mixed_f * mixed_f, axis=-1, keepdims=True) + norm_eps) * gain
-    )
+    normed[...] = norm(mixed, gain)
     for y in range(4):
         for xl in range(2):
             for k in range(4):
@@ -328,13 +371,48 @@
                     at = (k * 2 + j) * BLK
                     for xh in range(2):
                         for z in range(4):
-                            payload[xh * 32 + y * 8 + xl * 4 + z, :, at : at + BLK] = piece
-
-
-def open_body(c_ref, rows, attended, gain, mixed, payload, normed):
+                            payload[xh * 32 + xl * 16 + z * 4 + y, :, at : at + BLK] = piece
+
+
+def open_body(rows, attended, gain, mixed, normed):
     new = (rows[...].astype(F32) + attended[0]).astype(BF16)
     mixed[...] = new
-    normed_out(c_ref[0], new, gain[...], normed, payload)
+    normed[...] = norm(new, gain[...]).astype(BF16)
+
+
+def open_rows(rows, attended, gain):
+    vmem = pl.BlockSpec(memory_space=pltpu.VMEM)
+    return pl.pallas_call(
+        open_body,
+        in_specs=[vmem] * 3,
+        out_specs=[vmem] * 2,
+        out_shape=[jax.ShapeDtypeStruct(rows.shape, BF16)] * 2,
+        compiler_params=pltpu.CompilerParams(vmem_limit_bytes=4 << 20),
+    )(rows, attended, gain)
+
+
+def spread_body(y_ref, c_ref, *refs):
+    *rows, payload = refs
+    y, c = y_ref[0], c_ref[0]
+    for k, row in enumerate(rows):
+        for xl in range(2):
+            for b in range(8):
+                lo = ((y ^ (b // 2)) * 4 + xl * 2 + (c ^ (b % 2))) * BLK
+                piece = row[:, pl.ds(pl.multiple_of(lo, BLK), BLK)]
+                for xh in range(2):
+                    for z in range(4):
+                        payload[xh * 8 + xl * 4 + z, y ^ k, :, b * BLK : (b + 1) * BLK] = piece
+
+
+def spread_rows(y, c, rows):
+    vmem, smem = (pl.BlockSpec(memory_space=m) for m in (pltpu.VMEM, pltpu.SMEM))
+    return pl.pallas_call(
+        spread_body,
+        in_specs=[smem, smem] + [vmem] * 4,
+        out_specs=vmem,
+        out_shape=jax.ShapeDtypeStruct((16, 4, rows[0].shape[0], D // 2), BF16),
+        compiler_params=pltpu.CompilerParams(vmem_limit_bytes=8 << 20),
+    )(y, c, *rows)
 
 
 def next_body(c_ref, rows, got, attended, gain, mixed, payload, total, normed):
@@ -361,8 +439,16 @@
         out_specs=[vmem, vmem] if payload else vmem,
         out_shape=shape,
         scratch_shapes=[pltpu.VMEM(rows.shape, F32)] * scratch,
-        compiler_params=pltpu.CompilerParams(vmem_limit_bytes=48 << 20),
+        compiler_params=pltpu.CompilerParams(vmem_limit_bytes=8 << 20),
     )(c, rows, *arrays)
+
+
+def over_y(pieces):
+    return [p if k == 0 else lax.ppermute(p, "y", pairs("y", k)) for k, p in enumerate(pieces)]
+
+
+def over_c(pieces):
+    return [q for p in pieces for q in (p, lax.ppermute(p, "c", pairs("c", 1)))]
 
 
 def shards(
@@ -384,45 +470,37 @@
 ):
     y, xl, c = (lax.axis_index(a).astype(jnp.int32)[None] for a in ("y", "xl", "c"))
     squares = sum_of_squares(gate_up_grad, down_grad, 64)
+    page_table, squares = lax.optimization_barrier((page_table, squares))
     squares = lax.all_to_all(squares, ALL, 0, 0)
+    attended = attention(page_table, cache_len, queries, new_kv, kv_pool)
+    attended, squares = lax.optimization_barrier((attended, squares))
+    mixed, normed = open_rows(start_rows, attended, norm_gain[None])
+    payload = spread_rows(y, c, over_y([normed] * 4))
+    payload, squares = lax.optimization_barrier((payload, squares))
+    handed = lax.all_to_all(payload, PLANE, 0, 0)
     clip = jnp.minimum(1.0, 1.0 / jnp.sqrt(jnp.sum(squares[:, 0])))[None]
     wide = gate_up_master.shape[2] // 4
     pad = -(-wide // 128) * 128
-    gate_up = updated(
-        gate_up_body,
-        y,
-        clip,
-        (gate_up_master, gate_up_moment, gate_up_second, gate_up_grad),
-        2 * wide,
-        32,
+    gate_up = updated_gate_up(
+        y, clip, (gate_up_master, gate_up_moment, gate_up_second, gate_up_grad), 32
     )
-    page_table, *gate_up = lax.optimization_barrier((page_table, *gate_up))
-    attended = attention(page_table, cache_len, queries, new_kv, kv_pool)
-    mixed, payload = row_call(open_body, start_rows, 1, True, c, attended, norm_gain[None])
-    handed = lax.all_to_all(payload, GROUP, 0, 0)
-    clip, payload = lax.optimization_barrier((clip, payload))
-    down_t = updated(
-        down_body, y, clip, (down_master, down_moment, down_second, down_grad), pad, 64
+    clip, *gate_up = lax.optimization_barrier((clip, *gate_up))
+    down_t = updated_down(
+        y, clip, (down_master, down_moment, down_second, down_grad), pad, 64
     )
 
-    def over_y(pieces):
-        return [p if k == 0 else lax.ppermute(p, "y", pairs("y", k)) for k, p in enumerate(pieces)]
-
-    def over_c(pieces):
-        return [q for p in pieces for q in (p, lax.ppermute(p, "c", pairs("c", 1)))]
-
-    gate_up = over_c(over_y(gate_up))
-    gate_up, down_t = lax.optimization_barrier((gate_up, down_t))
-    down_t = over_y(down_t)
+    gate_up = [lax.optimization_barrier((p, down_t))[0] for p in over_y(gate_up)]
+    gate_up, down_t = over_c(gate_up), over_y(down_t)
 
     for step in range(queries.shape[0]):
         whole = handed.reshape(-1, D // 2)
-        send, keep = first_products(xl, whole, gate_up)
+        send = first_products(1 - xl, whole, gate_up, BF16)
         other = lax.ppermute(send, "xl", pairs("xl", 1))
+        keep = first_products(xl, whole, gate_up, F32)
         hidden = hidden_units(keep, other, pad)
+        hidden_other = lax.ppermute(hidden, "xl", pairs("xl", 1))
         if step == 0:
-            down_t = over_c(lax.optimization_barrier((down_t, hidden))[0])
-        hidden_other = lax.ppermute(hidden, "xl", pairs("xl", 1))
+            down_t = over_c(lax.optimization_barrier((down_t, hidden_other))[0])
         partial = second_products(xl, hidden, hidden_other, down_t)
         got = lax.all_to_all(partial.reshape(64, -1, D // 2), GROUP, 0, 0)
         if step == 0:

time: 284 us -> 242 us (0.85)
  waiting for transfers between devices: 72.9 us -> 45.5 us
  local copies, waits for them, and re-layouts: 25.1 us -> 13.6 us
    ppermute x6 -> x9, waiting for transfers between devices: 44 us -> 22.7 us  [over_y(): lax.ppermute(p, 'y', pairs('y', k))]
    unnamed x60 -> x40, local copies, waits for them, and re-layouts: 17.6 us -> 5.18 us
    ppermute x2, waiting for transfers between devices: 11.8 us -> 7.43 us  [shards(): hidden_other = lax.ppermute(hidden, 'xl', pairs('xl', 1))]
    pallas_call x2, Pallas kernels: 4.4 us -> 0.41 us  [hidden_units(): pl.pallas_call(hidden_body, in_specs=[vmem, vmem], out_specs=vmem, out_sh...]
    ppermute x6 -> x9, starting transfers between devices: 9.48 us -> 13 us  [over_y(): lax.ppermute(p, 'y', pairs('y', k))]
    ppermute x8, waiting for transfers between devices: 0.82 us -> 4.38 us  [over_c(): return [q for p in pieces for q in (p, lax.ppermute(p, 'c', pairs('c', 1)))]]
    ppermute x2, waiting for transfers between devices: 14.3 us -> 10.9 us  [shards(): other = lax.ppermute(send, 'xl', pairs('xl', 1))]
    pallas_call x2 -> x4, Pallas kernels: 8.9 us -> 11.4 us  [first_products(): pl.pallas_call(first_body, in_specs=[pl.BlockSpec(memory_space=pltpu.SMEM...]
  transfers between devices with their start and end apart: 20 -> 23, of which waited for: 12 -> 16; matrix products, arithmetic and copies ran while one was open for 3% -> 4% of each run, Pallas kernels for 2% -> 9%
where the time goes in v3:
time: 242 us; the launch traced here: 241 us
  blocking collectives  108 us (45%)
  waiting for transfers between devices  45.5 us (19%)
  starting transfers between devices  36.7 us (15%)
  Pallas kernels  35.3 us (15%)
  local copies, waits for them, and re-layouts  13.6 us (6%)
    all_to_all x2, blocking collectives, shards(): got = lax.all_to_all(partial.reshape(64, -1, D // 2), GROUP, 0, 0)  73.1 us
    all_to_all x1, blocking collectives, shards(): handed = lax.all_to_all(payload, GROUP, 0, 0)  35.1 us
    ppermute x9, waiting for transfers between devices, over_y(): lax.ppermute(p, 'y', pairs('y', k))  22.7 us
    ppermute x9, starting transfers between devices, over_y(): lax.ppermute(p, 'y', pairs('y', k))  13 us
    pallas_call x4, Pallas kernels, first_products(): pl.pallas_call(first_body, in_specs=[pl.BlockSpec(memory_space=pltpu.SMEM...  11.4 us
    all_to_all x1, starting transfers between devices, shards(): squares = lax.all_to_all(squares, ALL, 0, 0)  11.1 us
    ppermute x2, waiting for transfers between devices, shards(): other = lax.ppermute(send, 'xl', pairs('xl', 1))  10.9 us
    pallas_call x1, Pallas kernels, attention(): pl.pallas_call(attention_body, in_specs=[smem, smem, vmem, vmem, pl.Block...  7.96 us
  transfers between devices with their start and end apart: 23, of which 16 were waited for; matrix products, arithmetic and copies ran while one was open for 4% of the time, Pallas kernels for 9%

profile of v3, /device:TPU:0, one launch (start us, length us, event | category | flops | bytes accessed | tf_op | source)
XLA Modules:
  0.0 241.0 jit_solution(11855363602367726623)
XLA Ops:
  0.0 2.7 %shard_map.145 = f32[128,128]{1,0:T(8,128)} custom-call(bf16[2,256,1792]{2,1,0:T(8,128)(2,1)} %refs_3_.1, bf16[256,1792]{1,0:T(8,128)(2,1)} %grad.1), custom_call_target="tpu_custom_call" | custom-call | tf_op jit(solution)/shard_map/pallas_call | solution.py:66
  2.7 11.1 %all-to-all-start = ((f32[128,1,128]{2,1,0:T(1,128)}), f32[128,1,128]{2,1,0:T(1,128)S(1)}, u32[]{:S(2)}, u32[]{:S(2)}) async-start(f32[128,1,128]{2,1,0:T(1,128)} %bitcast.21), calls=%async_computation | async-start | bytes 131072 | tf_op jit(solution)/shard_map/all_to_all | solution.py:474
  13.8 0.7 reshape.24.fresh_ref
  15.1 7.2 %reshape.25.kv_far = bf16[64,32,1024]{2,1,0:T(8,128)(2,1)} reshape(bf16[64,16,2,1024]{3,2,1,0:T(2,128)(2,1)} %param.27) | data formatting | bytes 8388608 | tf_op jit(solution)/shard_map/reshape | solution.py:314
  22.3 8.0 %shard_map.146.attended = f32[2,8,4096]{2,1,0:T(8,128)} custom-call(s32[64]{0:T(128)} %reshape.23.pages, s32[8]{0:T(128)} %lens.1, bf16[2,8,4096]{2,1,0:T(8,128)(2,1)} %q_ref.1, bf16[2,8,2048]{2,1,0:T(8,128)(2,1)} %reshape.24.fresh_ref, bf16[64,32,1024]{2,1,0:T(8,128)(2,1)} %reshape.25.kv_far), custom_call_target="tpu_custom_call" | custom-call | flops 268435456 | bytes 33554432 | tf_op jit(solution)/shard_map/pallas_call | solution.py:316
  30.3 0.9 copy-done.3
  31.4 2.3 collective-permute-start.2
  33.7 0.8 collective-permute-start.1
  34.5 1.1 collective-permute-start
  35.6 1.4 collective-permute-done.2.refs_3_
  36.9 2.8 %collective-permute-done.1.refs_2_ = bf16[8,4096]{1,0:T(8,128)(2,1)S(1)} collective-permute-done((bf16[8,4096]{1,0:T(8,128)(2,1)S(1)}, bf16[8,4096]{1,0:T(8,128)(2,1)S(1)}, u32[]{:S(2)}, u32[]{:S(2)}) %collective-permute-start.1) | collective-permute-done | bytes 65568 | tf_op jit(solution)/shard_map/ppermute | solution.py:447
  39.9 1.3 copy-done
  41.3 7.3 %all-to-all-start.1 = ((bf16[16,4,8,2048]{3,2,1,0:T(8,128)(2,1)}), bf16[16,4,8,2048]{3,2,1,0:T(8,128)(2,1)S(1)}, u32[]{:S(2)}, u32[]{:S(2)}) async-start(bf16[16,4,8,2048]{3,2,1,0:T(8,128)(2,1)} %copy-done), calls=%async_computation.1 | async-start | bytes 4194304 | tf_op jit(solution)/shard_map/all_to_all | solution.py:480
  48.6 0.7 slice_reduce_fusion
  50.1 6.7 %shard_map.149 = (bf16[256,896]{1,0:T(8,128)(2,1)}, bf16[256,896]{1,0:T(8,128)(2,1)}, bf16[256,896]{1,0:T(8,128)(2,1)}, bf16[256,896]{1,0:T(8,128)(2,1)}) custom-call(s32[1]{0:T(128)} %bitcast.6.y_ref, f32[1]{0:T(128)} %bitcast.8.clip_ref, f32[2,256,1792]{2,1,0:T(8,128)} %refs_0_.1, f32[2,256,1792]{2,1,0:T(8,128)} %refs_1_.1, f32[2,256,1792]{2,1,0:T(8,128)} %refs_2_.1, ...), custom_call_target="tpu_custom_call" | custom-call | tf_op jit(solution)/shard_map/pallas_call | solution.py:107
  56.8 1.3 collective-permute-start.8
  58.1 1.2 collective-permute-start.6
  59.4 1.6 collective-permute-start.4
  61.0 1.8 shard_map.150
  62.8 0.7 copy-done.8
  63.5 0.7 copy-done.12
  64.2 0.7 copy-done.14
  65.0 0.7 copy-done.16
  65.7 13.0 %collective-permute-done.8.refs_6_ = bf16[256,896]{1,0:T(8,128)(2,1)S(1)} collective-permute-done((bf16[256,896]{1,0:T(8,128)(2,1)}, bf16[256,896]{1,0:T(8,128)(2,1)S(1)}, u32[]{:S(2)}, u32[]{:S(2)}) %collective-permute-start.8) | collective-permute-done | bytes 458784 | tf_op jit(solution)/shard_map/ppermute | solution.py:447
  78.7 0.7 collective-permute-done.4.refs_2_
  79.9 2.3 collective-permute-done.5.refs_3_
  82.7 2.9 %shard_map.152 = bf16[256,896]{1,0:T(8,128)(2,1)S(1)} custom-call(s32[1]{0:T(128)S(6)} %sub.4.part_ref, bf16[512,2048]{1,0:T(8,128)(2,1)S(1)} %bitcast.13, bf16[256,896]{1,0:T(8,128)(2,1)S(1)} %copy-done.1, bf16[256,896]{1,0:T(8,128)(2,1)} %collective-permute-done.3.refs_1_, bf16[256,896]{1,0:T(8,128)(2,1)} %collective-permute-done.4.refs_2_, ...), custom_call_target="tpu_custom_call" | custom-call | tf_op jit(solution)/shard_map/pallas_call | solution.py:161
  85.6 1.7 collective-permute-start.10
  87.3 0.7 collective-permute-start.12
  88.0 2.6 %collective-permute-start.13 = (bf16[256,512]{1,0:T(8,128)(2,1)S(1)}, bf16[256,512]{1,0:T(8,128)(2,1)S(1)}, u32[]{:S(2)}, u32[]{:S(2)}) collective-permute-start(bf16[256,512]{1,0:T(8,128)(2,1)S(1)} %copy-done.15), channel_id=1, source_target_pairs={{0,32},{16,48},{32,0},{48,16},{1,33},{17,49},{33,1},{49,17},{2,34}... | collective-permute-start | bytes 786440 | tf_op jit(solution)/shard_map/ppermute | solution.py:447
  90.6 1.4 collective-permute-start.14
  92.0 2.8 %shard_map.151.keep = f32[256,896]{1,0:T(8,128)S(1)} custom-call(s32[1]{0:T(128)} %bitcast.5.part_ref.xl_ref, bf16[512,2048]{1,0:T(8,128)(2,1)S(1)} %bitcast.14, bf16[256,896]{1,0:T(8,128)(2,1)S(1)} %copy-done.1, bf16[256,896]{1,0:T(8,128)(2,1)} %collective-permute-done.3.refs_1_, bf16[256,896]{1,0:T(8,128)(2,1)} %collective-permute-done.4.refs_2_, ...), custom_call_target="tpu_custom_call" | custom-call | tf_op jit(solution)/shard_map/pallas_call | solution.py:161
  94.9 3.4 %collective-permute-done.10.other = bf16[256,896]{1,0:T(8,128)(2,1)S(1)} collective-permute-done((bf16[256,896]{1,0:T(8,128)(2,1)S(1)}, bf16[256,896]{1,0:T(8,128)(2,1)S(1)}, u32[]{:S(2)}, u32[]{:S(2)}) %collective-permute-start.10) | collective-permute-done | bytes 458784 | tf_op jit(solution)/shard_map/ppermute | solution.py:498
  98.4 1.7 collective-permute-start.11
  100.2 2.2 collective-permute-done.13.refs_4_
  102.4 2.6 %collective-permute-done.14.refs_6_ = bf16[256,512]{1,0:T(8,128)(2,1)S(1)} collective-permute-done((bf16[256,512]{1,0:T(8,128)(2,1)S(1)}, bf16[256,512]{1,0:T(8,128)(2,1)S(1)}, u32[]{:S(2)}, u32[]{:S(2)}) %collective-permute-start.14) | collective-permute-done | bytes 262176 | tf_op jit(solution)/shard_map/ppermute | solution.py:447
  105.0 1.1 collective-permute-done.11.other
  108.7 1.3 shard_map.154
  110.0 39.5 %all_to_all.32.got = bf16[64,8,2048]{2,1,0:T(8,128)(2,1)S(1)} all-to-all(bf16[64,8,2048]{2,1,0:T(8,128)(2,1)S(1)} %bitcast.18), channel_id=1, replica_groups=mesh['xh'=2,'y'=4,'xl'=2,'c'=2,'z'=4] {'xh','xl','z','y'}, dimensions={0} | all-to-all | bytes 4194304 | tf_op jit(solution)/shard_map/all_to_all | solution.py:505
  149.5 0.6 shard_map.155
  150.1 35.1 %all_to_all.33 = bf16[64,8,2048]{2,1,0:T(8,128)(2,1)S(1)} all-to-all(bf16[64,8,2048]{2,1,0:T(8,128)(2,1)S(1)} %get-tuple-element.66), channel_id=1, replica_groups=mesh['xh'=2,'y'=4,'xl'=2,'c'=2,'z'=4] {'xh','xl','z','y'}, dimensions={0} | all-to-all | bytes 4194304 | tf_op jit(solution)/shard_map/all_to_all | solution.py:508
  185.2 2.8 %shard_map.157 = bf16[256,896]{1,0:T(8,128)(2,1)S(1)} custom-call(s32[1]{0:T(128)S(6)} %sub.4.part_ref, bf16[512,2048]{1,0:T(8,128)(2,1)S(1)} %bitcast.15, bf16[256,896]{1,0:T(8,128)(2,1)S(1)} %copy-done.1, bf16[256,896]{1,0:T(8,128)(2,1)} %collective-permute-done.3.refs_1_, bf16[256,896]{1,0:T(8,128)(2,1)} %collective-permute-done.4.refs_2_, ...), custom_call_target="tpu_custom_call" | custom-call | tf_op jit(solution)/shard_map/pallas_call | solution.py:161
  188.1 2.8 %shard_map.156.keep = f32[256,896]{1,0:T(8,128)S(1)} custom-call(s32[1]{0:T(128)} %bitcast.5.part_ref.xl_ref, bf16[512,2048]{1,0:T(8,128)(2,1)S(1)} %bitcast.16, bf16[256,896]{1,0:T(8,128)(2,1)S(1)} %copy-done.1, bf16[256,896]{1,0:T(8,128)(2,1)} %collective-permute-done.3.refs_1_, bf16[256,896]{1,0:T(8,128)(2,1)} %collective-permute-done.4.refs_2_, ...), custom_call_target="tpu_custom_call" | custom-call | tf_op jit(solution)/shard_map/pallas_call | solution.py:161
  190.9 7.5 %collective-permute-done.19.other = bf16[256,896]{1,0:T(8,128)(2,1)S(1)} collective-permute-done((bf16[256,896]{1,0:T(8,128)(2,1)S(1)}, bf16[256,896]{1,0:T(8,128)(2,1)S(1)}, u32[]{:S(2)}, u32[]{:S(2)}) %collective-permute-start.19) | collective-permute-done | bytes 458784 | tf_op jit(solution)/shard_map/ppermute | solution.py:498
  198.8 6.4 %collective-permute-done.20.other = bf16[256,512]{1,0:T(8,128)(2,1)S(1)} collective-permute-done((bf16[256,512]{1,0:T(8,128)(2,1)S(1)}, bf16[256,512]{1,0:T(8,128)(2,1)S(1)}, u32[]{:S(2)}, u32[]{:S(2)}) %collective-permute-start.20) | collective-permute-done | bytes 262176 | tf_op jit(solution)/shard_map/ppermute | solution.py:501
  205.1 1.3 shard_map.159
  206.4 33.6 %all_to_all.34.got = bf16[64,8,2048]{2,1,0:T(8,128)(2,1)S(1)} all-to-all(bf16[64,8,2048]{2,1,0:T(8,128)(2,1)S(1)} %bitcast.17), channel_id=1, replica_groups=mesh['xh'=2,'y'=4,'xl'=2,'c'=2,'z'=4] {'xh','xl','z','y'}, dimensions={0} | all-to-all | bytes 4194304 | tf_op jit(solution)/shard_map/all_to_all | solution.py:505
  240.0 0.9 shard_map.160
  (61 shorter events, 5.2 us)
Async XLA Ops:
  0.0 14.5 %copy-start.19 = (s32[8,8]{1,0:T(8,128)S(1)}, s32[8,8]{1,0:T(8,128)}, u32[]{:S(2)}) copy-start(s32[8,8]{1,0:T(8,128)} %param.28) | copy-start | bytes 772
  0.0 13.8 %copy-start.18 = (bf16[2,8,2,1024]{3,2,1,0:T(2,128)(2,1)S(1)}, bf16[2,8,2,1024]{3,2,1,0:T(2,128)(2,1)}, u32[]{:S(2)}) copy-start(bf16[2,8,2,1024]{3,2,1,0:T(2,128)(2,1)} %param.26) | copy-start | bytes 196612
  2.7 27.6 %all-to-all-start = ((f32[128,1,128]{2,1,0:T(1,128)}), f32[128,1,128]{2,1,0:T(1,128)S(1)}, u32[]{:S(2)}, u32[]{:S(2)}) async-start(f32[128,1,128]{2,1,0:T(1,128)} %bitcast.21), calls=%async_computation | async-start | bytes 131072 | tf_op jit(solution)/shard_map/all_to_all | solution.py:474
  22.3 8.0 %copy-start.10 = (f32[4096]{0:T(1024)S(1)}, f32[4096]{0:T(1024)}, u32[]{:S(2)}) copy-start(f32[4096]{0:T(1024)} %param.23) | copy-start | bytes 49156
  22.3 8.0 %copy-start.11 = (bf16[8,4096]{1,0:T(8,128)(2,1)S(1)}, bf16[8,4096]{1,0:T(8,128)(2,1)}, u32[]{:S(2)}) copy-start(bf16[8,4096]{1,0:T(8,128)(2,1)} %rows.1) | copy-start | bytes 196612
  30.3 1.0 copy-start.3
  31.4 5.6 %collective-permute-start.2 = (bf16[8,4096]{1,0:T(8,128)(2,1)S(1)}, bf16[8,4096]{1,0:T(8,128)(2,1)S(1)}, u32[]{:S(2)}, u32[]{:S(2)}) collective-permute-start(bf16[8,4096]{1,0:T(8,128)(2,1)S(1)} %get-tuple-element.40.refs_0_), channel_id=1, source_target_pairs={{0,48},{16,32},{32,16},{48,0},{1,49},{17,33},{33,17},{49,1},{2,50}... | collective-permute-start | bytes 196616 | tf_op jit(solution)/shard_map/ppermute | solution.py:447
  33.7 6.1 %collective-permute-start.1 = (bf16[8,4096]{1,0:T(8,128)(2,1)S(1)}, bf16[8,4096]{1,0:T(8,128)(2,1)S(1)}, u32[]{:S(2)}, u32[]{:S(2)}) collective-permute-start(bf16[8,4096]{1,0:T(8,128)(2,1)S(1)} %get-tuple-element.40.refs_0_), channel_id=1, source_target_pairs={{0,32},{16,48},{32,0},{48,16},{1,33},{17,49},{33,1},{49,17},{2,34}... | collective-permute-start | bytes 196616 | tf_op jit(solution)/shard_map/ppermute | solution.py:447
  34.5 5.3 %collective-permute-start = (bf16[8,4096]{1,0:T(8,128)(2,1)S(1)}, bf16[8,4096]{1,0:T(8,128)(2,1)S(1)}, u32[]{:S(2)}, u32[]{:S(2)}) collective-permute-start(bf16[8,4096]{1,0:T(8,128)(2,1)S(1)} %get-tuple-element.40.refs_0_), channel_id=1, source_target_pairs={{0,16},{16,0},{32,48},{48,32},{1,17},{17,1},{33,49},{49,33},{2,18}... | collective-permute-start | bytes 196616 | tf_op jit(solution)/shard_map/ppermute | solution.py:447
  39.9 1.3 copy-start
  41.3 41.4 %all-to-all-start.1 = ((bf16[16,4,8,2048]{3,2,1,0:T(8,128)(2,1)}), bf16[16,4,8,2048]{3,2,1,0:T(8,128)(2,1)S(1)}, u32[]{:S(2)}, u32[]{:S(2)}) async-start(bf16[16,4,8,2048]{3,2,1,0:T(8,128)(2,1)} %copy-done), calls=%async_computation.1 | async-start | bytes 4194304 | tf_op jit(solution)/shard_map/all_to_all | solution.py:480
  50.0 10.9 %copy-start.2 = (bf16[256,1792]{1,0:T(8,128)(2,1)S(1)}, bf16[256,1792]{1,0:T(8,128)(2,1)}, u32[]{:S(2)}) copy-start(bf16[256,1792]{1,0:T(8,128)(2,1)} %grad.1) | copy-start | bytes 2752516
  50.0 10.9 %copy-start.5 = (f32[256,1792]{1,0:T(8,128)S(1)}, f32[256,1792]{1,0:T(8,128)}, u32[]{:S(2)}) copy-start(f32[256,1792]{1,0:T(8,128)} %master.1) | copy-start | bytes 5505028
  50.0 10.9 %copy-start.6 = (f32[256,1792]{1,0:T(8,128)S(1)}, f32[256,1792]{1,0:T(8,128)}, u32[]{:S(2)}) copy-start(f32[256,1792]{1,0:T(8,128)} %moment.1) | copy-start | bytes 5505028
  50.0 10.9 %copy-start.7 = (f32[256,1792]{1,0:T(8,128)S(1)}, f32[256,1792]{1,0:T(8,128)}, u32[]{:S(2)}) copy-start(f32[256,1792]{1,0:T(8,128)} %second.3) | copy-start | bytes 5505028
  56.8 8.9 %copy-start.1 = (bf16[256,896]{1,0:T(8,128)(2,1)S(1)}, bf16[256,896]{1,0:T(8,128)(2,1)}, u32[]{:S(2)}) copy-start(bf16[256,896]{1,0:T(8,128)(2,1)} %get-tuple-element.54.refs_0_) | copy-start | bytes 1376260
  56.8 21.9 %collective-permute-start.8 = (bf16[256,896]{1,0:T(8,128)(2,1)}, bf16[256,896]{1,0:T(8,128)(2,1)S(1)}, u32[]{:S(2)}, u32[]{:S(2)}) collective-permute-start(bf16[256,896]{1,0:T(8,128)(2,1)} %get-tuple-element.59), channel_id=1, source_target_pairs={{0,48},{16,32},{32,16},{48,0},{1,49},{17,33},{33,17},{49,1},{2,50}... | collective-permute-start | bytes 1376264 | tf_op jit(solution)/shard_map/ppermute | solution.py:447
  58.1 20.6 %collective-permute-start.6 = (bf16[256,896]{1,0:T(8,128)(2,1)}, bf16[256,896]{1,0:T(8,128)(2,1)S(1)}, u32[]{:S(2)}, u32[]{:S(2)}) collective-permute-start(bf16[256,896]{1,0:T(8,128)(2,1)} %get-tuple-element.57), channel_id=1, source_target_pairs={{0,32},{16,48},{32,0},{48,16},{1,33},{17,49},{33,1},{49,17},{2,34}... | collective-permute-start | bytes 1376264 | tf_op jit(solution)/shard_map/ppermute | solution.py:447
  59.4 20.0 %collective-permute-start.4 = (bf16[256,896]{1,0:T(8,128)(2,1)}, bf16[256,896]{1,0:T(8,128)(2,1)}, u32[]{:S(2)}, u32[]{:S(2)}) collective-permute-start(bf16[256,896]{1,0:T(8,128)(2,1)} %get-tuple-element.55), channel_id=1, source_target_pairs={{0,16},{16,0},{32,48},{48,32},{1,17},{17,1},{33,49},{49,33},{2,18}... | collective-permute-start | bytes 1376264 | tf_op jit(solution)/shard_map/ppermute | solution.py:447
  62.8 0.7 copy-start.8
  63.5 0.7 copy-start.12
  64.2 0.7 copy-start.14
  65.0 0.7 copy-start.16
  65.7 14.3 %collective-permute-start.3 = (bf16[256,896]{1,0:T(8,128)(2,1)S(1)}, bf16[256,896]{1,0:T(8,128)(2,1)}, u32[]{:S(2)}, u32[]{:S(2)}) collective-permute-start(bf16[256,896]{1,0:T(8,128)(2,1)S(1)} %copy-done.1), channel_id=1, source_target_pairs={{0,4},{4,0},{1,5},{5,1},{2,6},{6,2},{3,7},{7,3},{8,12},{12,8},{9,1... | collective-permute-start | bytes 1376264 | tf_op jit(solution)/shard_map/ppermute | solution.py:451
  79.4 2.8 %collective-permute-start.5 = (bf16[256,896]{1,0:T(8,128)(2,1)}, bf16[256,896]{1,0:T(8,128)(2,1)}, u32[]{:S(2)}, u32[]{:S(2)}) collective-permute-start(bf16[256,896]{1,0:T(8,128)(2,1)} %collective-permute-done.4.refs_2_), channel_id=1, source_target_pairs={{0,4},{4,0},{1,5},{5,1},{2,6},{6,2},{3,7},{7,3},{8,12},{12,8},{9,1... | collective-permute-start | bytes 1376264 | tf_op jit(solution)/shard_map/ppermute | solution.py:451
  79.4 2.8 %collective-permute-start.7 = (bf16[256,896]{1,0:T(8,128)(2,1)S(1)}, bf16[256,896]{1,0:T(8,128)(2,1)}, u32[]{:S(2)}, u32[]{:S(2)}) collective-permute-start(bf16[256,896]{1,0:T(8,128)(2,1)S(1)} %collective-permute-done.6.refs_4_), channel_id=1, source_target_pairs={{0,4},{4,0},{1,5},{5,1},{2,6},{6,2},{3,7},{7,3},{8,12},{12,8},{9,1... | collective-permute-start | bytes 1376264 | tf_op jit(solution)/shard_map/ppermute | solution.py:451
  79.9 2.7 %collective-permute-start.9 = (bf16[256,896]{1,0:T(8,128)(2,1)S(1)}, bf16[256,896]{1,0:T(8,128)(2,1)}, u32[]{:S(2)}, u32[]{:S(2)}) collective-permute-start(bf16[256,896]{1,0:T(8,128)(2,1)S(1)} %collective-permute-done.8.refs_6_), channel_id=1, source_target_pairs={{0,4},{4,0},{1,5},{5,1},{2,6},{6,2},{3,7},{7,3},{8,12},{12,8},{9,1... | collective-permute-start | bytes 1376264 | tf_op jit(solution)/shard_map/ppermute | solution.py:451
  82.7 4.7 %copy-start.17 = (bf16[256,512]{1,0:T(8,128)(2,1)S(1)}, bf16[256,512]{1,0:T(8,128)(2,1)}, u32[]{:S(2)}) copy-start(bf16[256,512]{1,0:T(8,128)(2,1)} %copy-done.16) | copy-start | bytes 786436
  82.7 5.4 %copy-start.15 = (bf16[256,512]{1,0:T(8,128)(2,1)S(1)}, bf16[256,512]{1,0:T(8,128)(2,1)}, u32[]{:S(2)}) copy-start(bf16[256,512]{1,0:T(8,128)(2,1)} %copy-done.14) | copy-start | bytes 786436
  82.7 8.0 %copy-start.13 = (bf16[256,512]{1,0:T(8,128)(2,1)S(1)}, bf16[256,512]{1,0:T(8,128)(2,1)}, u32[]{:S(2)}) copy-start(bf16[256,512]{1,0:T(8,128)(2,1)} %copy-done.12) | copy-start | bytes 786436
  85.6 20.5 %copy-start.9 = (bf16[256,512]{1,0:T(8,128)(2,1)S(1)}, bf16[256,512]{1,0:T(8,128)(2,1)}, u32[]{:S(2)}) copy-start(bf16[256,512]{1,0:T(8,128)(2,1)} %copy-done.8) | copy-start | bytes 786436
  85.6 12.6 %collective-permute-start.10 = (bf16[256,896]{1,0:T(8,128)(2,1)S(1)}, bf16[256,896]{1,0:T(8,128)(2,1)S(1)}, u32[]{:S(2)}, u32[]{:S(2)}) collective-permute-start(bf16[256,896]{1,0:T(8,128)(2,1)S(1)} %shard_map.152), channel_id=1, source_target_pairs={{0,8},{8,0},{1,9},{9,1},{2,10},{10,2},{3,11},{11,3},{4,12},{12,4},... | collective-permute-start | bytes 1376264 | tf_op jit(solution)/shard_map/ppermute | solution.py:498
  87.3 12.9 %collective-permute-start.12 = (bf16[256,512]{1,0:T(8,128)(2,1)S(1)}, bf16[256,512]{1,0:T(8,128)(2,1)S(1)}, u32[]{:S(2)}, u32[]{:S(2)}) collective-permute-start(bf16[256,512]{1,0:T(8,128)(2,1)S(1)} %copy-done.17), channel_id=1, source_target_pairs={{0,16},{16,0},{32,48},{48,32},{1,17},{17,1},{33,49},{49,33},{2,18}... | collective-permute-start | bytes 786440 | tf_op jit(solution)/shard_map/ppermute | solution.py:447
  88.0 14.4 %collective-permute-start.13 = (bf16[256,512]{1,0:T(8,128)(2,1)S(1)}, bf16[256,512]{1,0:T(8,128)(2,1)S(1)}, u32[]{:S(2)}, u32[]{:S(2)}) collective-permute-start(bf16[256,512]{1,0:T(8,128)(2,1)S(1)} %copy-done.15), channel_id=1, source_target_pairs={{0,32},{16,48},{32,0},{48,16},{1,33},{17,49},{33,1},{49,17},{2,34}... | collective-permute-start | bytes 786440 | tf_op jit(solution)/shard_map/ppermute | solution.py:447
  90.6 14.3 %collective-permute-start.14 = (bf16[256,512]{1,0:T(8,128)(2,1)S(1)}, bf16[256,512]{1,0:T(8,128)(2,1)S(1)}, u32[]{:S(2)}, u32[]{:S(2)}) collective-permute-start(bf16[256,512]{1,0:T(8,128)(2,1)S(1)} %copy-done.13), channel_id=1, source_target_pairs={{0,48},{16,32},{32,16},{48,0},{1,49},{17,33},{33,17},{49,1},{2,50}... | collective-permute-start | bytes 786440 | tf_op jit(solution)/shard_map/ppermute | solution.py:447
  98.4 7.6 %collective-permute-start.11 = (bf16[256,512]{1,0:T(8,128)(2,1)S(1)}, bf16[256,512]{1,0:T(8,128)(2,1)S(1)}, u32[]{:S(2)}, u32[]{:S(2)}) collective-permute-start(bf16[256,512]{1,0:T(8,128)(2,1)S(1)} %shard_map.153.own), channel_id=1, source_target_pairs={{0,8},{8,0},{1,9},{9,1},{2,10},{10,2},{3,11},{11,3},{4,12},{12,4},... | collective-permute-start | bytes 786440 | tf_op jit(solution)/shard_map/ppermute | solution.py:501
  106.0 1.5 collective-permute-start.15
  106.0 1.9 collective-permute-start.16
  106.6 1.8 collective-permute-start.17
  106.6 2.1 collective-permute-start.18
  110.0 39.5 %copy-start.4 = (f32[2,8,4096]{2,1,0:T(8,128)S(1)}, f32[2,8,4096]{2,1,0:T(8,128)}, u32[]{:S(2)}) copy-start(f32[2,8,4096]{2,1,0:T(8,128)} %shard_map.146.attended) | copy-start | bytes 786436
  188.0 10.5 %collective-permute-start.19 = (bf16[256,896]{1,0:T(8,128)(2,1)S(1)}, bf16[256,896]{1,0:T(8,128)(2,1)S(1)}, u32[]{:S(2)}, u32[]{:S(2)}) collective-permute-start(bf16[256,896]{1,0:T(8,128)(2,1)S(1)} %shard_map.157), channel_id=1, source_target_pairs={{0,8},{8,0},{1,9},{9,1},{2,10},{10,2},{3,11},{11,3},{4,12},{12,4},... | collective-permute-start | bytes 1376264 | tf_op jit(solution)/shard_map/ppermute | solution.py:498
  198.7 6.5 %collective-permute-start.20 = (bf16[256,512]{1,0:T(8,128)(2,1)S(1)}, bf16[256,512]{1,0:T(8,128)(2,1)S(1)}, u32[]{:S(2)}, u32[]{:S(2)}) collective-permute-start(bf16[256,512]{1,0:T(8,128)(2,1)S(1)} %shard_map.158.own), channel_id=1, source_target_pairs={{0,8},{8,0},{1,9},{9,1},{2,10},{10,2},{3,11},{11,3},{4,12},{12,4},... | collective-permute-start | bytes 786440 | tf_op jit(solution)/shard_map/ppermute | solution.py:501

commit v4 on v3

--- a/solution.py
+++ b/solution.py
@@ -212,28 +212,45 @@
 
 
 def attention_body(
-    pages, lens, q_ref, fresh_ref, kv_far, out_ref, kv_ref, q32, fresh32, q_rows, sems
+    pages,
+    lens,
+    rows_ref,
+    gain_ref,
+    q_ref,
+    fresh_ref,
+    kv_far,
+    mixed_ref,
+    normed_ref,
+    next_ref,
+    kv_ref,
+    q32,
+    fresh32,
+    q_rows,
+    opening,
+    sems,
 ):
-    chunk = kv_far.shape[0] // sems.shape[0]
-    fetches = [
-        pltpu.make_async_copy(
-            kv_far.at[pl.ds(i * chunk, chunk)], kv_ref.at[pl.ds(i * chunk, chunk)], sems.at[i]
-        )
-        for i in range(sems.shape[0])
-    ]
-    for fetch in fetches:
-        fetch.start()
-    steps, rows, _ = q_ref.shape
-    heads = kv_ref.shape[2] // HD
-    group = q_ref.shape[2] // HD // heads
-    n_pages = kv_ref.shape[0] // rows
+    n_pages = pages.shape[1]
+
+    def fetch(r, p):
+        return pltpu.make_async_copy(kv_far.at[pages[r, p]], kv_ref.at[r, p], sems.at[r, p])
+
+    for r in range(pages.shape[0]):
+        for p in range(n_pages):
+            fetch(r, p).start()
+    steps, rows, width = q_ref.shape
+    pairs_of = kv_ref.shape[3]
+    heads = pairs_of // 2
+    group = width // HD // heads
     per_head = steps * group
     count = heads * per_head
     scale = HD**-0.5
     q32[...] = q_ref[...].astype(F32)
     fresh32[...] = fresh_ref[...].astype(F32)
-    ctx = n_pages * kv_ref.shape[1]
+    ctx = n_pages * kv_ref.shape[2] * pairs_of
     lane = lax.broadcasted_iota(jnp.int32, (count, ctx), 1)
+    head_of = lax.broadcasted_iota(jnp.int32, (count, ctx), 0) // per_head
+    own_key = lane % pairs_of == 2 * head_of
+    place = jnp.where(own_key, lane // pairs_of, ctx)
     step_of = lax.broadcasted_iota(jnp.int32, (count, 1), 0) % per_head // group
     for r in range(rows):
         for j in range(heads):
@@ -243,38 +260,22 @@
                     lo = (j * group + g) * HD
                     q_rows[at : at + 1, :] = q32[s, r : r + 1, lo : lo + HD]
 
-    def spread(t, r, first):
+    def spread(t, r, which):
         parts = []
         for j in range(heads):
-            lo = (first + j) * HD
-            row = fresh32[t, r : r + 1, lo : lo + HD]
-            parts.append(jnp.broadcast_to(row, (per_head, HD)))
+            at = 2 * j + which
+            parts.append(jnp.broadcast_to(fresh32[t, r, at : at + 1, :], (per_head, HD)))
         return jnp.concatenate(parts, axis=0)
 
-    for fetch in fetches:
-        fetch.wait()
     for r in range(rows):
-        kv = [kv_ref[pages[r * n_pages + p]] for p in range(n_pages)]
-        head_kv = [
-            jnp.concatenate([page[:, j * HD : (j + 1) * HD] for page in kv], axis=0)
-            for j in range(heads)
-        ]
+        for p in range(n_pages):
+            fetch(r, p).wait()
+        kv = kv_ref[r].reshape(ctx, HD)
         q = q_rows[r * count : (r + 1) * count, :]
-        q_low = q.astype(BF16)
-        old = jnp.concatenate(
-            [
-                lax.dot_general(
-                    q_low[j * per_head : (j + 1) * per_head],
-                    head_kv[j],
-                    (((1,), (1,)), ((), ())),
-                    preferred_element_type=F32,
-                )
-                for j in range(heads)
-            ],
-            axis=0,
+        old = lax.dot_general(
+            q.astype(BF16), kv, (((1,), (1,)), ((), ())), preferred_element_type=F32
         )
-        usable = (lane % 2 == 0) & (lane // 2 < lens[r])
-        old = jnp.where(usable, old * scale, -1e30)
+        old = jnp.where(place < lens[r], old * scale, -1e30)
         top = jnp.max(old, axis=-1, keepdims=True)
         new = []
         for t in range(steps):
@@ -285,53 +286,60 @@
         old = jnp.exp(old - top)
         new = [jnp.exp(n - top) for n in new]
         total = jnp.sum(old, axis=-1, keepdims=True) + sum(new)
-        weights = pltpu.roll(old / total, 1, axis=1).astype(BF16)
-        out = jnp.concatenate(
-            [
-                jnp.dot(
-                    weights[j * per_head : (j + 1) * per_head],
-                    head_kv[j],
-                    preferred_element_type=F32,
-                )
-                for j in range(heads)
-            ],
-            axis=0,
+        weights = old / total
+        weights = jnp.concatenate(
+            [pltpu.roll(weights[:, lo : lo + 128], 1, axis=1) for lo in range(0, ctx, 128)], axis=1
         )
+        out = jnp.dot(weights.astype(BF16), kv, preferred_element_type=F32)
         for t in range(steps):
-            out = out + (new[t] / total).astype(BF16).astype(F32) * spread(t, r, heads)
+            out = out + (new[t] / total).astype(BF16).astype(F32) * spread(t, r, 1)
         for j in range(heads):
             for s in range(steps):
                 for g in range(group):
                     lo = (j * group + g) * HD
                     at = j * per_head + s * group + g
-                    out_ref[s, r : r + 1, lo : lo + HD] = out[at : at + 1, :]
-
-
-def attention(page_table, cache_len, queries, new_kv, kv_pool):
+                    target = opening if s == 0 else next_ref.at[s - 1]
+                    target[r : r + 1, lo : lo + HD] = out[at : at + 1, :]
+    mixed = (rows_ref[...].astype(F32) + opening[...]).astype(BF16)
+    mixed_ref[...] = mixed
+    normed_ref[...] = norm(mixed, gain_ref[...]).astype(BF16)
+
+
+def attention(page_table, cache_len, start_rows, gain, queries, new_kv, kv_pool):
     steps, rows, width = queries.shape
     kv_width = new_kv.shape[-1]
-    fresh = new_kv.reshape(steps, rows, 2 * kv_width)
-    pool = kv_pool.reshape(kv_pool.shape[0], -1, kv_width)
+    heads = kv_width // HD
+
+    def by_head(kv):
+        kv = kv.reshape(*kv.shape[:-1], heads, HD).swapaxes(-3, -2)
+        return kv.reshape(*kv.shape[:-3], 2 * heads, HD)
+
+    fresh, pool = by_head(new_kv), by_head(kv_pool)
     smem, vmem = (pl.BlockSpec(memory_space=m) for m in (pltpu.SMEM, pltpu.VMEM))
     return pl.pallas_call(
         attention_body,
-        in_specs=[smem, smem, vmem, vmem, pl.BlockSpec(memory_space=pltpu.HBM)],
-        out_specs=vmem,
-        out_shape=jax.ShapeDtypeStruct((steps, rows, width), F32),
+        in_specs=[smem, smem] + [vmem] * 4 + [pl.BlockSpec(memory_space=pltpu.HBM)],
+        out_specs=[vmem] * 3,
+        out_shape=[
+            jax.ShapeDtypeStruct((rows, width), BF16),
+            jax.ShapeDtypeStruct((rows, width), BF16),
+            jax.ShapeDtypeStruct((steps - 1, rows, width), F32),
+        ],
         scratch_shapes=[
-            pltpu.VMEM(pool.shape, pool.dtype),
+            pltpu.VMEM(page_table.shape + pool.shape[1:], pool.dtype),
             pltpu.VMEM((steps, rows, width), F32),
-            pltpu.VMEM((steps, rows, 2 * kv_width), F32),
+            pltpu.VMEM((steps, rows, 2 * heads, HD), F32),
             pltpu.VMEM((steps * rows * width // HD, HD), F32),
-            pltpu.SemaphoreType.DMA((8,)),
+            pltpu.VMEM((rows, width), F32),
+            pltpu.SemaphoreType.DMA(page_table.shape),
         ],
         cost_estimate=pl.CostEstimate(
-            flops=16 * steps * width * pool.shape[0] * pool.shape[1],
-            transcendentals=steps * width // HD * pool.shape[0] * pool.shape[1],
+            flops=16 * steps * width * pool.shape[0] * pool.shape[1] * pool.shape[2],
+            transcendentals=steps * width // HD * pool.size // HD,
             bytes_accessed=16 * pool.size,
         ),
-        compiler_params=pltpu.CompilerParams(vmem_limit_bytes=60 << 20),
-    )(page_table.reshape(-1), cache_len, queries, fresh, pool)
+        compiler_params=pltpu.CompilerParams(vmem_limit_bytes=57 << 20),
+    )(page_table, cache_len, start_rows, gain, queries, fresh, pool)
 
 
 def pairs(axis, k):
@@ -374,23 +382,6 @@
                             payload[xh * 32 + xl * 16 + z * 4 + y, :, at : at + BLK] = piece
 
 
-def open_body(rows, attended, gain, mixed, normed):
-    new = (rows[...].astype(F32) + attended[0]).astype(BF16)
-    mixed[...] = new
-    normed[...] = norm(new, gain[...]).astype(BF16)
-
-
-def open_rows(rows, attended, gain):
-    vmem = pl.BlockSpec(memory_space=pltpu.VMEM)
-    return pl.pallas_call(
-        open_body,
-        in_specs=[vmem] * 3,
-        out_specs=[vmem] * 2,
-        out_shape=[jax.ShapeDtypeStruct(rows.shape, BF16)] * 2,
-        compiler_params=pltpu.CompilerParams(vmem_limit_bytes=4 << 20),
-    )(rows, attended, gain)
-
-
 def spread_body(y_ref, c_ref, *refs):
     *rows, payload = refs
     y, c = y_ref[0], c_ref[0]
@@ -418,7 +409,7 @@
 def next_body(c_ref, rows, got, attended, gain, mixed, payload, total, normed):
     add_partials(c_ref[0], got, total)
     done = (rows[...].astype(F32) + total[...]).astype(BF16)
-    new = (done.astype(F32) + attended[1]).astype(BF16)
+    new = (done.astype(F32) + attended[0]).astype(BF16)
     mixed[...] = new
     normed_out(c_ref[0], new, gain[...], normed, payload)
 
@@ -472,19 +463,21 @@
     squares = sum_of_squares(gate_up_grad, down_grad, 64)
     page_table, squares = lax.optimization_barrier((page_table, squares))
     squares = lax.all_to_all(squares, ALL, 0, 0)
-    attended = attention(page_table, cache_len, queries, new_kv, kv_pool)
-    attended, squares = lax.optimization_barrier((attended, squares))
-    mixed, normed = open_rows(start_rows, attended, norm_gain[None])
-    payload = spread_rows(y, c, over_y([normed] * 4))
-    payload, squares = lax.optimization_barrier((payload, squares))
-    handed = lax.all_to_all(payload, PLANE, 0, 0)
+    mixed, normed, attended = attention(
+        page_table, cache_len, start_rows, norm_gain[None], queries, new_kv, kv_pool
+    )
+    opened = over_y([normed] * 4)
     clip = jnp.minimum(1.0, 1.0 / jnp.sqrt(jnp.sum(squares[:, 0])))[None]
+    clip, normed = lax.optimization_barrier((clip, normed))
     wide = gate_up_master.shape[2] // 4
     pad = -(-wide // 128) * 128
     gate_up = updated_gate_up(
         y, clip, (gate_up_master, gate_up_moment, gate_up_second, gate_up_grad), 32
     )
-    clip, *gate_up = lax.optimization_barrier((clip, *gate_up))
+    opened, gate_up = lax.optimization_barrier((opened, gate_up))
+    payload = spread_rows(y, c, opened)
+    handed = lax.all_to_all(payload, PLANE, 0, 0)
+    clip, payload = lax.optimization_barrier((clip, payload))
     down_t = updated_down(
         y, clip, (down_master, down_moment, down_second, down_grad), pad, 64
     )

time: 242 us -> 230 us (0.950)
  waiting for transfers between devices: 45.5 us -> 37.9 us
  local copies, waits for them, and re-layouts: 13.6 us -> 9.88 us
    reshape x3 -> x0, local copies, waits for them, and re-layouts: 8.44 us -> none  [the longest x1 7.2 us: attention(): pool = kv_pool.reshape(kv_pool.shape[0], -1, kv_width)]
    ppermute x9, waiting for transfers between devices: 22.7 us -> 14.8 us  [over_y(): lax.ppermute(p, 'y', pairs('y', k))]
    unnamed x40 -> x36, local copies, waits for them, and re-layouts: 5.18 us -> 9.88 us
    all_to_all x1, waiting for transfers between devices: 0.01 us -> 2.54 us  [shards(): handed = lax.all_to_all(payload, PLANE, 0, 0)]
    pallas_call x2 -> x1, Pallas kernels: 8.1 us -> 9.95 us  [attention(): pl.pallas_call(attention_body, in_specs=[smem, smem] + [vmem] * 4 + [pl.B...]
  transfers between devices with their start and end apart: 23 -> 23, of which waited for: 16 -> 14; matrix products, arithmetic and copies ran while one was open for 4% -> 0% of each run, Pallas kernels for 9% -> 11%
where the time goes in v4:
time: 230 us
  blocking collectives  109 us (47%)
  waiting for transfers between devices  37.9 us (16%)
  Pallas kernels  37 us (16%)
  starting transfers between devices  34.6 us (15%)
  local copies, waits for them, and re-layouts  9.88 us (4%)
    all_to_all x2, blocking collectives, shards(): got = lax.all_to_all(partial.reshape(64, -1, D // 2), GROUP, 0, 0)  73.8 us
    all_to_all x1, blocking collectives, shards(): handed = lax.all_to_all(payload, GROUP, 0, 0)  35 us
    ppermute x9, waiting for transfers between devices, over_y(): lax.ppermute(p, 'y', pairs('y', k))  14.8 us
    ppermute x9, starting transfers between devices, over_y(): lax.ppermute(p, 'y', pairs('y', k))  13.3 us
    pallas_call x4, Pallas kernels, first_products(): pl.pallas_call(first_body, in_specs=[pl.BlockSpec(memory_space=pltpu.SMEM...  11.4 us
    all_to_all x1, starting transfers between devices, shards(): squares = lax.all_to_all(squares, ALL, 0, 0)  11.1 us
    pallas_call x1, Pallas kernels, attention(): pl.pallas_call(attention_body, in_specs=[smem, smem] + [vmem] * 4 + [pl.B...  9.95 us
    unnamed x36, local copies, waits for them, and re-layouts  9.88 us
  transfers between devices with their start and end apart: 23, of which 14 were waited for; matrix products, arithmetic and copies ran while one was open for 0% of the time, Pallas kernels for 11%

profile of v4, /device:TPU:0, one launch (start us, length us, event | category | flops | bytes accessed | tf_op | source)
XLA Modules:
  0.0 229.8 jit_solution(21738091493375587)
XLA Ops:
  0.0 2.6 %shard_map.145 = f32[128,128]{1,0:T(8,128)} custom-call(bf16[2,256,1792]{2,1,0:T(8,128)(2,1)} %refs_3_.1, bf16[256,1792]{1,0:T(8,128)(2,1)} %grad.1), custom_call_target="tpu_custom_call" | custom-call | tf_op jit(solution)/shard_map/pallas_call | solution.py:66
  2.6 11.1 %all-to-all-start = ((f32[128,1,128]{2,1,0:T(1,128)}), f32[128,1,128]{2,1,0:T(1,128)S(1)}, u32[]{:S(2)}, u32[]{:S(2)}) async-start(f32[128,1,128]{2,1,0:T(1,128)} %bitcast.31), calls=%async_computation | async-start | bytes 131072 | tf_op jit(solution)/shard_map/all_to_all | solution.py:465
  13.8 9.9 %shard_map.146 = (bf16[8,4096]{1,0:T(8,128)(2,1)}, bf16[8,4096]{1,0:T(8,128)(2,1)}, f32[1,8,4096]{2,1,0:T(8,128)}) custom-call(s32[8,8]{1,0:T(8,128)} %pages, s32[8]{0:T(128)} %lens.1, bf16[8,4096]{1,0:T(8,128)(2,1)} %rows_ref.1, f32[1,4096]{1,0:T(1,128)} %bitcast.29, bf16[2,8,4096]{2,1,0:T(8,128)(2,1)} %q_ref.1, bf16[2,8,16,128]{3,2,1,0:T(8,128)(2,1)} %bitcast.34, ...), custom_call_target="tpu_custom_call" | custom-call | flops 2147483648 | bytes 33554432 | tf_op jit(solution)/shard_map/pallas_call | solution.py:319
  23.8 2.3 collective-permute-start.2
  26.0 0.8 collective-permute-start.1
  26.9 1.1 collective-permute-start
  27.9 0.7 slice_reduce_fusion
  29.3 6.6 %shard_map.147 = (bf16[256,896]{1,0:T(8,128)(2,1)}, bf16[256,896]{1,0:T(8,128)(2,1)}, bf16[256,896]{1,0:T(8,128)(2,1)}, bf16[256,896]{1,0:T(8,128)(2,1)}) custom-call(s32[1]{0:T(128)} %bitcast.9.y_ref, f32[1]{0:T(128)} %bitcast.13.clip_ref, f32[2,256,1792]{2,1,0:T(8,128)} %refs_0_.1, f32[2,256,1792]{2,1,0:T(8,128)} %refs_1_.1, f32[2,256,1792]{2,1,0:T(8,128)} %refs_2_.1, ...), custom_call_target="tpu_custom_call" | custom-call | tf_op jit(solution)/shard_map/pallas_call | solution.py:107
  36.1 1.3 copy-done
  37.4 6.7 %all-to-all-start.1 = ((bf16[16,4,8,2048]{3,2,1,0:T(8,128)(2,1)}), bf16[16,4,8,2048]{3,2,1,0:T(8,128)(2,1)S(1)}, u32[]{:S(2)}, u32[]{:S(2)}) async-start(bf16[16,4,8,2048]{3,2,1,0:T(8,128)(2,1)} %copy-done), calls=%async_computation.1 | async-start | bytes 4194304 | tf_op jit(solution)/shard_map/all_to_all | solution.py:479
  44.1 2.9 %collective-permute-start.8 = (bf16[256,896]{1,0:T(8,128)(2,1)}, bf16[256,896]{1,0:T(8,128)(2,1)S(1)}, u32[]{:S(2)}, u32[]{:S(2)}) collective-permute-start(bf16[256,896]{1,0:T(8,128)(2,1)} %get-tuple-element.62), channel_id=1, source_target_pairs={{0,48},{16,32},{32,16},{48,0},{1,49},{17,33},{33,17},{49,1},{2,50}... | collective-permute-start | bytes 1376264 | tf_op jit(solution)/shard_map/ppermute | solution.py:438
  47.1 0.7 collective-permute-start.6
  47.8 0.5 collective-permute-start.4
  48.3 1.2 copy-done.2
  49.5 1.5 copy-done.3
  51.0 1.5 copy-done.4
  52.5 1.5 copy-done.5
  54.0 1.8 shard_map.149
  55.8 0.7 copy-done.6
  56.5 0.7 copy-done.12
  57.2 0.7 copy-done.14
  57.9 0.7 copy-done.16
  58.6 8.3 %collective-permute-done.8.refs_6_ = bf16[256,896]{1,0:T(8,128)(2,1)S(1)} collective-permute-done((bf16[256,896]{1,0:T(8,128)(2,1)}, bf16[256,896]{1,0:T(8,128)(2,1)S(1)}, u32[]{:S(2)}, u32[]{:S(2)}) %collective-permute-start.8) | collective-permute-done | bytes 458784 | tf_op jit(solution)/shard_map/ppermute | solution.py:438
  66.9 0.7 collective-permute-done.4.refs_2_
  67.6 0.5 collective-permute-start.7
  68.2 2.3 collective-permute-done.5.refs_3_
  70.9 2.5 %all-to-all-done.1 = bf16[16,4,8,2048]{3,2,1,0:T(8,128)(2,1)S(1)} async-done(((bf16[16,4,8,2048]{3,2,1,0:T(8,128)(2,1)}), bf16[16,4,8,2048]{3,2,1,0:T(8,128)(2,1)S(1)}, u32[]{:S(2)}, u32[]{:S(2)}) %all-to-all-start.1) | async-done | bytes 2097184 | tf_op jit(solution)/shard_map/all_to_all | solution.py:479
  73.5 2.9 %shard_map.151 = bf16[256,896]{1,0:T(8,128)(2,1)S(1)} custom-call(s32[1]{0:T(128)S(6)} %sub.4.part_ref, bf16[512,2048]{1,0:T(8,128)(2,1)S(1)} %bitcast.23, bf16[256,896]{1,0:T(8,128)(2,1)S(1)} %copy-done.1, bf16[256,896]{1,0:T(8,128)(2,1)} %collective-permute-done.3.refs_1_, bf16[256,896]{1,0:T(8,128)(2,1)} %collective-permute-done.4.refs_2_, ...), custom_call_target="tpu_custom_call" | custom-call | tf_op jit(solution)/shard_map/pallas_call | solution.py:161
  76.5 1.8 collective-permute-start.12
  78.2 2.8 %collective-permute-start.13 = (bf16[256,512]{1,0:T(8,128)(2,1)S(1)}, bf16[256,512]{1,0:T(8,128)(2,1)S(1)}, u32[]{:S(2)}, u32[]{:S(2)}) collective-permute-start(bf16[256,512]{1,0:T(8,128)(2,1)S(1)} %copy-done.15), channel_id=1, source_target_pairs={{0,32},{16,48},{32,0},{48,16},{1,33},{17,49},{33,1},{49,17},{2,34}... | collective-permute-start | bytes 786440 | tf_op jit(solution)/shard_map/ppermute | solution.py:438
  81.4 2.8 %shard_map.150.keep = f32[256,896]{1,0:T(8,128)S(1)} custom-call(s32[1]{0:T(128)} %bitcast.8.part_ref.xl_ref, bf16[512,2048]{1,0:T(8,128)(2,1)S(1)} %bitcast.24, bf16[256,896]{1,0:T(8,128)(2,1)S(1)} %copy-done.1, bf16[256,896]{1,0:T(8,128)(2,1)} %collective-permute-done.3.refs_1_, bf16[256,896]{1,0:T(8,128)(2,1)} %collective-permute-done.4.refs_2_, ...), custom_call_target="tpu_custom_call" | custom-call | tf_op jit(solution)/shard_map/pallas_call | solution.py:161
  84.3 2.2 collective-permute-done.10.other
  86.7 1.7 collective-permute-start.11
  88.4 3.2 %collective-permute-done.13.refs_4_ = bf16[256,512]{1,0:T(8,128)(2,1)S(1)} collective-permute-done((bf16[256,512]{1,0:T(8,128)(2,1)S(1)}, bf16[256,512]{1,0:T(8,128)(2,1)S(1)}, u32[]{:S(2)}, u32[]{:S(2)}) %collective-permute-start.13) | collective-permute-done | bytes 262176 | tf_op jit(solution)/shard_map/ppermute | solution.py:438
  91.6 2.6 %collective-permute-done.14.refs_6_ = bf16[256,512]{1,0:T(8,128)(2,1)S(1)} collective-permute-done((bf16[256,512]{1,0:T(8,128)(2,1)S(1)}, bf16[256,512]{1,0:T(8,128)(2,1)S(1)}, u32[]{:S(2)}, u32[]{:S(2)}) %collective-permute-start.14) | collective-permute-done | bytes 262176 | tf_op jit(solution)/shard_map/ppermute | solution.py:438
  94.2 0.5 collective-permute-start.16
  95.3 0.5 collective-permute-done.15.refs_1_
  96.9 1.3 shard_map.153
  98.2 40.3 %all_to_all.32.got = bf16[64,8,2048]{2,1,0:T(8,128)(2,1)S(1)} all-to-all(bf16[64,8,2048]{2,1,0:T(8,128)(2,1)S(1)} %bitcast.28), channel_id=1, replica_groups=mesh['xh'=2,'y'=4,'xl'=2,'c'=2,'z'=4] {'xh','xl','z','y'}, dimensions={0} | all-to-all | bytes 4194304 | tf_op jit(solution)/shard_map/all_to_all | solution.py:498
  138.5 0.6 shard_map.154
  139.1 35.0 %all_to_all.33 = bf16[64,8,2048]{2,1,0:T(8,128)(2,1)S(1)} all-to-all(bf16[64,8,2048]{2,1,0:T(8,128)(2,1)S(1)} %get-tuple-element.70), channel_id=1, replica_groups=mesh['xh'=2,'y'=4,'xl'=2,'c'=2,'z'=4] {'xh','xl','z','y'}, dimensions={0} | all-to-all | bytes 4194304 | tf_op jit(solution)/shard_map/all_to_all | solution.py:501
  174.1 2.8 %shard_map.156 = bf16[256,896]{1,0:T(8,128)(2,1)S(1)} custom-call(s32[1]{0:T(128)S(6)} %sub.4.part_ref, bf16[512,2048]{1,0:T(8,128)(2,1)S(1)} %bitcast.25, bf16[256,896]{1,0:T(8,128)(2,1)S(1)} %copy-done.1, bf16[256,896]{1,0:T(8,128)(2,1)} %collective-permute-done.3.refs_1_, bf16[256,896]{1,0:T(8,128)(2,1)} %collective-permute-done.4.refs_2_, ...), custom_call_target="tpu_custom_call" | custom-call | tf_op jit(solution)/shard_map/pallas_call | solution.py:161
  177.0 2.8 %shard_map.155.keep = f32[256,896]{1,0:T(8,128)S(1)} custom-call(s32[1]{0:T(128)} %bitcast.8.part_ref.xl_ref, bf16[512,2048]{1,0:T(8,128)(2,1)S(1)} %bitcast.26, bf16[256,896]{1,0:T(8,128)(2,1)S(1)} %copy-done.1, bf16[256,896]{1,0:T(8,128)(2,1)} %collective-permute-done.3.refs_1_, bf16[256,896]{1,0:T(8,128)(2,1)} %collective-permute-done.4.refs_2_, ...), custom_call_target="tpu_custom_call" | custom-call | tf_op jit(solution)/shard_map/pallas_call | solution.py:161
  179.9 7.5 %collective-permute-done.19.other = bf16[256,896]{1,0:T(8,128)(2,1)S(1)} collective-permute-done((bf16[256,896]{1,0:T(8,128)(2,1)S(1)}, bf16[256,896]{1,0:T(8,128)(2,1)S(1)}, u32[]{:S(2)}, u32[]{:S(2)}) %collective-permute-start.19) | collective-permute-done | bytes 458784 | tf_op jit(solution)/shard_map/ppermute | solution.py:491
  187.7 6.4 %collective-permute-done.20.other = bf16[256,512]{1,0:T(8,128)(2,1)S(1)} collective-permute-done((bf16[256,512]{1,0:T(8,128)(2,1)S(1)}, bf16[256,512]{1,0:T(8,128)(2,1)S(1)}, u32[]{:S(2)}, u32[]{:S(2)}) %collective-permute-start.20) | collective-permute-done | bytes 262176 | tf_op jit(solution)/shard_map/ppermute | solution.py:494
  194.1 1.3 shard_map.158
  195.4 33.5 %all_to_all.34.got = bf16[64,8,2048]{2,1,0:T(8,128)(2,1)S(1)} all-to-all(bf16[64,8,2048]{2,1,0:T(8,128)(2,1)S(1)} %bitcast.27), channel_id=1, replica_groups=mesh['xh'=2,'y'=4,'xl'=2,'c'=2,'z'=4] {'xh','xl','z','y'}, dimensions={0} | all-to-all | bytes 4194304 | tf_op jit(solution)/shard_map/all_to_all | solution.py:498
  228.9 0.9 shard_map.159
  (53 shorter events, 3.4 us)
Async XLA Ops:
  2.6 25.3 %all-to-all-start = ((f32[128,1,128]{2,1,0:T(1,128)}), f32[128,1,128]{2,1,0:T(1,128)S(1)}, u32[]{:S(2)}, u32[]{:S(2)}) async-start(f32[128,1,128]{2,1,0:T(1,128)} %bitcast.31), calls=%async_computation | async-start | bytes 131072 | tf_op jit(solution)/shard_map/all_to_all | solution.py:465
  23.8 12.1 %collective-permute-start.2 = (bf16[8,4096]{1,0:T(8,128)(2,1)}, bf16[8,4096]{1,0:T(8,128)(2,1)S(1)}, u32[]{:S(2)}, u32[]{:S(2)}) collective-permute-start(bf16[8,4096]{1,0:T(8,128)(2,1)} %get-tuple-element.47.refs_0_), channel_id=1, source_target_pairs={{0,48},{16,32},{32,16},{48,0},{1,49},{17,33},{33,17},{49,1},{2,50}... | collective-permute-start | bytes 196616 | tf_op jit(solution)/shard_map/ppermute | solution.py:438
  26.0 9.8 %collective-permute-start.1 = (bf16[8,4096]{1,0:T(8,128)(2,1)}, bf16[8,4096]{1,0:T(8,128)(2,1)S(1)}, u32[]{:S(2)}, u32[]{:S(2)}) collective-permute-start(bf16[8,4096]{1,0:T(8,128)(2,1)} %get-tuple-element.47.refs_0_), channel_id=1, source_target_pairs={{0,32},{16,48},{32,0},{48,16},{1,33},{17,49},{33,1},{49,17},{2,34}... | collective-permute-start | bytes 196616 | tf_op jit(solution)/shard_map/ppermute | solution.py:438
  26.9 9.0 %collective-permute-start = (bf16[8,4096]{1,0:T(8,128)(2,1)}, bf16[8,4096]{1,0:T(8,128)(2,1)S(1)}, u32[]{:S(2)}, u32[]{:S(2)}) collective-permute-start(bf16[8,4096]{1,0:T(8,128)(2,1)} %get-tuple-element.47.refs_0_), channel_id=1, source_target_pairs={{0,16},{16,0},{32,48},{48,32},{1,17},{17,1},{33,49},{49,33},{2,18}... | collective-permute-start | bytes 196616 | tf_op jit(solution)/shard_map/ppermute | solution.py:438
  29.3 6.6 %copy-start.10 = (bf16[8,4096]{1,0:T(8,128)(2,1)S(1)}, bf16[8,4096]{1,0:T(8,128)(2,1)}, u32[]{:S(2)}) copy-start(bf16[8,4096]{1,0:T(8,128)(2,1)} %get-tuple-element.47.refs_0_) | copy-start | bytes 196612
  36.1 1.4 copy-start
  37.4 36.0 %all-to-all-start.1 = ((bf16[16,4,8,2048]{3,2,1,0:T(8,128)(2,1)}), bf16[16,4,8,2048]{3,2,1,0:T(8,128)(2,1)S(1)}, u32[]{:S(2)}, u32[]{:S(2)}) async-start(bf16[16,4,8,2048]{3,2,1,0:T(8,128)(2,1)} %copy-done), calls=%async_computation.1 | async-start | bytes 4194304 | tf_op jit(solution)/shard_map/all_to_all | solution.py:479
  44.1 14.5 %copy-start.1 = (bf16[256,896]{1,0:T(8,128)(2,1)S(1)}, bf16[256,896]{1,0:T(8,128)(2,1)}, u32[]{:S(2)}) copy-start(bf16[256,896]{1,0:T(8,128)(2,1)} %get-tuple-element.57.refs_0_) | copy-start | bytes 1376260
  44.1 22.8 %collective-permute-start.8 = (bf16[256,896]{1,0:T(8,128)(2,1)}, bf16[256,896]{1,0:T(8,128)(2,1)S(1)}, u32[]{:S(2)}, u32[]{:S(2)}) collective-permute-start(bf16[256,896]{1,0:T(8,128)(2,1)} %get-tuple-element.62), channel_id=1, source_target_pairs={{0,48},{16,32},{32,16},{48,0},{1,49},{17,33},{33,17},{49,1},{2,50}... | collective-permute-start | bytes 1376264 | tf_op jit(solution)/shard_map/ppermute | solution.py:438
  47.1 19.8 %collective-permute-start.6 = (bf16[256,896]{1,0:T(8,128)(2,1)}, bf16[256,896]{1,0:T(8,128)(2,1)S(1)}, u32[]{:S(2)}, u32[]{:S(2)}) collective-permute-start(bf16[256,896]{1,0:T(8,128)(2,1)} %get-tuple-element.60), channel_id=1, source_target_pairs={{0,32},{16,48},{32,0},{48,16},{1,33},{17,49},{33,1},{49,17},{2,34}... | collective-permute-start | bytes 1376264 | tf_op jit(solution)/shard_map/ppermute | solution.py:438
  47.8 19.9 %collective-permute-start.4 = (bf16[256,896]{1,0:T(8,128)(2,1)}, bf16[256,896]{1,0:T(8,128)(2,1)}, u32[]{:S(2)}, u32[]{:S(2)}) collective-permute-start(bf16[256,896]{1,0:T(8,128)(2,1)} %get-tuple-element.58), channel_id=1, source_target_pairs={{0,16},{16,0},{32,48},{48,32},{1,17},{17,1},{33,49},{49,33},{2,18}... | collective-permute-start | bytes 1376264 | tf_op jit(solution)/shard_map/ppermute | solution.py:438
  48.3 1.2 copy-start.2
  49.5 1.5 copy-start.3
  51.0 1.5 copy-start.4
  52.5 1.5 copy-start.5
  55.8 0.7 copy-start.6
  56.5 0.7 copy-start.12
  57.2 0.7 copy-start.14
  57.9 0.7 copy-start.16
  58.6 9.5 %collective-permute-start.3 = (bf16[256,896]{1,0:T(8,128)(2,1)S(1)}, bf16[256,896]{1,0:T(8,128)(2,1)}, u32[]{:S(2)}, u32[]{:S(2)}) collective-permute-start(bf16[256,896]{1,0:T(8,128)(2,1)S(1)} %copy-done.1), channel_id=1, source_target_pairs={{0,4},{4,0},{1,5},{5,1},{2,6},{6,2},{3,7},{7,3},{8,12},{12,8},{9,1... | collective-permute-start | bytes 1376264 | tf_op jit(solution)/shard_map/ppermute | solution.py:442
  67.6 2.8 %collective-permute-start.5 = (bf16[256,896]{1,0:T(8,128)(2,1)}, bf16[256,896]{1,0:T(8,128)(2,1)}, u32[]{:S(2)}, u32[]{:S(2)}) collective-permute-start(bf16[256,896]{1,0:T(8,128)(2,1)} %collective-permute-done.4.refs_2_), channel_id=1, source_target_pairs={{0,4},{4,0},{1,5},{5,1},{2,6},{6,2},{3,7},{7,3},{8,12},{12,8},{9,1... | collective-permute-start | bytes 1376264 | tf_op jit(solution)/shard_map/ppermute | solution.py:442
  67.6 2.8 %collective-permute-start.7 = (bf16[256,896]{1,0:T(8,128)(2,1)S(1)}, bf16[256,896]{1,0:T(8,128)(2,1)}, u32[]{:S(2)}, u32[]{:S(2)}) collective-permute-start(bf16[256,896]{1,0:T(8,128)(2,1)S(1)} %collective-permute-done.6.refs_4_), channel_id=1, source_target_pairs={{0,4},{4,0},{1,5},{5,1},{2,6},{6,2},{3,7},{7,3},{8,12},{12,8},{9,1... | collective-permute-start | bytes 1376264 | tf_op jit(solution)/shard_map/ppermute | solution.py:442
  68.2 2.7 %collective-permute-start.9 = (bf16[256,896]{1,0:T(8,128)(2,1)S(1)}, bf16[256,896]{1,0:T(8,128)(2,1)}, u32[]{:S(2)}, u32[]{:S(2)}) collective-permute-start(bf16[256,896]{1,0:T(8,128)(2,1)S(1)} %collective-permute-done.8.refs_6_), channel_id=1, source_target_pairs={{0,4},{4,0},{1,5},{5,1},{2,6},{6,2},{3,7},{7,3},{8,12},{12,8},{9,1... | collective-permute-start | bytes 1376264 | tf_op jit(solution)/shard_map/ppermute | solution.py:442
  73.4 3.0 %copy-start.17 = (bf16[256,512]{1,0:T(8,128)(2,1)S(1)}, bf16[256,512]{1,0:T(8,128)(2,1)}, u32[]{:S(2)}) copy-start(bf16[256,512]{1,0:T(8,128)(2,1)} %copy-done.16) | copy-start | bytes 786436
  73.4 4.8 %copy-start.15 = (bf16[256,512]{1,0:T(8,128)(2,1)S(1)}, bf16[256,512]{1,0:T(8,128)(2,1)}, u32[]{:S(2)}) copy-start(bf16[256,512]{1,0:T(8,128)(2,1)} %copy-done.14) | copy-start | bytes 786436
  73.4 7.6 %copy-start.13 = (bf16[256,512]{1,0:T(8,128)(2,1)S(1)}, bf16[256,512]{1,0:T(8,128)(2,1)}, u32[]{:S(2)}) copy-start(bf16[256,512]{1,0:T(8,128)(2,1)} %copy-done.12) | copy-start | bytes 786436
  76.4 17.9 %copy-start.7 = (bf16[256,512]{1,0:T(8,128)(2,1)S(1)}, bf16[256,512]{1,0:T(8,128)(2,1)}, u32[]{:S(2)}) copy-start(bf16[256,512]{1,0:T(8,128)(2,1)} %copy-done.6) | copy-start | bytes 786436
  76.4 10.1 %collective-permute-start.10 = (bf16[256,896]{1,0:T(8,128)(2,1)S(1)}, bf16[256,896]{1,0:T(8,128)(2,1)S(1)}, u32[]{:S(2)}, u32[]{:S(2)}) collective-permute-start(bf16[256,896]{1,0:T(8,128)(2,1)S(1)} %shard_map.151), channel_id=1, source_target_pairs={{0,8},{8,0},{1,9},{9,1},{2,10},{10,2},{3,11},{11,3},{4,12},{12,4},... | collective-permute-start | bytes 1376264 | tf_op jit(solution)/shard_map/ppermute | solution.py:491
  76.5 11.9 %collective-permute-start.12 = (bf16[256,512]{1,0:T(8,128)(2,1)S(1)}, bf16[256,512]{1,0:T(8,128)(2,1)S(1)}, u32[]{:S(2)}, u32[]{:S(2)}) collective-permute-start(bf16[256,512]{1,0:T(8,128)(2,1)S(1)} %copy-done.17), channel_id=1, source_target_pairs={{0,16},{16,0},{32,48},{48,32},{1,17},{17,1},{33,49},{49,33},{2,18}... | collective-permute-start | bytes 786440 | tf_op jit(solution)/shard_map/ppermute | solution.py:438
  78.2 13.4 %collective-permute-start.13 = (bf16[256,512]{1,0:T(8,128)(2,1)S(1)}, bf16[256,512]{1,0:T(8,128)(2,1)S(1)}, u32[]{:S(2)}, u32[]{:S(2)}) collective-permute-start(bf16[256,512]{1,0:T(8,128)(2,1)S(1)} %copy-done.15), channel_id=1, source_target_pairs={{0,32},{16,48},{32,0},{48,16},{1,33},{17,49},{33,1},{49,17},{2,34}... | collective-permute-start | bytes 786440 | tf_op jit(solution)/shard_map/ppermute | solution.py:438
  81.0 13.2 %collective-permute-start.14 = (bf16[256,512]{1,0:T(8,128)(2,1)S(1)}, bf16[256,512]{1,0:T(8,128)(2,1)S(1)}, u32[]{:S(2)}, u32[]{:S(2)}) collective-permute-start(bf16[256,512]{1,0:T(8,128)(2,1)S(1)} %copy-done.13), channel_id=1, source_target_pairs={{0,48},{16,32},{32,16},{48,0},{1,49},{17,33},{33,17},{49,1},{2,50}... | collective-permute-start | bytes 786440 | tf_op jit(solution)/shard_map/ppermute | solution.py:438
  86.7 7.5 %collective-permute-start.11 = (bf16[256,512]{1,0:T(8,128)(2,1)S(1)}, bf16[256,512]{1,0:T(8,128)(2,1)S(1)}, u32[]{:S(2)}, u32[]{:S(2)}) collective-permute-start(bf16[256,512]{1,0:T(8,128)(2,1)S(1)} %shard_map.152.own), channel_id=1, source_target_pairs={{0,8},{8,0},{1,9},{9,1},{2,10},{10,2},{3,11},{11,3},{4,12},{12,4},... | collective-permute-start | bytes 786440 | tf_op jit(solution)/shard_map/ppermute | solution.py:494
  94.2 1.5 collective-permute-start.15
  94.2 1.9 collective-permute-start.16
  94.7 1.8 collective-permute-start.17
  94.8 2.1 collective-permute-start.18
  98.2 40.3 %copy-start.8 = (f32[1,8,4096]{2,1,0:T(8,128)S(1)}, f32[1,8,4096]{2,1,0:T(8,128)}, u32[]{:S(2)}) copy-start(f32[1,8,4096]{2,1,0:T(8,128)} %get-tuple-element.68.attended) | copy-start | bytes 393220
  98.2 40.3 %copy-start.9 = (bf16[8,4096]{1,0:T(8,128)(2,1)S(1)}, bf16[8,4096]{1,0:T(8,128)(2,1)}, u32[]{:S(2)}) copy-start(bf16[8,4096]{1,0:T(8,128)(2,1)} %get-tuple-element.39.rows) | copy-start | bytes 196612
  98.2 40.3 %copy-start.11 = (f32[4096]{0:T(1024)S(1)}, f32[4096]{0:T(1024)}, u32[]{:S(2)}) copy-start(f32[4096]{0:T(1024)} %param.23) | copy-start | bytes 49156
  176.9 10.5 %collective-permute-start.19 = (bf16[256,896]{1,0:T(8,128)(2,1)S(1)}, bf16[256,896]{1,0:T(8,128)(2,1)S(1)}, u32[]{:S(2)}, u32[]{:S(2)}) collective-permute-start(bf16[256,896]{1,0:T(8,128)(2,1)S(1)} %shard_map.156), channel_id=1, source_target_pairs={{0,8},{8,0},{1,9},{9,1},{2,10},{10,2},{3,11},{11,3},{4,12},{12,4},... | collective-permute-start | bytes 1376264 | tf_op jit(solution)/shard_map/ppermute | solution.py:491
  187.6 6.5 %collective-permute-start.20 = (bf16[256,512]{1,0:T(8,128)(2,1)S(1)}, bf16[256,512]{1,0:T(8,128)(2,1)S(1)}, u32[]{:S(2)}, u32[]{:S(2)}) collective-permute-start(bf16[256,512]{1,0:T(8,128)(2,1)S(1)} %shard_map.157.own), channel_id=1, source_target_pairs={{0,8},{8,0},{1,9},{9,1},{2,10},{10,2},{3,11},{11,3},{4,12},{12,4},... | collective-permute-start | bytes 786440 | tf_op jit(solution)/shard_map/ppermute | solution.py:494

commit v5 on v4

--- a/solution.py
+++ b/solution.py
@@ -231,14 +231,17 @@
 ):
     n_pages = pages.shape[1]
 
-    def fetch(r, p):
-        return pltpu.make_async_copy(kv_far.at[pages[r, p]], kv_ref.at[r, p], sems.at[r, p])
-
-    for r in range(pages.shape[0]):
-        for p in range(n_pages):
-            fetch(r, p).start()
+    part = kv_far.shape[0] // sems.shape[0]
+    fetches = [
+        pltpu.make_async_copy(
+            kv_far.at[pl.ds(i * part, part)], kv_ref.at[pl.ds(i * part, part)], sems.at[i]
+        )
+        for i in range(sems.shape[0])
+    ]
+    for fetch in fetches:
+        fetch.start()
     steps, rows, width = q_ref.shape
-    pairs_of = kv_ref.shape[3]
+    pairs_of = kv_ref.shape[2]
     heads = pairs_of // 2
     group = width // HD // heads
     per_head = steps * group
@@ -246,7 +249,7 @@
     scale = HD**-0.5
     q32[...] = q_ref[...].astype(F32)
     fresh32[...] = fresh_ref[...].astype(F32)
-    ctx = n_pages * kv_ref.shape[2] * pairs_of
+    ctx = n_pages * kv_ref.shape[1] * pairs_of
     lane = lax.broadcasted_iota(jnp.int32, (count, ctx), 1)
     head_of = lax.broadcasted_iota(jnp.int32, (count, ctx), 0) // per_head
     own_key = lane % pairs_of == 2 * head_of
@@ -267,10 +270,12 @@
             parts.append(jnp.broadcast_to(fresh32[t, r, at : at + 1, :], (per_head, HD)))
         return jnp.concatenate(parts, axis=0)
 
+    for fetch in fetches:
+        fetch.wait()
     for r in range(rows):
-        for p in range(n_pages):
-            fetch(r, p).wait()
-        kv = kv_ref[r].reshape(ctx, HD)
+        kv = jnp.concatenate(
+            [kv_ref[pages[r, p]].reshape(ctx // n_pages, HD) for p in range(n_pages)], axis=0
+        )
         q = q_rows[r * count : (r + 1) * count, :]
         old = lax.dot_general(
             q.astype(BF16), kv, (((1,), (1,)), ((), ())), preferred_element_type=F32
@@ -326,12 +331,12 @@
             jax.ShapeDtypeStruct((steps - 1, rows, width), F32),
         ],
         scratch_shapes=[
-            pltpu.VMEM(page_table.shape + pool.shape[1:], pool.dtype),
+            pltpu.VMEM(pool.shape, pool.dtype),
             pltpu.VMEM((steps, rows, width), F32),
             pltpu.VMEM((steps, rows, 2 * heads, HD), F32),
             pltpu.VMEM((steps * rows * width // HD, HD), F32),
             pltpu.VMEM((rows, width), F32),
-            pltpu.SemaphoreType.DMA(page_table.shape),
+            pltpu.SemaphoreType.DMA((16,)),
         ],
         cost_estimate=pl.CostEstimate(
             flops=16 * steps * width * pool.shape[0] * pool.shape[1] * pool.shape[2],

time: 230 us -> 230 us (level)
  transfers between devices with their start and end apart: 23 -> 23, of which waited for: 14 -> 14; matrix products, arithmetic and copies ran while one was open for 0% -> 0% of each run, Pallas kernels for 11% -> 10%
where the time goes in v5:
time: 230 us
  blocking collectives  109 us (47%)
  waiting for transfers between devices  38.1 us (17%)
  Pallas kernels  36.6 us (16%)
  starting transfers between devices  34.5 us (15%)
  local copies, waits for them, and re-layouts  9.88 us (4%)
    all_to_all x2, blocking collectives, shards(): got = lax.all_to_all(partial.reshape(64, -1, D // 2), GROUP, 0, 0)  73.8 us
    all_to_all x1, blocking collectives, shards(): handed = lax.all_to_all(payload, GROUP, 0, 0)  35.1 us
    ppermute x9, waiting for transfers between devices, over_y(): lax.ppermute(p, 'y', pairs('y', k))  14.8 us
    ppermute x9, starting transfers between devices, over_y(): lax.ppermute(p, 'y', pairs('y', k))  13.1 us
    pallas_call x4, Pallas kernels, first_products(): pl.pallas_call(first_body, in_specs=[pl.BlockSpec(memory_space=pltpu.SMEM...  11.4 us
    all_to_all x1, starting transfers between devices, shards(): squares = lax.all_to_all(squares, ALL, 0, 0)  11.1 us
    ppermute x2, waiting for transfers between devices, shards(): other = lax.ppermute(send, 'xl', pairs('xl', 1))  9.93 us
    unnamed x36, local copies, waits for them, and re-layouts  9.88 us
  transfers between devices with their start and end apart: 23, of which 14 were waited for; matrix products, arithmetic and copies ran while one was open for 0% of the time, Pallas kernels for 10%

profile of v5, /device:TPU:0, one launch (start us, length us, event | category | flops | bytes accessed | tf_op | source)
XLA Modules:
  0.0 229.6 jit_solution(10730813631846286732)
XLA Ops:
  0.0 2.6 %shard_map.145 = f32[128,128]{1,0:T(8,128)} custom-call(bf16[2,256,1792]{2,1,0:T(8,128)(2,1)} %refs_3_.1, bf16[256,1792]{1,0:T(8,128)(2,1)} %grad.1), custom_call_target="tpu_custom_call" | custom-call | tf_op jit(solution)/shard_map/pallas_call | solution.py:66
  2.6 11.1 %all-to-all-start = ((f32[128,1,128]{2,1,0:T(1,128)}), f32[128,1,128]{2,1,0:T(1,128)S(1)}, u32[]{:S(2)}, u32[]{:S(2)}) async-start(f32[128,1,128]{2,1,0:T(1,128)} %bitcast.31), calls=%async_computation | async-start | bytes 131072 | tf_op jit(solution)/shard_map/all_to_all | solution.py:470
  13.8 9.6 %shard_map.146 = (bf16[8,4096]{1,0:T(8,128)(2,1)}, bf16[8,4096]{1,0:T(8,128)(2,1)}, f32[1,8,4096]{2,1,0:T(8,128)}) custom-call(s32[8,8]{1,0:T(8,128)} %pages, s32[8]{0:T(128)} %lens.1, bf16[8,4096]{1,0:T(8,128)(2,1)} %rows_ref.1, f32[1,4096]{1,0:T(1,128)} %bitcast.29, bf16[2,8,4096]{2,1,0:T(8,128)(2,1)} %q_ref.1, bf16[2,8,16,128]{3,2,1,0:T(8,128)(2,1)} %bitcast.34, ...), custom_call_target="tpu_custom_call" | custom-call | flops 2147483648 | bytes 33554432 | tf_op jit(solution)/shard_map/pallas_call | solution.py:324
  23.4 2.3 %collective-permute-start.2 = (bf16[8,4096]{1,0:T(8,128)(2,1)}, bf16[8,4096]{1,0:T(8,128)(2,1)S(1)}, u32[]{:S(2)}, u32[]{:S(2)}) collective-permute-start(bf16[8,4096]{1,0:T(8,128)(2,1)} %get-tuple-element.47.refs_0_), channel_id=1, source_target_pairs={{0,48},{16,32},{32,16},{48,0},{1,49},{17,33},{33,17},{49,1},{2,50}... | collective-permute-start | bytes 196616 | tf_op jit(solution)/shard_map/ppermute | solution.py:443
  25.7 0.8 collective-permute-start.1
  26.5 1.1 collective-permute-start
  27.6 0.7 slice_reduce_fusion
  29.0 6.6 %shard_map.147 = (bf16[256,896]{1,0:T(8,128)(2,1)}, bf16[256,896]{1,0:T(8,128)(2,1)}, bf16[256,896]{1,0:T(8,128)(2,1)}, bf16[256,896]{1,0:T(8,128)(2,1)}) custom-call(s32[1]{0:T(128)} %bitcast.9.y_ref, f32[1]{0:T(128)} %bitcast.13.clip_ref, f32[2,256,1792]{2,1,0:T(8,128)} %refs_0_.1, f32[2,256,1792]{2,1,0:T(8,128)} %refs_1_.1, f32[2,256,1792]{2,1,0:T(8,128)} %refs_2_.1, ...), custom_call_target="tpu_custom_call" | custom-call | tf_op jit(solution)/shard_map/pallas_call | solution.py:107
  35.7 1.3 copy-done
  37.1 6.7 %all-to-all-start.1 = ((bf16[16,4,8,2048]{3,2,1,0:T(8,128)(2,1)}), bf16[16,4,8,2048]{3,2,1,0:T(8,128)(2,1)S(1)}, u32[]{:S(2)}, u32[]{:S(2)}) async-start(bf16[16,4,8,2048]{3,2,1,0:T(8,128)(2,1)} %copy-done), calls=%async_computation.1 | async-start | bytes 4194304 | tf_op jit(solution)/shard_map/all_to_all | solution.py:484
  43.8 3.0 %collective-permute-start.8 = (bf16[256,896]{1,0:T(8,128)(2,1)}, bf16[256,896]{1,0:T(8,128)(2,1)S(1)}, u32[]{:S(2)}, u32[]{:S(2)}) collective-permute-start(bf16[256,896]{1,0:T(8,128)(2,1)} %get-tuple-element.62), channel_id=1, source_target_pairs={{0,48},{16,32},{32,16},{48,0},{1,49},{17,33},{33,17},{49,1},{2,50}... | collective-permute-start | bytes 1376264 | tf_op jit(solution)/shard_map/ppermute | solution.py:443
  46.8 0.7 collective-permute-start.6
  47.4 0.5 collective-permute-start.4
  47.9 1.2 copy-done.2
  49.1 1.5 copy-done.3
  50.6 1.5 copy-done.4
  52.1 1.5 copy-done.5
  53.6 1.8 shard_map.149
  55.5 0.7 copy-done.6
  56.1 0.7 copy-done.12
  56.9 0.7 copy-done.14
  57.6 0.7 copy-done.16
  58.3 8.3 %collective-permute-done.8.refs_6_ = bf16[256,896]{1,0:T(8,128)(2,1)S(1)} collective-permute-done((bf16[256,896]{1,0:T(8,128)(2,1)}, bf16[256,896]{1,0:T(8,128)(2,1)S(1)}, u32[]{:S(2)}, u32[]{:S(2)}) %collective-permute-start.8) | collective-permute-done | bytes 458784 | tf_op jit(solution)/shard_map/ppermute | solution.py:443
  66.6 0.7 collective-permute-done.4.refs_2_
  67.3 0.5 collective-permute-start.7
  67.8 2.3 collective-permute-done.5.refs_3_
  70.6 2.5 %all-to-all-done.1 = bf16[16,4,8,2048]{3,2,1,0:T(8,128)(2,1)S(1)} async-done(((bf16[16,4,8,2048]{3,2,1,0:T(8,128)(2,1)}), bf16[16,4,8,2048]{3,2,1,0:T(8,128)(2,1)S(1)}, u32[]{:S(2)}, u32[]{:S(2)}) %all-to-all-start.1) | async-done | bytes 2097184 | tf_op jit(solution)/shard_map/all_to_all | solution.py:484
  73.1 2.9 %shard_map.151 = bf16[256,896]{1,0:T(8,128)(2,1)S(1)} custom-call(s32[1]{0:T(128)S(6)} %sub.4.part_ref, bf16[512,2048]{1,0:T(8,128)(2,1)S(1)} %bitcast.23, bf16[256,896]{1,0:T(8,128)(2,1)S(1)} %copy-done.1, bf16[256,896]{1,0:T(8,128)(2,1)} %collective-permute-done.3.refs_1_, bf16[256,896]{1,0:T(8,128)(2,1)} %collective-permute-done.4.refs_2_, ...), custom_call_target="tpu_custom_call" | custom-call | tf_op jit(solution)/shard_map/pallas_call | solution.py:161
  76.1 1.6 collective-permute-start.12
  77.7 2.8 %collective-permute-start.13 = (bf16[256,512]{1,0:T(8,128)(2,1)S(1)}, bf16[256,512]{1,0:T(8,128)(2,1)S(1)}, u32[]{:S(2)}, u32[]{:S(2)}) collective-permute-start(bf16[256,512]{1,0:T(8,128)(2,1)S(1)} %copy-done.15), channel_id=1, source_target_pairs={{0,32},{16,48},{32,0},{48,16},{1,33},{17,49},{33,1},{49,17},{2,34}... | collective-permute-start | bytes 786440 | tf_op jit(solution)/shard_map/ppermute | solution.py:443
  80.9 2.8 %shard_map.150.keep = f32[256,896]{1,0:T(8,128)S(1)} custom-call(s32[1]{0:T(128)} %bitcast.8.part_ref.xl_ref, bf16[512,2048]{1,0:T(8,128)(2,1)S(1)} %bitcast.24, bf16[256,896]{1,0:T(8,128)(2,1)S(1)} %copy-done.1, bf16[256,896]{1,0:T(8,128)(2,1)} %collective-permute-done.3.refs_1_, bf16[256,896]{1,0:T(8,128)(2,1)} %collective-permute-done.4.refs_2_, ...), custom_call_target="tpu_custom_call" | custom-call | tf_op jit(solution)/shard_map/pallas_call | solution.py:161
  83.7 2.4 %collective-permute-done.10.other = bf16[256,896]{1,0:T(8,128)(2,1)S(1)} collective-permute-done((bf16[256,896]{1,0:T(8,128)(2,1)S(1)}, bf16[256,896]{1,0:T(8,128)(2,1)S(1)}, u32[]{:S(2)}, u32[]{:S(2)}) %collective-permute-start.10) | collective-permute-done | bytes 458784 | tf_op jit(solution)/shard_map/ppermute | solution.py:496
  86.3 1.7 collective-permute-start.11
  88.1 3.2 %collective-permute-done.13.refs_4_ = bf16[256,512]{1,0:T(8,128)(2,1)S(1)} collective-permute-done((bf16[256,512]{1,0:T(8,128)(2,1)S(1)}, bf16[256,512]{1,0:T(8,128)(2,1)S(1)}, u32[]{:S(2)}, u32[]{:S(2)}) %collective-permute-start.13) | collective-permute-done | bytes 262176 | tf_op jit(solution)/shard_map/ppermute | solution.py:443
  91.3 2.6 %collective-permute-done.14.refs_6_ = bf16[256,512]{1,0:T(8,128)(2,1)S(1)} collective-permute-done((bf16[256,512]{1,0:T(8,128)(2,1)S(1)}, bf16[256,512]{1,0:T(8,128)(2,1)S(1)}, u32[]{:S(2)}, u32[]{:S(2)}) %collective-permute-start.14) | collective-permute-done | bytes 262176 | tf_op jit(solution)/shard_map/ppermute | solution.py:443
  93.9 0.5 collective-permute-start.16
  94.9 0.5 collective-permute-done.15.refs_1_
  96.5 1.3 shard_map.153
  97.9 40.2 %all_to_all.32.got = bf16[64,8,2048]{2,1,0:T(8,128)(2,1)S(1)} all-to-all(bf16[64,8,2048]{2,1,0:T(8,128)(2,1)S(1)} %bitcast.28), channel_id=1, replica_groups=mesh['xh'=2,'y'=4,'xl'=2,'c'=2,'z'=4] {'xh','xl','z','y'}, dimensions={0} | all-to-all | bytes 4194304 | tf_op jit(solution)/shard_map/all_to_all | solution.py:503
  138.1 0.6 shard_map.154
  138.7 35.1 %all_to_all.33 = bf16[64,8,2048]{2,1,0:T(8,128)(2,1)S(1)} all-to-all(bf16[64,8,2048]{2,1,0:T(8,128)(2,1)S(1)} %get-tuple-element.70), channel_id=1, replica_groups=mesh['xh'=2,'y'=4,'xl'=2,'c'=2,'z'=4] {'xh','xl','z','y'}, dimensions={0} | all-to-all | bytes 4194304 | tf_op jit(solution)/shard_map/all_to_all | solution.py:506
  173.8 2.8 %shard_map.156 = bf16[256,896]{1,0:T(8,128)(2,1)S(1)} custom-call(s32[1]{0:T(128)S(6)} %sub.4.part_ref, bf16[512,2048]{1,0:T(8,128)(2,1)S(1)} %bitcast.25, bf16[256,896]{1,0:T(8,128)(2,1)S(1)} %copy-done.1, bf16[256,896]{1,0:T(8,128)(2,1)} %collective-permute-done.3.refs_1_, bf16[256,896]{1,0:T(8,128)(2,1)} %collective-permute-done.4.refs_2_, ...), custom_call_target="tpu_custom_call" | custom-call | tf_op jit(solution)/shard_map/pallas_call | solution.py:161
  176.7 2.8 %shard_map.155.keep = f32[256,896]{1,0:T(8,128)S(1)} custom-call(s32[1]{0:T(128)} %bitcast.8.part_ref.xl_ref, bf16[512,2048]{1,0:T(8,128)(2,1)S(1)} %bitcast.26, bf16[256,896]{1,0:T(8,128)(2,1)S(1)} %copy-done.1, bf16[256,896]{1,0:T(8,128)(2,1)} %collective-permute-done.3.refs_1_, bf16[256,896]{1,0:T(8,128)(2,1)} %collective-permute-done.4.refs_2_, ...), custom_call_target="tpu_custom_call" | custom-call | tf_op jit(solution)/shard_map/pallas_call | solution.py:161
  179.5 7.5 %collective-permute-done.19.other = bf16[256,896]{1,0:T(8,128)(2,1)S(1)} collective-permute-done((bf16[256,896]{1,0:T(8,128)(2,1)S(1)}, bf16[256,896]{1,0:T(8,128)(2,1)S(1)}, u32[]{:S(2)}, u32[]{:S(2)}) %collective-permute-start.19) | collective-permute-done | bytes 458784 | tf_op jit(solution)/shard_map/ppermute | solution.py:496
  187.4 6.4 %collective-permute-done.20.other = bf16[256,512]{1,0:T(8,128)(2,1)S(1)} collective-permute-done((bf16[256,512]{1,0:T(8,128)(2,1)S(1)}, bf16[256,512]{1,0:T(8,128)(2,1)S(1)}, u32[]{:S(2)}, u32[]{:S(2)}) %collective-permute-start.20) | collective-permute-done | bytes 262176 | tf_op jit(solution)/shard_map/ppermute | solution.py:499
  193.8 1.3 shard_map.158
  195.0 33.6 %all_to_all.34.got = bf16[64,8,2048]{2,1,0:T(8,128)(2,1)S(1)} all-to-all(bf16[64,8,2048]{2,1,0:T(8,128)(2,1)S(1)} %bitcast.27), channel_id=1, replica_groups=mesh['xh'=2,'y'=4,'xl'=2,'c'=2,'z'=4] {'xh','xl','z','y'}, dimensions={0} | all-to-all | bytes 4194304 | tf_op jit(solution)/shard_map/all_to_all | solution.py:503
  228.6 0.9 shard_map.159
  (53 shorter events, 3.4 us)
Async XLA Ops:
  2.6 24.9 %all-to-all-start = ((f32[128,1,128]{2,1,0:T(1,128)}), f32[128,1,128]{2,1,0:T(1,128)S(1)}, u32[]{:S(2)}, u32[]{:S(2)}) async-start(f32[128,1,128]{2,1,0:T(1,128)} %bitcast.31), calls=%async_computation | async-start | bytes 131072 | tf_op jit(solution)/shard_map/all_to_all | solution.py:470
  23.4 12.1 %collective-permute-start.2 = (bf16[8,4096]{1,0:T(8,128)(2,1)}, bf16[8,4096]{1,0:T(8,128)(2,1)S(1)}, u32[]{:S(2)}, u32[]{:S(2)}) collective-permute-start(bf16[8,4096]{1,0:T(8,128)(2,1)} %get-tuple-element.47.refs_0_), channel_id=1, source_target_pairs={{0,48},{16,32},{32,16},{48,0},{1,49},{17,33},{33,17},{49,1},{2,50}... | collective-permute-start | bytes 196616 | tf_op jit(solution)/shard_map/ppermute | solution.py:443
  25.7 9.8 %collective-permute-start.1 = (bf16[8,4096]{1,0:T(8,128)(2,1)}, bf16[8,4096]{1,0:T(8,128)(2,1)S(1)}, u32[]{:S(2)}, u32[]{:S(2)}) collective-permute-start(bf16[8,4096]{1,0:T(8,128)(2,1)} %get-tuple-element.47.refs_0_), channel_id=1, source_target_pairs={{0,32},{16,48},{32,0},{48,16},{1,33},{17,49},{33,1},{49,17},{2,34}... | collective-permute-start | bytes 196616 | tf_op jit(solution)/shard_map/ppermute | solution.py:443
  26.5 9.0 %collective-permute-start = (bf16[8,4096]{1,0:T(8,128)(2,1)}, bf16[8,4096]{1,0:T(8,128)(2,1)S(1)}, u32[]{:S(2)}, u32[]{:S(2)}) collective-permute-start(bf16[8,4096]{1,0:T(8,128)(2,1)} %get-tuple-element.47.refs_0_), channel_id=1, source_target_pairs={{0,16},{16,0},{32,48},{48,32},{1,17},{17,1},{33,49},{49,33},{2,18}... | collective-permute-start | bytes 196616 | tf_op jit(solution)/shard_map/ppermute | solution.py:443
  28.9 6.6 %copy-start.10 = (bf16[8,4096]{1,0:T(8,128)(2,1)S(1)}, bf16[8,4096]{1,0:T(8,128)(2,1)}, u32[]{:S(2)}) copy-start(bf16[8,4096]{1,0:T(8,128)(2,1)} %get-tuple-element.47.refs_0_) | copy-start | bytes 196612
  35.7 1.4 copy-start
  37.1 36.0 %all-to-all-start.1 = ((bf16[16,4,8,2048]{3,2,1,0:T(8,128)(2,1)}), bf16[16,4,8,2048]{3,2,1,0:T(8,128)(2,1)S(1)}, u32[]{:S(2)}, u32[]{:S(2)}) async-start(bf16[16,4,8,2048]{3,2,1,0:T(8,128)(2,1)} %copy-done), calls=%async_computation.1 | async-start | bytes 4194304 | tf_op jit(solution)/shard_map/all_to_all | solution.py:484
  43.8 14.5 %copy-start.1 = (bf16[256,896]{1,0:T(8,128)(2,1)S(1)}, bf16[256,896]{1,0:T(8,128)(2,1)}, u32[]{:S(2)}) copy-start(bf16[256,896]{1,0:T(8,128)(2,1)} %get-tuple-element.57.refs_0_) | copy-start | bytes 1376260
  43.8 22.8 %collective-permute-start.8 = (bf16[256,896]{1,0:T(8,128)(2,1)}, bf16[256,896]{1,0:T(8,128)(2,1)S(1)}, u32[]{:S(2)}, u32[]{:S(2)}) collective-permute-start(bf16[256,896]{1,0:T(8,128)(2,1)} %get-tuple-element.62), channel_id=1, source_target_pairs={{0,48},{16,32},{32,16},{48,0},{1,49},{17,33},{33,17},{49,1},{2,50}... | collective-permute-start | bytes 1376264 | tf_op jit(solution)/shard_map/ppermute | solution.py:443
  46.8 19.8 %collective-permute-start.6 = (bf16[256,896]{1,0:T(8,128)(2,1)}, bf16[256,896]{1,0:T(8,128)(2,1)S(1)}, u32[]{:S(2)}, u32[]{:S(2)}) collective-permute-start(bf16[256,896]{1,0:T(8,128)(2,1)} %get-tuple-element.60), channel_id=1, source_target_pairs={{0,32},{16,48},{32,0},{48,16},{1,33},{17,49},{33,1},{49,17},{2,34}... | collective-permute-start | bytes 1376264 | tf_op jit(solution)/shard_map/ppermute | solution.py:443
  47.4 19.8 %collective-permute-start.4 = (bf16[256,896]{1,0:T(8,128)(2,1)}, bf16[256,896]{1,0:T(8,128)(2,1)}, u32[]{:S(2)}, u32[]{:S(2)}) collective-permute-start(bf16[256,896]{1,0:T(8,128)(2,1)} %get-tuple-element.58), channel_id=1, source_target_pairs={{0,16},{16,0},{32,48},{48,32},{1,17},{17,1},{33,49},{49,33},{2,18}... | collective-permute-start | bytes 1376264 | tf_op jit(solution)/shard_map/ppermute | solution.py:443
  47.9 1.2 copy-start.2
  49.1 1.5 copy-start.3
  50.6 1.5 copy-start.4
  52.1 1.5 copy-start.5
  55.4 0.7 copy-start.6
  56.1 0.7 copy-start.12
  56.9 0.7 copy-start.14
  57.6 0.7 copy-start.16
  58.3 9.5 %collective-permute-start.3 = (bf16[256,896]{1,0:T(8,128)(2,1)S(1)}, bf16[256,896]{1,0:T(8,128)(2,1)}, u32[]{:S(2)}, u32[]{:S(2)}) collective-permute-start(bf16[256,896]{1,0:T(8,128)(2,1)S(1)} %copy-done.1), channel_id=1, source_target_pairs={{0,4},{4,0},{1,5},{5,1},{2,6},{6,2},{3,7},{7,3},{8,12},{12,8},{9,1... | collective-permute-start | bytes 1376264 | tf_op jit(solution)/shard_map/ppermute | solution.py:447
  67.3 2.8 %collective-permute-start.5 = (bf16[256,896]{1,0:T(8,128)(2,1)}, bf16[256,896]{1,0:T(8,128)(2,1)}, u32[]{:S(2)}, u32[]{:S(2)}) collective-permute-start(bf16[256,896]{1,0:T(8,128)(2,1)} %collective-permute-done.4.refs_2_), channel_id=1, source_target_pairs={{0,4},{4,0},{1,5},{5,1},{2,6},{6,2},{3,7},{7,3},{8,12},{12,8},{9,1... | collective-permute-start | bytes 1376264 | tf_op jit(solution)/shard_map/ppermute | solution.py:447
  67.3 2.8 %collective-permute-start.7 = (bf16[256,896]{1,0:T(8,128)(2,1)S(1)}, bf16[256,896]{1,0:T(8,128)(2,1)}, u32[]{:S(2)}, u32[]{:S(2)}) collective-permute-start(bf16[256,896]{1,0:T(8,128)(2,1)S(1)} %collective-permute-done.6.refs_4_), channel_id=1, source_target_pairs={{0,4},{4,0},{1,5},{5,1},{2,6},{6,2},{3,7},{7,3},{8,12},{12,8},{9,1... | collective-permute-start | bytes 1376264 | tf_op jit(solution)/shard_map/ppermute | solution.py:447
  67.8 2.7 %collective-permute-start.9 = (bf16[256,896]{1,0:T(8,128)(2,1)S(1)}, bf16[256,896]{1,0:T(8,128)(2,1)}, u32[]{:S(2)}, u32[]{:S(2)}) collective-permute-start(bf16[256,896]{1,0:T(8,128)(2,1)S(1)} %collective-permute-done.8.refs_6_), channel_id=1, source_target_pairs={{0,4},{4,0},{1,5},{5,1},{2,6},{6,2},{3,7},{7,3},{8,12},{12,8},{9,1... | collective-permute-start | bytes 1376264 | tf_op jit(solution)/shard_map/ppermute | solution.py:447
  73.1 3.0 %copy-start.17 = (bf16[256,512]{1,0:T(8,128)(2,1)S(1)}, bf16[256,512]{1,0:T(8,128)(2,1)}, u32[]{:S(2)}) copy-start(bf16[256,512]{1,0:T(8,128)(2,1)} %copy-done.16) | copy-start | bytes 786436
  73.1 4.6 %copy-start.15 = (bf16[256,512]{1,0:T(8,128)(2,1)S(1)}, bf16[256,512]{1,0:T(8,128)(2,1)}, u32[]{:S(2)}) copy-start(bf16[256,512]{1,0:T(8,128)(2,1)} %copy-done.14) | copy-start | bytes 786436
  73.1 7.4 %copy-start.13 = (bf16[256,512]{1,0:T(8,128)(2,1)S(1)}, bf16[256,512]{1,0:T(8,128)(2,1)}, u32[]{:S(2)}) copy-start(bf16[256,512]{1,0:T(8,128)(2,1)} %copy-done.12) | copy-start | bytes 786436
  76.0 17.9 %copy-start.7 = (bf16[256,512]{1,0:T(8,128)(2,1)S(1)}, bf16[256,512]{1,0:T(8,128)(2,1)}, u32[]{:S(2)}) copy-start(bf16[256,512]{1,0:T(8,128)(2,1)} %copy-done.6) | copy-start | bytes 786436
  76.0 10.1 %collective-permute-start.10 = (bf16[256,896]{1,0:T(8,128)(2,1)S(1)}, bf16[256,896]{1,0:T(8,128)(2,1)S(1)}, u32[]{:S(2)}, u32[]{:S(2)}) collective-permute-start(bf16[256,896]{1,0:T(8,128)(2,1)S(1)} %shard_map.151), channel_id=1, source_target_pairs={{0,8},{8,0},{1,9},{9,1},{2,10},{10,2},{3,11},{11,3},{4,12},{12,4},... | collective-permute-start | bytes 1376264 | tf_op jit(solution)/shard_map/ppermute | solution.py:496
  76.1 11.9 %collective-permute-start.12 = (bf16[256,512]{1,0:T(8,128)(2,1)S(1)}, bf16[256,512]{1,0:T(8,128)(2,1)S(1)}, u32[]{:S(2)}, u32[]{:S(2)}) collective-permute-start(bf16[256,512]{1,0:T(8,128)(2,1)S(1)} %copy-done.17), channel_id=1, source_target_pairs={{0,16},{16,0},{32,48},{48,32},{1,17},{17,1},{33,49},{49,33},{2,18}... | collective-permute-start | bytes 786440 | tf_op jit(solution)/shard_map/ppermute | solution.py:443
  77.7 13.6 %collective-permute-start.13 = (bf16[256,512]{1,0:T(8,128)(2,1)S(1)}, bf16[256,512]{1,0:T(8,128)(2,1)S(1)}, u32[]{:S(2)}, u32[]{:S(2)}) collective-permute-start(bf16[256,512]{1,0:T(8,128)(2,1)S(1)} %copy-done.15), channel_id=1, source_target_pairs={{0,32},{16,48},{32,0},{48,16},{1,33},{17,49},{33,1},{49,17},{2,34}... | collective-permute-start | bytes 786440 | tf_op jit(solution)/shard_map/ppermute | solution.py:443
  80.5 13.4 %collective-permute-start.14 = (bf16[256,512]{1,0:T(8,128)(2,1)S(1)}, bf16[256,512]{1,0:T(8,128)(2,1)S(1)}, u32[]{:S(2)}, u32[]{:S(2)}) collective-permute-start(bf16[256,512]{1,0:T(8,128)(2,1)S(1)} %copy-done.13), channel_id=1, source_target_pairs={{0,48},{16,32},{32,16},{48,0},{1,49},{17,33},{33,17},{49,1},{2,50}... | collective-permute-start | bytes 786440 | tf_op jit(solution)/shard_map/ppermute | solution.py:443
  86.3 7.5 %collective-permute-start.11 = (bf16[256,512]{1,0:T(8,128)(2,1)S(1)}, bf16[256,512]{1,0:T(8,128)(2,1)S(1)}, u32[]{:S(2)}, u32[]{:S(2)}) collective-permute-start(bf16[256,512]{1,0:T(8,128)(2,1)S(1)} %shard_map.152.own), channel_id=1, source_target_pairs={{0,8},{8,0},{1,9},{9,1},{2,10},{10,2},{3,11},{11,3},{4,12},{12,4},... | collective-permute-start | bytes 786440 | tf_op jit(solution)/shard_map/ppermute | solution.py:499
  93.9 1.5 collective-permute-start.15
  93.9 1.9 collective-permute-start.16
  94.4 1.8 collective-permute-start.17
  94.5 2.1 collective-permute-start.18
  97.8 40.3 %copy-start.8 = (f32[1,8,4096]{2,1,0:T(8,128)S(1)}, f32[1,8,4096]{2,1,0:T(8,128)}, u32[]{:S(2)}) copy-start(f32[1,8,4096]{2,1,0:T(8,128)} %get-tuple-element.68.attended) | copy-start | bytes 393220
  97.8 40.3 %copy-start.9 = (bf16[8,4096]{1,0:T(8,128)(2,1)S(1)}, bf16[8,4096]{1,0:T(8,128)(2,1)}, u32[]{:S(2)}) copy-start(bf16[8,4096]{1,0:T(8,128)(2,1)} %get-tuple-element.39.rows) | copy-start | bytes 196612
  97.9 40.3 %copy-start.11 = (f32[4096]{0:T(1024)S(1)}, f32[4096]{0:T(1024)}, u32[]{:S(2)}) copy-start(f32[4096]{0:T(1024)} %param.23) | copy-start | bytes 49156
  176.6 10.5 %collective-permute-start.19 = (bf16[256,896]{1,0:T(8,128)(2,1)S(1)}, bf16[256,896]{1,0:T(8,128)(2,1)S(1)}, u32[]{:S(2)}, u32[]{:S(2)}) collective-permute-start(bf16[256,896]{1,0:T(8,128)(2,1)S(1)} %shard_map.156), channel_id=1, source_target_pairs={{0,8},{8,0},{1,9},{9,1},{2,10},{10,2},{3,11},{11,3},{4,12},{12,4},... | collective-permute-start | bytes 1376264 | tf_op jit(solution)/shard_map/ppermute | solution.py:496
  187.3 6.5 %collective-permute-start.20 = (bf16[256,512]{1,0:T(8,128)(2,1)S(1)}, bf16[256,512]{1,0:T(8,128)(2,1)S(1)}, u32[]{:S(2)}, u32[]{:S(2)}) collective-permute-start(bf16[256,512]{1,0:T(8,128)(2,1)S(1)} %shard_map.157.own), channel_id=1, source_target_pairs={{0,8},{8,0},{1,9},{9,1},{2,10},{10,2},{3,11},{11,3},{4,12},{12,4},... | collective-permute-start | bytes 786440 | tf_op jit(solution)/shard_map/ppermute | solution.py:499

commit v6 on v5

--- a/solution.py
+++ b/solution.py
@@ -191,13 +191,14 @@
     half = own.shape[0]
     xl = xl_ref[0]
     for h, part in ((own, xl), (other, 1 - xl)):
-        for b, w in enumerate(blocks):
+        at = 0
+        for w in blocks:
             dot = lax.dot_general(
                 h[...], w[...], (((1,), (1,)), ((), ())), preferred_element_type=F32
             )
-            out[pl.ds(pl.multiple_of(part * half, half), half), b * BLK : (b + 1) * BLK] = (
-                dot.astype(BF16)
-            )
+            rows = pl.ds(pl.multiple_of(part * half, half), half)
+            out[rows, at : at + w.shape[0]] = dot.astype(BF16)
+            at += w.shape[0]
 
 
 def second_products(xl, own, other, blocks):
@@ -206,7 +207,7 @@
         second_body,
         in_specs=[pl.BlockSpec(memory_space=pltpu.SMEM)] + [vmem] * (2 + len(blocks)),
         out_specs=vmem,
-        out_shape=jax.ShapeDtypeStruct((2 * own.shape[0], BLK * len(blocks)), BF16),
+        out_shape=jax.ShapeDtypeStruct((2 * own.shape[0], D // 2), BF16),
         compiler_params=pltpu.CompilerParams(vmem_limit_bytes=8 << 20),
     )(xl, own, other, *blocks)
 
@@ -498,7 +499,12 @@
         hidden = hidden_units(keep, other, pad)
         hidden_other = lax.ppermute(hidden, "xl", pairs("xl", 1))
         if step == 0:
-            down_t = over_c(lax.optimization_barrier((down_t, hidden_other))[0])
+            down_t = lax.optimization_barrier((down_t, hidden))[0]
+            down_t = [
+                q
+                for p in down_t
+                for q in (p, *(lax.ppermute(h, "c", pairs("c", 1)) for h in jnp.split(p, 2)))
+            ]
         partial = second_products(xl, hidden, hidden_other, down_t)
         got = lax.all_to_all(partial.reshape(64, -1, D // 2), GROUP, 0, 0)
         if step == 0:

time: 230 us -> 231 us (level)
  transfers between devices with their start and end apart: 23 -> 27, of which waited for: 14 -> 16; matrix products, arithmetic and copies ran while one was open for 0% -> 0% of each run, Pallas kernels for 10% -> 10%
where the time goes in v6:
time: 231 us; the launch traced here: 230 us
  blocking collectives  108 us (47%)
  Pallas kernels  37.8 us (16%)
  waiting for transfers between devices  37.3 us (16%)
  starting transfers between devices  36 us (16%)
  local copies, waits for them, and re-layouts  10 us (4%)
    all_to_all x2, blocking collectives, shards(): got = lax.all_to_all(partial.reshape(64, -1, D // 2), GROUP, 0, 0)  72.1 us
    all_to_all x1, blocking collectives, shards(): handed = lax.all_to_all(payload, GROUP, 0, 0)  35.5 us
    ppermute x9, waiting for transfers between devices, over_y(): lax.ppermute(p, 'y', pairs('y', k))  14.8 us
    ppermute x9, starting transfers between devices, over_y(): lax.ppermute(p, 'y', pairs('y', k))  13.1 us
    pallas_call x4, Pallas kernels, first_products(): pl.pallas_call(first_body, in_specs=[pl.BlockSpec(memory_space=pltpu.SMEM...  11.4 us
    all_to_all x1, starting transfers between devices, shards(): squares = lax.all_to_all(squares, ALL, 0, 0)  11.1 us
    unnamed x36, local copies, waits for them, and re-layouts  9.93 us
    ppermute x2, waiting for transfers between devices, shards(): other = lax.ppermute(send, 'xl', pairs('xl', 1))  9.73 us
  transfers between devices with their start and end apart: 27, of which 16 were waited for; matrix products, arithmetic and copies ran while one was open for 0% of the time, Pallas kernels for 10%

profile of v6, /device:TPU:0, one launch (start us, length us, event | category | flops | bytes accessed | tf_op | source)
XLA Modules:
  0.0 230.2 jit_solution(6471080093669654291)
XLA Ops:
  0.0 2.6 %shard_map.145 = f32[128,128]{1,0:T(8,128)} custom-call(bf16[2,256,1792]{2,1,0:T(8,128)(2,1)} %refs_3_.1, bf16[256,1792]{1,0:T(8,128)(2,1)} %grad.1), custom_call_target="tpu_custom_call" | custom-call | tf_op jit(solution)/shard_map/pallas_call | solution.py:66
  2.6 11.1 %all-to-all-start = ((f32[128,1,128]{2,1,0:T(1,128)}), f32[128,1,128]{2,1,0:T(1,128)S(1)}, u32[]{:S(2)}, u32[]{:S(2)}) async-start(f32[128,1,128]{2,1,0:T(1,128)} %bitcast.31), calls=%async_computation | async-start | bytes 131072 | tf_op jit(solution)/shard_map/all_to_all | solution.py:471
  13.8 9.6 %shard_map.146 = (bf16[8,4096]{1,0:T(8,128)(2,1)}, bf16[8,4096]{1,0:T(8,128)(2,1)}, f32[1,8,4096]{2,1,0:T(8,128)}) custom-call(s32[8,8]{1,0:T(8,128)} %pages, s32[8]{0:T(128)} %lens.1, bf16[8,4096]{1,0:T(8,128)(2,1)} %rows_ref.1, f32[1,4096]{1,0:T(1,128)} %bitcast.29, bf16[2,8,4096]{2,1,0:T(8,128)(2,1)} %q_ref.1, bf16[2,8,16,128]{3,2,1,0:T(8,128)(2,1)} %bitcast.34, ...), custom_call_target="tpu_custom_call" | custom-call | flops 2147483648 | bytes 33554432 | tf_op jit(solution)/shard_map/pallas_call | solution.py:325
  23.4 2.3 collective-permute-start.2
  25.7 0.8 collective-permute-start.1
  26.5 1.1 collective-permute-start
  27.6 0.6 slice_reduce_fusion
  28.9 6.6 %shard_map.147 = (bf16[256,896]{1,0:T(8,128)(2,1)}, bf16[256,896]{1,0:T(8,128)(2,1)}, bf16[256,896]{1,0:T(8,128)(2,1)}, bf16[256,896]{1,0:T(8,128)(2,1)}) custom-call(s32[1]{0:T(128)} %bitcast.9.y_ref, f32[1]{0:T(128)} %bitcast.13.clip_ref, f32[2,256,1792]{2,1,0:T(8,128)} %refs_0_.1, f32[2,256,1792]{2,1,0:T(8,128)} %refs_1_.1, f32[2,256,1792]{2,1,0:T(8,128)} %refs_2_.1, ...), custom_call_target="tpu_custom_call" | custom-call | tf_op jit(solution)/shard_map/pallas_call | solution.py:107
  35.8 1.3 copy-done
  37.1 6.7 %all-to-all-start.1 = ((bf16[16,4,8,2048]{3,2,1,0:T(8,128)(2,1)}), bf16[16,4,8,2048]{3,2,1,0:T(8,128)(2,1)S(1)}, u32[]{:S(2)}, u32[]{:S(2)}) async-start(bf16[16,4,8,2048]{3,2,1,0:T(8,128)(2,1)} %copy-done), calls=%async_computation.1 | async-start | bytes 4194304 | tf_op jit(solution)/shard_map/all_to_all | solution.py:485
  43.8 2.9 %collective-permute-start.8 = (bf16[256,896]{1,0:T(8,128)(2,1)}, bf16[256,896]{1,0:T(8,128)(2,1)S(1)}, u32[]{:S(2)}, u32[]{:S(2)}) collective-permute-start(bf16[256,896]{1,0:T(8,128)(2,1)} %get-tuple-element.62), channel_id=1, source_target_pairs={{0,48},{16,32},{32,16},{48,0},{1,49},{17,33},{33,17},{49,1},{2,50}... | collective-permute-start | bytes 1376264 | tf_op jit(solution)/shard_map/ppermute | solution.py:444
  46.7 0.7 collective-permute-start.6
  47.4 0.5 collective-permute-start.4
  48.0 1.2 copy-done.2
  49.1 1.5 copy-done.5
  50.6 1.5 copy-done.6
  52.1 1.5 copy-done.7
  53.6 1.8 shard_map.149
  55.5 0.7 copy-done.3
  56.2 0.7 copy-done.12
  56.9 0.7 copy-done.14
  57.6 0.7 copy-done.16
  58.4 8.2 %collective-permute-done.8.refs_6_ = bf16[256,896]{1,0:T(8,128)(2,1)S(1)} collective-permute-done((bf16[256,896]{1,0:T(8,128)(2,1)}, bf16[256,896]{1,0:T(8,128)(2,1)S(1)}, u32[]{:S(2)}, u32[]{:S(2)}) %collective-permute-start.8) | collective-permute-done | bytes 458784 | tf_op jit(solution)/shard_map/ppermute | solution.py:444
  66.6 0.7 collective-permute-done.4.refs_2_
  67.3 0.5 collective-permute-start.7
  67.8 2.3 collective-permute-done.5.refs_3_
  70.6 2.5 %all-to-all-done.1 = bf16[16,4,8,2048]{3,2,1,0:T(8,128)(2,1)S(1)} async-done(((bf16[16,4,8,2048]{3,2,1,0:T(8,128)(2,1)}), bf16[16,4,8,2048]{3,2,1,0:T(8,128)(2,1)S(1)}, u32[]{:S(2)}, u32[]{:S(2)}) %all-to-all-start.1) | async-done | bytes 2097184 | tf_op jit(solution)/shard_map/all_to_all | solution.py:485
  73.1 2.9 %shard_map.151 = bf16[256,896]{1,0:T(8,128)(2,1)S(1)} custom-call(s32[1]{0:T(128)S(6)} %sub.4.part_ref, bf16[512,2048]{1,0:T(8,128)(2,1)S(1)} %bitcast.23, bf16[256,896]{1,0:T(8,128)(2,1)S(1)} %copy-done.1, bf16[256,896]{1,0:T(8,128)(2,1)} %collective-permute-done.3.refs_1_, bf16[256,896]{1,0:T(8,128)(2,1)} %collective-permute-done.4.refs_2_, ...), custom_call_target="tpu_custom_call" | custom-call | tf_op jit(solution)/shard_map/pallas_call | solution.py:161
  76.1 1.6 collective-permute-start.12
  77.7 2.8 %collective-permute-start.13 = (bf16[256,512]{1,0:T(8,128)(2,1)S(1)}, bf16[256,512]{1,0:T(8,128)(2,1)S(1)}, u32[]{:S(2)}, u32[]{:S(2)}) collective-permute-start(bf16[256,512]{1,0:T(8,128)(2,1)S(1)} %copy-done.15), channel_id=1, source_target_pairs={{0,32},{16,48},{32,0},{48,16},{1,33},{17,49},{33,1},{49,17},{2,34}... | collective-permute-start | bytes 786440 | tf_op jit(solution)/shard_map/ppermute | solution.py:444
  80.9 2.8 %shard_map.150.keep = f32[256,896]{1,0:T(8,128)S(1)} custom-call(s32[1]{0:T(128)} %bitcast.8.part_ref.xl_ref, bf16[512,2048]{1,0:T(8,128)(2,1)S(1)} %bitcast.24, bf16[256,896]{1,0:T(8,128)(2,1)S(1)} %copy-done.1, bf16[256,896]{1,0:T(8,128)(2,1)} %collective-permute-done.3.refs_1_, bf16[256,896]{1,0:T(8,128)(2,1)} %collective-permute-done.4.refs_2_, ...), custom_call_target="tpu_custom_call" | custom-call | tf_op jit(solution)/shard_map/pallas_call | solution.py:161
  83.7 2.4 %collective-permute-done.10.other = bf16[256,896]{1,0:T(8,128)(2,1)S(1)} collective-permute-done((bf16[256,896]{1,0:T(8,128)(2,1)S(1)}, bf16[256,896]{1,0:T(8,128)(2,1)S(1)}, u32[]{:S(2)}, u32[]{:S(2)}) %collective-permute-start.10) | collective-permute-done | bytes 458784 | tf_op jit(solution)/shard_map/ppermute | solution.py:497
  86.3 1.7 collective-permute-start.11
  88.1 3.2 %collective-permute-done.13.refs_6_ = bf16[256,512]{1,0:T(8,128)(2,1)S(1)} collective-permute-done((bf16[256,512]{1,0:T(8,128)(2,1)S(1)}, bf16[256,512]{1,0:T(8,128)(2,1)S(1)}, u32[]{:S(2)}, u32[]{:S(2)}) %collective-permute-start.13) | collective-permute-done | bytes 262176 | tf_op jit(solution)/shard_map/ppermute | solution.py:444
  91.3 2.6 %collective-permute-done.14.refs_9_ = bf16[256,512]{1,0:T(8,128)(2,1)S(1)} collective-permute-done((bf16[256,512]{1,0:T(8,128)(2,1)S(1)}, bf16[256,512]{1,0:T(8,128)(2,1)S(1)}, u32[]{:S(2)}, u32[]{:S(2)}) %collective-permute-start.14) | collective-permute-done | bytes 262176 | tf_op jit(solution)/shard_map/ppermute | solution.py:444
  94.0 0.5 collective-permute-start.15
  97.5 1.8 shard_map.153
  99.3 37.4 %all_to_all.32.got = bf16[64,8,2048]{2,1,0:T(8,128)(2,1)S(1)} all-to-all(bf16[64,8,2048]{2,1,0:T(8,128)(2,1)S(1)} %bitcast.28), channel_id=1, replica_groups=mesh['xh'=2,'y'=4,'xl'=2,'c'=2,'z'=4] {'xh','xl','z','y'}, dimensions={0} | all-to-all | bytes 4194304 | tf_op jit(solution)/shard_map/all_to_all | solution.py:509
  136.8 0.6 shard_map.154
  137.3 35.5 %all_to_all.33 = bf16[64,8,2048]{2,1,0:T(8,128)(2,1)S(1)} all-to-all(bf16[64,8,2048]{2,1,0:T(8,128)(2,1)S(1)} %get-tuple-element.70), channel_id=1, replica_groups=mesh['xh'=2,'y'=4,'xl'=2,'c'=2,'z'=4] {'xh','xl','z','y'}, dimensions={0} | all-to-all | bytes 4194304 | tf_op jit(solution)/shard_map/all_to_all | solution.py:512
  172.8 2.8 %shard_map.156 = bf16[256,896]{1,0:T(8,128)(2,1)S(1)} custom-call(s32[1]{0:T(128)S(6)} %sub.4.part_ref, bf16[512,2048]{1,0:T(8,128)(2,1)S(1)} %bitcast.25, bf16[256,896]{1,0:T(8,128)(2,1)S(1)} %copy-done.1, bf16[256,896]{1,0:T(8,128)(2,1)} %collective-permute-done.3.refs_1_, bf16[256,896]{1,0:T(8,128)(2,1)} %collective-permute-done.4.refs_2_, ...), custom_call_target="tpu_custom_call" | custom-call | tf_op jit(solution)/shard_map/pallas_call | solution.py:161
  175.7 2.8 %shard_map.155.keep = f32[256,896]{1,0:T(8,128)S(1)} custom-call(s32[1]{0:T(128)} %bitcast.8.part_ref.xl_ref, bf16[512,2048]{1,0:T(8,128)(2,1)S(1)} %bitcast.26, bf16[256,896]{1,0:T(8,128)(2,1)S(1)} %copy-done.1, bf16[256,896]{1,0:T(8,128)(2,1)} %collective-permute-done.3.refs_1_, bf16[256,896]{1,0:T(8,128)(2,1)} %collective-permute-done.4.refs_2_, ...), custom_call_target="tpu_custom_call" | custom-call | tf_op jit(solution)/shard_map/pallas_call | solution.py:161
  178.6 7.3 %collective-permute-done.23.other = bf16[256,896]{1,0:T(8,128)(2,1)S(1)} collective-permute-done((bf16[256,896]{1,0:T(8,128)(2,1)S(1)}, bf16[256,896]{1,0:T(8,128)(2,1)S(1)}, u32[]{:S(2)}, u32[]{:S(2)}) %collective-permute-start.23) | collective-permute-done | bytes 458784 | tf_op jit(solution)/shard_map/ppermute | solution.py:497
  186.1 0.6 collective-permute-start.24
  186.7 6.1 %collective-permute-done.24.other = bf16[256,512]{1,0:T(8,128)(2,1)S(1)} collective-permute-done((bf16[256,512]{1,0:T(8,128)(2,1)S(1)}, bf16[256,512]{1,0:T(8,128)(2,1)S(1)}, u32[]{:S(2)}, u32[]{:S(2)}) %collective-permute-start.24) | collective-permute-done | bytes 262176 | tf_op jit(solution)/shard_map/ppermute | solution.py:500
  192.8 1.8 shard_map.158
  194.6 34.7 %all_to_all.34.got = bf16[64,8,2048]{2,1,0:T(8,128)(2,1)S(1)} all-to-all(bf16[64,8,2048]{2,1,0:T(8,128)(2,1)S(1)} %bitcast.27), channel_id=1, replica_groups=mesh['xh'=2,'y'=4,'xl'=2,'c'=2,'z'=4] {'xh','xl','z','y'}, dimensions={0} | all-to-all | bytes 4194304 | tf_op jit(solution)/shard_map/all_to_all | solution.py:509
  229.3 0.9 shard_map.159
  (65 shorter events, 4.7 us)
Async XLA Ops:
  2.6 24.9 %all-to-all-start = ((f32[128,1,128]{2,1,0:T(1,128)}), f32[128,1,128]{2,1,0:T(1,128)S(1)}, u32[]{:S(2)}, u32[]{:S(2)}) async-start(f32[128,1,128]{2,1,0:T(1,128)} %bitcast.31), calls=%async_computation | async-start | bytes 131072 | tf_op jit(solution)/shard_map/all_to_all | solution.py:471
  23.4 12.1 %collective-permute-start.2 = (bf16[8,4096]{1,0:T(8,128)(2,1)}, bf16[8,4096]{1,0:T(8,128)(2,1)S(1)}, u32[]{:S(2)}, u32[]{:S(2)}) collective-permute-start(bf16[8,4096]{1,0:T(8,128)(2,1)} %get-tuple-element.47.refs_0_), channel_id=1, source_target_pairs={{0,48},{16,32},{32,16},{48,0},{1,49},{17,33},{33,17},{49,1},{2,50}... | collective-permute-start | bytes 196616 | tf_op jit(solution)/shard_map/ppermute | solution.py:444
  25.7 9.8 %collective-permute-start.1 = (bf16[8,4096]{1,0:T(8,128)(2,1)}, bf16[8,4096]{1,0:T(8,128)(2,1)S(1)}, u32[]{:S(2)}, u32[]{:S(2)}) collective-permute-start(bf16[8,4096]{1,0:T(8,128)(2,1)} %get-tuple-element.47.refs_0_), channel_id=1, source_target_pairs={{0,32},{16,48},{32,0},{48,16},{1,33},{17,49},{33,1},{49,17},{2,34}... | collective-permute-start | bytes 196616 | tf_op jit(solution)/shard_map/ppermute | solution.py:444
  26.5 9.0 %collective-permute-start = (bf16[8,4096]{1,0:T(8,128)(2,1)}, bf16[8,4096]{1,0:T(8,128)(2,1)S(1)}, u32[]{:S(2)}, u32[]{:S(2)}) collective-permute-start(bf16[8,4096]{1,0:T(8,128)(2,1)} %get-tuple-element.47.refs_0_), channel_id=1, source_target_pairs={{0,16},{16,0},{32,48},{48,32},{1,17},{17,1},{33,49},{49,33},{2,18}... | collective-permute-start | bytes 196616 | tf_op jit(solution)/shard_map/ppermute | solution.py:444
  28.9 6.7 %copy-start.10 = (bf16[8,4096]{1,0:T(8,128)(2,1)S(1)}, bf16[8,4096]{1,0:T(8,128)(2,1)}, u32[]{:S(2)}) copy-start(bf16[8,4096]{1,0:T(8,128)(2,1)} %get-tuple-element.47.refs_0_) | copy-start | bytes 196612
  35.7 1.3 copy-start
  37.1 36.0 %all-to-all-start.1 = ((bf16[16,4,8,2048]{3,2,1,0:T(8,128)(2,1)}), bf16[16,4,8,2048]{3,2,1,0:T(8,128)(2,1)S(1)}, u32[]{:S(2)}, u32[]{:S(2)}) async-start(bf16[16,4,8,2048]{3,2,1,0:T(8,128)(2,1)} %copy-done), calls=%async_computation.1 | async-start | bytes 4194304 | tf_op jit(solution)/shard_map/all_to_all | solution.py:485
  43.8 14.6 %copy-start.1 = (bf16[256,896]{1,0:T(8,128)(2,1)S(1)}, bf16[256,896]{1,0:T(8,128)(2,1)}, u32[]{:S(2)}) copy-start(bf16[256,896]{1,0:T(8,128)(2,1)} %get-tuple-element.57.refs_0_) | copy-start | bytes 1376260
  43.8 22.8 %collective-permute-start.8 = (bf16[256,896]{1,0:T(8,128)(2,1)}, bf16[256,896]{1,0:T(8,128)(2,1)S(1)}, u32[]{:S(2)}, u32[]{:S(2)}) collective-permute-start(bf16[256,896]{1,0:T(8,128)(2,1)} %get-tuple-element.62), channel_id=1, source_target_pairs={{0,48},{16,32},{32,16},{48,0},{1,49},{17,33},{33,17},{49,1},{2,50}... | collective-permute-start | bytes 1376264 | tf_op jit(solution)/shard_map/ppermute | solution.py:444
  46.7 19.8 %collective-permute-start.6 = (bf16[256,896]{1,0:T(8,128)(2,1)}, bf16[256,896]{1,0:T(8,128)(2,1)S(1)}, u32[]{:S(2)}, u32[]{:S(2)}) collective-permute-start(bf16[256,896]{1,0:T(8,128)(2,1)} %get-tuple-element.60), channel_id=1, source_target_pairs={{0,32},{16,48},{32,0},{48,16},{1,33},{17,49},{33,1},{49,17},{2,34}... | collective-permute-start | bytes 1376264 | tf_op jit(solution)/shard_map/ppermute | solution.py:444
  47.4 19.8 %collective-permute-start.4 = (bf16[256,896]{1,0:T(8,128)(2,1)}, bf16[256,896]{1,0:T(8,128)(2,1)}, u32[]{:S(2)}, u32[]{:S(2)}) collective-permute-start(bf16[256,896]{1,0:T(8,128)(2,1)} %get-tuple-element.58), channel_id=1, source_target_pairs={{0,16},{16,0},{32,48},{48,32},{1,17},{17,1},{33,49},{49,33},{2,18}... | collective-permute-start | bytes 1376264 | tf_op jit(solution)/shard_map/ppermute | solution.py:444
  48.0 1.2 copy-start.2
  49.1 1.5 copy-start.5
  50.6 1.5 copy-start.6
  52.1 1.5 copy-start.7
  55.5 0.7 copy-start.3
  56.2 0.7 copy-start.12
  56.9 0.7 copy-start.14
  57.6 0.7 copy-start.16
  58.4 9.5 %collective-permute-start.3 = (bf16[256,896]{1,0:T(8,128)(2,1)S(1)}, bf16[256,896]{1,0:T(8,128)(2,1)}, u32[]{:S(2)}, u32[]{:S(2)}) collective-permute-start(bf16[256,896]{1,0:T(8,128)(2,1)S(1)} %copy-done.1), channel_id=1, source_target_pairs={{0,4},{4,0},{1,5},{5,1},{2,6},{6,2},{3,7},{7,3},{8,12},{12,8},{9,1... | collective-permute-start | bytes 1376264 | tf_op jit(solution)/shard_map/ppermute | solution.py:448
  67.3 2.8 %collective-permute-start.5 = (bf16[256,896]{1,0:T(8,128)(2,1)}, bf16[256,896]{1,0:T(8,128)(2,1)}, u32[]{:S(2)}, u32[]{:S(2)}) collective-permute-start(bf16[256,896]{1,0:T(8,128)(2,1)} %collective-permute-done.4.refs_2_), channel_id=1, source_target_pairs={{0,4},{4,0},{1,5},{5,1},{2,6},{6,2},{3,7},{7,3},{8,12},{12,8},{9,1... | collective-permute-start | bytes 1376264 | tf_op jit(solution)/shard_map/ppermute | solution.py:448
  67.3 2.8 %collective-permute-start.7 = (bf16[256,896]{1,0:T(8,128)(2,1)S(1)}, bf16[256,896]{1,0:T(8,128)(2,1)}, u32[]{:S(2)}, u32[]{:S(2)}) collective-permute-start(bf16[256,896]{1,0:T(8,128)(2,1)S(1)} %collective-permute-done.6.refs_4_), channel_id=1, source_target_pairs={{0,4},{4,0},{1,5},{5,1},{2,6},{6,2},{3,7},{7,3},{8,12},{12,8},{9,1... | collective-permute-start | bytes 1376264 | tf_op jit(solution)/shard_map/ppermute | solution.py:448
  67.8 2.7 %collective-permute-start.9 = (bf16[256,896]{1,0:T(8,128)(2,1)S(1)}, bf16[256,896]{1,0:T(8,128)(2,1)}, u32[]{:S(2)}, u32[]{:S(2)}) collective-permute-start(bf16[256,896]{1,0:T(8,128)(2,1)S(1)} %collective-permute-done.8.refs_6_), channel_id=1, source_target_pairs={{0,4},{4,0},{1,5},{5,1},{2,6},{6,2},{3,7},{7,3},{8,12},{12,8},{9,1... | collective-permute-start | bytes 1376264 | tf_op jit(solution)/shard_map/ppermute | solution.py:448
  73.1 3.0 %copy-start.17 = (bf16[256,512]{1,0:T(8,128)(2,1)S(1)}, bf16[256,512]{1,0:T(8,128)(2,1)}, u32[]{:S(2)}) copy-start(bf16[256,512]{1,0:T(8,128)(2,1)} %copy-done.16) | copy-start | bytes 786436
  73.1 4.6 %copy-start.15 = (bf16[256,512]{1,0:T(8,128)(2,1)S(1)}, bf16[256,512]{1,0:T(8,128)(2,1)}, u32[]{:S(2)}) copy-start(bf16[256,512]{1,0:T(8,128)(2,1)} %copy-done.14) | copy-start | bytes 786436
  73.1 7.4 %copy-start.13 = (bf16[256,512]{1,0:T(8,128)(2,1)S(1)}, bf16[256,512]{1,0:T(8,128)(2,1)}, u32[]{:S(2)}) copy-start(bf16[256,512]{1,0:T(8,128)(2,1)} %copy-done.12) | copy-start | bytes 786436
  76.0 17.9 %copy-start.4 = (bf16[256,512]{1,0:T(8,128)(2,1)S(1)}, bf16[256,512]{1,0:T(8,128)(2,1)}, u32[]{:S(2)}) copy-start(bf16[256,512]{1,0:T(8,128)(2,1)} %copy-done.3) | copy-start | bytes 786436
  76.0 10.1 %collective-permute-start.10 = (bf16[256,896]{1,0:T(8,128)(2,1)S(1)}, bf16[256,896]{1,0:T(8,128)(2,1)S(1)}, u32[]{:S(2)}, u32[]{:S(2)}) collective-permute-start(bf16[256,896]{1,0:T(8,128)(2,1)S(1)} %shard_map.151), channel_id=1, source_target_pairs={{0,8},{8,0},{1,9},{9,1},{2,10},{10,2},{3,11},{11,3},{4,12},{12,4},... | collective-permute-start | bytes 1376264 | tf_op jit(solution)/shard_map/ppermute | solution.py:497
  76.1 12.0 %collective-permute-start.12 = (bf16[256,512]{1,0:T(8,128)(2,1)S(1)}, bf16[256,512]{1,0:T(8,128)(2,1)S(1)}, u32[]{:S(2)}, u32[]{:S(2)}) collective-permute-start(bf16[256,512]{1,0:T(8,128)(2,1)S(1)} %copy-done.17), channel_id=1, source_target_pairs={{0,16},{16,0},{32,48},{48,32},{1,17},{17,1},{33,49},{49,33},{2,18}... | collective-permute-start | bytes 786440 | tf_op jit(solution)/shard_map/ppermute | solution.py:444
  77.7 13.6 %collective-permute-start.13 = (bf16[256,512]{1,0:T(8,128)(2,1)S(1)}, bf16[256,512]{1,0:T(8,128)(2,1)S(1)}, u32[]{:S(2)}, u32[]{:S(2)}) collective-permute-start(bf16[256,512]{1,0:T(8,128)(2,1)S(1)} %copy-done.15), channel_id=1, source_target_pairs={{0,32},{16,48},{32,0},{48,16},{1,33},{17,49},{33,1},{49,17},{2,34}... | collective-permute-start | bytes 786440 | tf_op jit(solution)/shard_map/ppermute | solution.py:444
  80.5 13.4 %collective-permute-start.14 = (bf16[256,512]{1,0:T(8,128)(2,1)S(1)}, bf16[256,512]{1,0:T(8,128)(2,1)S(1)}, u32[]{:S(2)}, u32[]{:S(2)}) collective-permute-start(bf16[256,512]{1,0:T(8,128)(2,1)S(1)} %copy-done.13), channel_id=1, source_target_pairs={{0,48},{16,32},{32,16},{48,0},{1,49},{17,33},{33,17},{49,1},{2,50}... | collective-permute-start | bytes 786440 | tf_op jit(solution)/shard_map/ppermute | solution.py:444
  86.3 11.1 %collective-permute-start.11 = (bf16[256,512]{1,0:T(8,128)(2,1)S(1)}, bf16[256,512]{1,0:T(8,128)(2,1)S(1)}, u32[]{:S(2)}, u32[]{:S(2)}) collective-permute-start(bf16[256,512]{1,0:T(8,128)(2,1)S(1)} %shard_map.152.own), channel_id=1, source_target_pairs={{0,8},{8,0},{1,9},{9,1},{2,10},{10,2},{3,11},{11,3},{4,12},{12,4},... | collective-permute-start | bytes 786440 | tf_op jit(solution)/shard_map/ppermute | solution.py:500
  93.9 1.4 collective-permute-start.16
  94.0 1.5 collective-permute-start.15
  94.5 1.4 collective-permute-start.18
  94.7 1.4 collective-permute-start.17
  95.3 1.3 collective-permute-start.20
  95.5 1.3 collective-permute-start.19
  95.9 1.3 collective-permute-start.22
  96.1 1.3 collective-permute-start.21
  99.3 37.4 %copy-start.8 = (f32[1,8,4096]{2,1,0:T(8,128)S(1)}, f32[1,8,4096]{2,1,0:T(8,128)}, u32[]{:S(2)}) copy-start(f32[1,8,4096]{2,1,0:T(8,128)} %get-tuple-element.68.attended) | copy-start | bytes 393220
  99.3 37.4 %copy-start.9 = (bf16[8,4096]{1,0:T(8,128)(2,1)S(1)}, bf16[8,4096]{1,0:T(8,128)(2,1)}, u32[]{:S(2)}) copy-start(bf16[8,4096]{1,0:T(8,128)(2,1)} %get-tuple-element.39.rows) | copy-start | bytes 196612
  99.3 37.4 %copy-start.11 = (f32[4096]{0:T(1024)S(1)}, f32[4096]{0:T(1024)}, u32[]{:S(2)}) copy-start(f32[4096]{0:T(1024)} %param.23) | copy-start | bytes 49156
  175.6 10.3 %collective-permute-start.23 = (bf16[256,896]{1,0:T(8,128)(2,1)S(1)}, bf16[256,896]{1,0:T(8,128)(2,1)S(1)}, u32[]{:S(2)}, u32[]{:S(2)}) collective-permute-start(bf16[256,896]{1,0:T(8,128)(2,1)S(1)} %shard_map.156), channel_id=1, source_target_pairs={{0,8},{8,0},{1,9},{9,1},{2,10},{10,2},{3,11},{11,3},{4,12},{12,4},... | collective-permute-start | bytes 1376264 | tf_op jit(solution)/shard_map/ppermute | solution.py:497
  186.1 6.7 %collective-permute-start.24 = (bf16[256,512]{1,0:T(8,128)(2,1)S(1)}, bf16[256,512]{1,0:T(8,128)(2,1)S(1)}, u32[]{:S(2)}, u32[]{:S(2)}) collective-permute-start(bf16[256,512]{1,0:T(8,128)(2,1)S(1)} %shard_map.157.own), channel_id=1, source_target_pairs={{0,8},{8,0},{1,9},{9,1},{2,10},{10,2},{3,11},{11,3},{4,12},{12,4},... | collective-permute-start | bytes 786440 | tf_op jit(solution)/shard_map/ppermute | solution.py:500
